TPU v7x, 256 devices: a whole 4x4x8 slice. The times are simulated.
256 devices in a mesh: gx: 16 (over z_hi, y), gz: 16 (over z_lo, x, core).
Axes of the slice: x: 4, y: 4, z: 8 (z_hi: 4, z_lo: 2; z = z_hi * 2 + z_lo), core: 2. Of those that a mesh axis runs over, the one named last changes fastest.
Arguments:
- rho_prev: float32 [128, 512, 512], P('gz', 'gx'), may hold values from 0.3 to 8.2, as said below
- potential: float32 [128, 512, 512], P('gz', 'gx'), may hold values from 0 to 1.5
Outputs:
- rho_next: float32 [128, 512, 512], P('gz', 'gx')
- mass_ratio: float32 [1], replicated
Inputs may be any that keep to these rules, and one draw needn't show every extreme that they name: `rho_prev`: strictly positive in every cell.
All inputs are finite; a program needn't handle non-finite values.
Results may differ from a plain program's by a relative error of at most 0.0001.
Values sent between devices are 32-bit elements; how exact they have to be, the bound alone decides.
No kernel may reach another device: no remote copies, remote signals or barrier semaphores. Data moves between devices by JAX's collectives and lax.ppermute only.
A program may use at most 64 MiB of HBM per device.

v0:
```python
import functools

import jax
import jax.numpy as jnp
import numpy as np
from jax import lax
from jax.experimental import pallas as pl
from jax.experimental.pallas import tpu as pltpu
from jax.sharding import PartitionSpec as P


HALF = 8
ITERS = 3
NEWTON = 6
LANES = 128


EDGE, INNER = (0, 3), (1, 2)


def scale():
    offsets = np.arange(-HALF, HALF + 1)
    return float(np.sum(np.exp(-2.0 * offsets * offsets / (HALF * HALF))))


def weight(gap):
    gap = gap.astype(jnp.float32)
    raw = jnp.exp(-2.0 * gap * gap / (HALF * HALF)) / scale()
    return jnp.where(jnp.abs(gap) <= HALF, raw, 0.0)


def inside_mass(cell, whole):
    total = jnp.zeros(cell.shape, jnp.float32)
    for gap in range(-HALF, HALF + 1):
        share = float(np.exp(-2.0 * gap * gap / (HALF * HALF)) / scale())
        total += jnp.where((cell + gap >= 0) & (cell + gap < whole), share, 0.0)
    return total


def split(value):
    high = value.astype(jnp.bfloat16)
    return high, (value - high.astype(jnp.float32)).astype(jnp.bfloat16)


def dot3(left, right):
    dot = functools.partial(jnp.dot, preferred_element_type=jnp.float32)
    return dot(left[0], right[0]) + (dot(left[0], right[1]) + dot(left[1], right[0]))


def iota(shape, dim):
    return lax.broadcasted_iota(jnp.int32, shape, dim)


def swap(value, axis, first):
    size = lax.axis_size(axis)
    pairs = [(i, i + 1) for i in range(first, size - 1, 2)]
    return lax.ppermute(value, axis, pairs + [(j, i) for i, j in pairs])


def group(ref, at):
    return ref[:, at * HALF : (at + 1) * HALF, :]


def groups(ref, which):
    return jnp.concatenate([group(ref, at).reshape(-1, ref.shape[2]) for at in which], axis=0)


def tables_kernel(depth, where, z_high, z_low, x_high, x_low, side_high, side_low, y_high, y_low):
    even = where[1]
    shape = z_high.shape
    rows = shape[0]
    row, col = iota(shape, 0), iota(shape, 1)
    block, cell = col // rows, col % rows
    far = jnp.where(even == 1, -depth, depth)
    gap = row // HALF - cell // HALF - jnp.where(block == 0, 0, jnp.where(block == 1, far, -far))
    z_high[...], z_low[...] = split(jnp.where(row % HALF == cell % HALF, weight(gap), 0.0))
    shape = x_high.shape
    row, col = iota(shape, 0), iota(shape, 1)
    gap = row % HALF - col % HALF + HALF * (row // rows - col // rows)
    same = row % rows // HALF == col % rows // HALF
    x_high[...], x_low[...] = split(jnp.where(same, weight(gap), 0.0))
    shape = side_high.shape
    row, col = iota(shape, 0), iota(shape, 1)
    gap = row % HALF - col % HALF + jnp.where(row < rows, HALF, -HALF)
    side_high[...], side_low[...] = split(jnp.where(row % rows // HALF == col // HALF, weight(gap), 0.0))
    shape = y_high.shape
    y_high[...], y_low[...] = split(weight(iota(shape, 0) - iota(shape, 1)))


def first_kernel(sizes, where, rho_prev, edge, inner):
    depth, _, length = rho_prev.shape
    whole_x, whole_z = sizes
    mass_z = inside_mass(where[3] + iota((depth, LANES), 0), whole_z)
    mass_y = inside_mass(iota((1, length), 1), length)
    rows = depth * HALF
    for ref, which in ((edge, EDGE), (inner, INNER)):
        for place, at in enumerate(which):
            mass_x = inside_mass(where[2] + at * HALF + iota((HALF, LANES), 0), whole_x)
            for z in range(depth):
                mass = (mass_x[:, :1] * mass_z[z : z + 1, :1]) * mass_y
                start = place * rows + z * HALF
                ref[start : start + HALF] = rho_prev[z, at * HALF : (at + 1) * HALF, :] / mass


def zy(own, far, near, z_high, z_low, y_high, y_low, high, low):
    rows = z_high.shape[0]
    results = []
    for place in range(2):
        span = slice(place * rows, (place + 1) * rows)
        for block, ref in enumerate((own, far, near)):
            to = slice((3 * place + block) * rows, (3 * place + block + 1) * rows)
            high[to], low[to] = split(ref[span])
        at = slice(3 * place * rows, 3 * (place + 1) * rows)
        results.append(dot3((z_high[...], z_low[...]), (high[at], low[at])))
    return dot3(split(jnp.concatenate(results, axis=0)), (y_high[...], y_low[...]))


def edge_kernel(where, own, far, near, z_high, z_low, y_high, y_low, send1, send0, high, low):
    value = zy(own, far, near, z_high, z_low, y_high, y_low, high, low)
    rows = value.shape[0] // 2
    before, after = value[:rows], value[rows:]
    send0[...] = jnp.where(where[0] == 1, after, before)
    send1[...] = jnp.where(where[0] == 1, before, after)


def prox(target):
    current = target
    for _ in range(NEWTON):
        grown = 0.5 * jnp.exp(current)
        current = (grown * (current - 1.0) + target) / (1.0 + grown)
    return jnp.exp(current)


def finish(kind, value, which, whole, scaling):
    if kind == "dual":
        return groups(whole, which) / value
    inner = value if scaling is None else scaling[...] * value
    rho = prox(jnp.log(inner) - groups(whole, which))
    return rho if kind == "last" else rho / value


def lane_sums(value):
    rows = jnp.sum(value, axis=0, keepdims=True)
    return sum(rows[:, i : i + LANES] for i in range(0, rows.shape[1], LANES))


def inner_kernel(kind, started, where, send1, send0, own, far, near, z_high, z_low, y_high, y_low, x_high, x_low, whole, *rest):
    scaling = None
    if started:
        scaling, *rest = rest
    if kind == "last":
        rho_prev, out, part, sums, high, low, zy_high, zy_low = rest
    else:
        out, part, high, low, zy_high, zy_low = rest
    rows = z_high.shape[0]
    value = zy(own, far, near, z_high, z_low, y_high, y_low, high, low)
    before = jnp.where(where[0] == 1, send1[...], send0[...])
    after = jnp.where(where[0] == 1, send0[...], send1[...])
    zy_high[:rows], zy_low[:rows] = split(before)
    zy_high[rows : 3 * rows], zy_low[rows : 3 * rows] = split(value)
    zy_high[3 * rows :], zy_low[3 * rows :] = split(after)
    along_x = dot3((x_high[...], x_low[...]), (zy_high[...], zy_low[...]))
    part[:rows], part[rows:] = along_x[:rows], along_x[3 * rows :]
    result = finish(kind, along_x[rows : 3 * rows], INNER, whole, scaling)
    out[...] = result
    if kind == "last":
        depth, width, length = rho_prev.shape
        sums[:, :LANES] = lane_sums(rho_prev[...].reshape(depth * width, length))
        sums[:, LANES:] = lane_sums(result)


def outer_kernel(kind, started, where, part, recv1, recv0, side_high, side_low, whole, *rest):
    scaling = None
    if started:
        scaling, *rest = rest
    if kind == "last":
        sums_inner, out, sums = rest
    else:
        (out,) = rest
    rows = recv0.shape[0]
    before = split(jnp.where(where[0] == 1, recv1[...], recv0[...]))
    after = split(jnp.where(where[0] == 1, recv0[...], recv1[...]))
    first = part[:rows] + dot3((side_high[:rows], side_low[:rows]), before)
    second = part[rows:] + dot3((side_high[rows:], side_low[rows:]), after)
    result = finish(kind, jnp.concatenate([first, second], axis=0), EDGE, whole, scaling)
    out[...] = result
    if kind == "last":
        sums[...] = sums_inner[...]
        sums[:, LANES:] += lane_sums(result)


def scale_kernel(edge, inner, sums, out, ratio):
    totals = jnp.sum(sums[...], axis=0, keepdims=True)
    mass_prev, mass_new = jnp.sum(totals[:, :LANES]), jnp.sum(totals[:, LANES:])
    ones = jnp.ones((1, LANES), jnp.float32)
    prev, new = mass_prev * ones, mass_new * ones
    ratio[...] = new / prev
    factor = (prev / new)[:, :1]
    depth, _, length = out.shape
    rows = depth * HALF
    for ref, which in ((edge, EDGE), (inner, INNER)):
        for place, at in enumerate(which):
            value = ref[place * rows : (place + 1) * rows] * factor
            out[:, at * HALF : (at + 1) * HALF, :] = value.reshape(depth, HALF, length)


def call(kernel, inputs, shapes, scratch=(), scalars=1, dtype=jnp.float32):
    specs = [pl.BlockSpec(memory_space=pltpu.SMEM)] * scalars
    specs += [pl.BlockSpec(memory_space=pltpu.VMEM)] * (len(inputs) - scalars)
    return pl.pallas_call(
        kernel,
        out_shape=[jax.ShapeDtypeStruct(shape, dtype) for shape in shapes],
        in_specs=specs,
        out_specs=[pl.BlockSpec(memory_space=pltpu.VMEM)] * len(shapes),
        scratch_shapes=scratch,
        compiler_params=pltpu.CompilerParams(vmem_limit_bytes=20 << 20),
    )(*inputs)


def step(rho_prev, potential):
    depth, width, length = rho_prev.shape
    at_x, at_z = lax.axis_index("gx"), lax.axis_index("gz")
    size_x, size_z = lax.axis_size("gx"), lax.axis_size("gz")
    where = jnp.stack([1 - at_x % 2, 1 - at_z % 2, at_x * width, at_z * depth]).astype(jnp.int32)
    rows = depth * HALF
    one, two = (rows, length), (2 * rows, length)
    zy_scratch = [pltpu.VMEM((6 * rows, length), jnp.bfloat16)] * 2
    x_scratch = [pltpu.VMEM((4 * rows, length), jnp.bfloat16)] * 2

    first = functools.partial(first_kernel, (width * size_x, depth * size_z))
    edge, inner = call(first, (where, rho_prev), [two, two])
    table_shapes = [(rows, 3 * rows), (4 * rows, 4 * rows), (2 * rows, rows), (length, length)]
    doubled = [shape for shape in table_shapes for _ in range(2)]
    tables = call(functools.partial(tables_kernel, depth), (where,), doubled, dtype=jnp.bfloat16)
    z_table, x_table, side_table, y_table = (tuple(tables[i : i + 2]) for i in range(0, 8, 2))

    def heat_step(kind, edge, inner, whole, scaling):
        far_edge = swap(edge, "gz", 1)
        near_edge = swap(edge, "gz", 0)
        far_inner = swap(inner, "gz", 1)
        near_inner = swap(inner, "gz", 0)
        sends = call(edge_kernel, (where, edge, far_edge, near_edge, *z_table, *y_table), [one, one], zy_scratch)
        recv1 = swap(sends[0], "gx", 1)
        recv0 = swap(sends[1], "gx", 0)
        started, last = scaling is not None, kind == "last"
        inputs = (where, *sends, inner, far_inner, near_inner, *z_table, *y_table, *x_table, whole)
        more = ((scaling[1],) if started else ()) + ((rho_prev,) if last else ())
        shapes = [two, two] + ([(1, 2 * LANES)] if last else [])
        new_inner, part, *sums = call(
            functools.partial(inner_kernel, kind, started), inputs + more, shapes, zy_scratch + x_scratch
        )
        more = ((scaling[0],) if started else ()) + tuple(sums)
        shapes = [two] + ([(1, 2 * LANES)] if last else [])
        new_edge, *sums = call(
            functools.partial(outer_kernel, kind, started),
            (where, part, recv1, recv0, *side_table, whole, *more),
            shapes,
        )
        return new_edge, new_inner, *sums

    scaling = None
    for sweep in range(ITERS):
        if sweep:
            edge, inner = heat_step("dual", edge, inner, rho_prev, None)
        if sweep < ITERS - 1:
            edge, inner = scaling = heat_step("scaling", edge, inner, potential, scaling)
        else:
            edge, inner, sums = heat_step("last", edge, inner, potential, scaling)
    everyone = size_x * size_z
    sums = jnp.broadcast_to(sums[None], (everyone, 1, 2 * LANES))
    sums = lax.all_to_all(sums, ("gx", "gz"), 0, 0, tiled=True).reshape(everyone, 2 * LANES)
    rho_next, ratio = call(scale_kernel, (edge, inner, sums), [(depth, width, length), (1, LANES)], scalars=0)
    return rho_next, ratio[0, :1]


def solution(mesh):
    return jax.shard_map(
        step,
        mesh=mesh,
        in_specs=(P("gz", "gx", None), P("gz", "gx", None)),
        out_specs=(P("gz", "gx", None), P()),
        check_vma=False,
    )
```

profile of v0, /device:TPU:1, one launch (start us, length us, event | category | flops | bytes accessed | tf_op | source)
XLA Modules:
  0.0 154.8 jit_solution(16520676500334709326)
XLA Ops:
  0.7 1.0 copy-done
  1.8 0.7 shard_map.41
  2.5 4.5 %collective-permute-start = (f32[128,512]{1,0:T(8,128)S(1)}, f32[128,512]{1,0:T(8,128)S(1)}, u32[]{:S(2)}, u32[]{:S(2)}) collective-permute-start(f32[128,512]{1,0:T(8,128)S(1)} %get-tuple-element.37.own), channel_id=1, source_target_pairs={{1,2},{3,4},{5,6},{7,8},{9,10},{11,12},{13,14},{2,1},{4,3},{6,5},{... | collective-permute-start | bytes 786440 | tf_op jit(solution)/shard_map/ppermute | solution.py:57
  7.0 0.1 collective-permute-start.1
  7.1 3.5 %collective-permute-start.2 = (f32[128,512]{1,0:T(8,128)S(1)}, f32[128,512]{1,0:T(8,128)S(1)}, u32[]{:S(2)}, u32[]{:S(2)}) collective-permute-start(f32[128,512]{1,0:T(8,128)S(1)} %get-tuple-element.44.own), channel_id=1, source_target_pairs={{1,2},{3,4},{5,6},{7,8},{9,10},{11,12},{13,14},{2,1},{4,3},{6,5},{... | collective-permute-start | bytes 786440 | tf_op jit(solution)/shard_map/ppermute | solution.py:57
  10.6 0.1 collective-permute-start.3
  10.7 1.4 shard_map.42
  12.1 1.2 shard_map.43
  13.3 0.7 collective-permute-start.4
  14.0 3.9 %collective-permute-start.5 = (f32[64,512]{1,0:T(8,128)S(1)}, f32[64,512]{1,0:T(8,128)S(1)}, u32[]{:S(2)}, u32[]{:S(2)}) collective-permute-start(f32[64,512]{1,0:T(8,128)S(1)} %get-tuple-element.43.send0), channel_id=1, source_target_pairs={{0,16},{32,48},{64,80},{96,112},{128,144},{160,176},{192,208},{224... | collective-permute-start | bytes 393224 | tf_op jit(solution)/shard_map/ppermute | solution.py:57
  17.9 2.1 %shard_map.44 = (f32[128,512]{1,0:T(8,128)S(1)}, f32[128,512]{1,0:T(8,128)S(1)}) custom-call(s32[4]{0:T(128)S(1)} %pad_add_fusion.where, f32[64,512]{1,0:T(8,128)S(1)} %get-tuple-element.42.send1, f32[64,512]{1,0:T(8,128)S(1)} %get-tuple-element.43.send0, f32[128,512]{1,0:T(8,128)S(1)} %get-tuple-element.44.own, f32[128,512]{1,0:T(8,128)S(1)} %collective-permute-done.2.far, ...), custom_call_target="tpu_custom_call" | custom-call | tf_op jit(solution)/shard_map/pallas_call | solution.py:210
  20.0 0.9 collective-permute-done.5.recv0
  21.0 1.3 shard_map.45.own.rest_0_
  22.3 4.1 %collective-permute-start.6 = (f32[128,512]{1,0:T(8,128)S(1)}, f32[128,512]{1,0:T(8,128)S(1)}, u32[]{:S(2)}, u32[]{:S(2)}) collective-permute-start(f32[128,512]{1,0:T(8,128)S(1)} %shard_map.45.own.rest_0_), channel_id=1, source_target_pairs={{1,2},{3,4},{5,6},{7,8},{9,10},{11,12},{13,14},{2,1},{4,3},{6,5},{... | collective-permute-start | bytes 786440 | tf_op jit(solution)/shard_map/ppermute | solution.py:57
  26.5 4.0 %collective-permute-start.8 = (f32[128,512]{1,0:T(8,128)S(1)}, f32[128,512]{1,0:T(8,128)S(1)}, u32[]{:S(2)}, u32[]{:S(2)}) collective-permute-start(f32[128,512]{1,0:T(8,128)S(1)} %get-tuple-element.52.own.rest_0_), channel_id=1, source_target_pairs={{1,2},{3,4},{5,6},{7,8},{9,10},{11,12},{13,14},{2,1},{4,3},{6,5},{... | collective-permute-start | bytes 786440 | tf_op jit(solution)/shard_map/ppermute | solution.py:57
  30.6 1.2 shard_map.46
  31.8 0.7 collective-permute-start.10
  32.5 5.0 %collective-permute-start.11 = (f32[64,512]{1,0:T(8,128)S(1)}, f32[64,512]{1,0:T(8,128)S(1)}, u32[]{:S(2)}, u32[]{:S(2)}) collective-permute-start(f32[64,512]{1,0:T(8,128)S(1)} %get-tuple-element.51.send0), channel_id=1, source_target_pairs={{0,16},{32,48},{64,80},{96,112},{128,144},{160,176},{192,208},{224... | collective-permute-start | bytes 393224 | tf_op jit(solution)/shard_map/ppermute | solution.py:57
  37.5 1.6 %shard_map.47 = (f32[128,512]{1,0:T(8,128)S(1)}, f32[128,512]{1,0:T(8,128)S(1)}) custom-call(s32[4]{0:T(128)S(1)} %pad_add_fusion.where, f32[64,512]{1,0:T(8,128)S(1)} %get-tuple-element.50.send1, f32[64,512]{1,0:T(8,128)S(1)} %get-tuple-element.51.send0, f32[128,512]{1,0:T(8,128)S(1)} %get-tuple-element.52.own.rest_0_, ...), custom_call_target="tpu_custom_call" | custom-call | tf_op jit(solution)/shard_map/pallas_call | solution.py:210
  39.1 1.5 collective-permute-done.11.recv0
  40.6 0.8 shard_map.48.own
  41.4 5.0 %collective-permute-start.12 = (f32[128,512]{1,0:T(8,128)S(1)}, f32[128,512]{1,0:T(8,128)S(1)}, u32[]{:S(2)}, u32[]{:S(2)}) collective-permute-start(f32[128,512]{1,0:T(8,128)S(1)} %shard_map.48.own), channel_id=1, source_target_pairs={{1,2},{3,4},{5,6},{7,8},{9,10},{11,12},{13,14},{2,1},{4,3},{6,5},{... | collective-permute-start | bytes 786440 | tf_op jit(solution)/shard_map/ppermute | solution.py:57
  46.5 4.0 %collective-permute-start.14 = (f32[128,512]{1,0:T(8,128)S(1)}, f32[128,512]{1,0:T(8,128)S(1)}, u32[]{:S(2)}, u32[]{:S(2)}) collective-permute-start(f32[128,512]{1,0:T(8,128)S(1)} %get-tuple-element.56.own), channel_id=1, source_target_pairs={{1,2},{3,4},{5,6},{7,8},{9,10},{11,12},{13,14},{2,1},{4,3},{6,5},{... | collective-permute-start | bytes 786440 | tf_op jit(solution)/shard_map/ppermute | solution.py:57
  50.6 1.2 shard_map.49
  51.8 0.7 collective-permute-start.16
  52.5 7.2 %collective-permute-start.17 = (f32[64,512]{1,0:T(8,128)S(1)}, f32[64,512]{1,0:T(8,128)S(1)}, u32[]{:S(2)}, u32[]{:S(2)}) collective-permute-start(f32[64,512]{1,0:T(8,128)S(1)} %get-tuple-element.55.send0), channel_id=1, source_target_pairs={{0,16},{32,48},{64,80},{96,112},{128,144},{160,176},{192,208},{224... | collective-permute-start | bytes 393224 | tf_op jit(solution)/shard_map/ppermute | solution.py:57
  59.7 2.1 %shard_map.50 = (f32[128,512]{1,0:T(8,128)S(1)}, f32[128,512]{1,0:T(8,128)S(1)}) custom-call(s32[4]{0:T(128)S(1)} %pad_add_fusion.where, f32[64,512]{1,0:T(8,128)S(1)} %get-tuple-element.54.send1, f32[64,512]{1,0:T(8,128)S(1)} %get-tuple-element.55.send0, f32[128,512]{1,0:T(8,128)S(1)} %get-tuple-element.56.own, f32[128,512]{1,0:T(8,128)S(1)} %collective-permute-done.14.far, ...), custom_call_target="tpu_custom_call" | custom-call | tf_op jit(solution)/shard_map/pallas_call | solution.py:210
  61.9 0.9 collective-permute-done.17.recv0
  62.8 1.3 shard_map.51.own.rest_0_
  64.2 4.7 %collective-permute-start.18 = (f32[128,512]{1,0:T(8,128)S(1)}, f32[128,512]{1,0:T(8,128)S(1)}, u32[]{:S(2)}, u32[]{:S(2)}) collective-permute-start(f32[128,512]{1,0:T(8,128)S(1)} %shard_map.51.own.rest_0_), channel_id=1, source_target_pairs={{1,2},{3,4},{5,6},{7,8},{9,10},{11,12},{13,14},{2,1},{4,3},{6,5},{... | collective-permute-start | bytes 786440 | tf_op jit(solution)/shard_map/ppermute | solution.py:57
  69.0 5.1 %collective-permute-start.20 = (f32[128,512]{1,0:T(8,128)S(1)}, f32[128,512]{1,0:T(8,128)S(1)}, u32[]{:S(2)}, u32[]{:S(2)}) collective-permute-start(f32[128,512]{1,0:T(8,128)S(1)} %get-tuple-element.60.own.rest_0_), channel_id=1, source_target_pairs={{1,2},{3,4},{5,6},{7,8},{9,10},{11,12},{13,14},{2,1},{4,3},{6,5},{... | collective-permute-start | bytes 786440 | tf_op jit(solution)/shard_map/ppermute | solution.py:57
  74.2 1.2 shard_map.52
  75.4 0.7 collective-permute-start.22
  76.1 6.6 %collective-permute-start.23 = (f32[64,512]{1,0:T(8,128)S(1)}, f32[64,512]{1,0:T(8,128)S(1)}, u32[]{:S(2)}, u32[]{:S(2)}) collective-permute-start(f32[64,512]{1,0:T(8,128)S(1)} %get-tuple-element.59.send0), channel_id=1, source_target_pairs={{0,16},{32,48},{64,80},{96,112},{128,144},{160,176},{192,208},{224... | collective-permute-start | bytes 393224 | tf_op jit(solution)/shard_map/ppermute | solution.py:57
  82.8 1.6 %shard_map.53 = (f32[128,512]{1,0:T(8,128)S(1)}, f32[128,512]{1,0:T(8,128)S(1)}) custom-call(s32[4]{0:T(128)S(1)} %pad_add_fusion.where, f32[64,512]{1,0:T(8,128)S(1)} %get-tuple-element.58.send1, f32[64,512]{1,0:T(8,128)S(1)} %get-tuple-element.59.send0, f32[128,512]{1,0:T(8,128)S(1)} %get-tuple-element.60.own.rest_0_, ...), custom_call_target="tpu_custom_call" | custom-call | tf_op jit(solution)/shard_map/pallas_call | solution.py:210
  84.3 1.5 collective-permute-done.23.recv0
  85.9 0.8 shard_map.54.own
  86.7 3.6 %collective-permute-start.24 = (f32[128,512]{1,0:T(8,128)S(1)}, f32[128,512]{1,0:T(8,128)S(1)}, u32[]{:S(2)}, u32[]{:S(2)}) collective-permute-start(f32[128,512]{1,0:T(8,128)S(1)} %shard_map.54.own), channel_id=1, source_target_pairs={{1,2},{3,4},{5,6},{7,8},{9,10},{11,12},{13,14},{2,1},{4,3},{6,5},{... | collective-permute-start | bytes 786440 | tf_op jit(solution)/shard_map/ppermute | solution.py:57
  90.4 6.2 %collective-permute-start.26 = (f32[128,512]{1,0:T(8,128)S(1)}, f32[128,512]{1,0:T(8,128)S(1)}, u32[]{:S(2)}, u32[]{:S(2)}) collective-permute-start(f32[128,512]{1,0:T(8,128)S(1)} %get-tuple-element.64.own), channel_id=1, source_target_pairs={{1,2},{3,4},{5,6},{7,8},{9,10},{11,12},{13,14},{2,1},{4,3},{6,5},{... | collective-permute-start | bytes 786440 | tf_op jit(solution)/shard_map/ppermute | solution.py:57
  96.7 1.2 shard_map.55
  97.9 0.7 collective-permute-start.28
  98.6 7.7 %collective-permute-start.29 = (f32[64,512]{1,0:T(8,128)S(1)}, f32[64,512]{1,0:T(8,128)S(1)}, u32[]{:S(2)}, u32[]{:S(2)}) collective-permute-start(f32[64,512]{1,0:T(8,128)S(1)} %get-tuple-element.63.send0), channel_id=1, source_target_pairs={{0,16},{32,48},{64,80},{96,112},{128,144},{160,176},{192,208},{224... | collective-permute-start | bytes 393224 | tf_op jit(solution)/shard_map/ppermute | solution.py:57
  106.3 2.1 %shard_map.56 = (f32[128,512]{1,0:T(8,128)S(1)}, f32[128,512]{1,0:T(8,128)S(1)}, f32[1,256]{1,0:T(1,128)S(1)}) custom-call(s32[4]{0:T(128)S(1)} %pad_add_fusion.where, f32[64,512]{1,0:T(8,128)S(1)} %get-tuple-element.62.send1, f32[64,512]{1,0:T(8,128)S(1)} %get-tuple-element.63.send0, f32[128,512]{1,0:T(8,128)S(1)} %get-tuple-element.64.own, ...), custom_call_target="tpu_custom_call" | custom-call | tf_op jit(solution)/shard_map/pallas_call | solution.py:210
  108.4 1.0 collective-permute-done.29.recv0
  109.4 1.3 shard_map.57
  110.7 0.1 broadcast_in_dim.9
  110.9 42.9 %all_to_all.5 = f32[256,1,256]{2,1,0:T(1,128)S(1)} all-to-all(f32[256,1,256]{2,1,0:T(1,128)S(1)} %broadcast_in_dim.9), channel_id=1, replica_groups=mesh['gx'=16,'gz'=16] {'gx','gz'}, dimensions={0} | all-to-all | bytes 524288 | tf_op jit(solution)/shard_map/all_to_all | solution.py:271
  153.8 1.0 shard_map.58
  (40 shorter events, 0.9 us)
Async XLA Ops:
  0.7 1.0 copy-start
  2.5 9.6 %collective-permute-start = (f32[128,512]{1,0:T(8,128)S(1)}, f32[128,512]{1,0:T(8,128)S(1)}, u32[]{:S(2)}, u32[]{:S(2)}) collective-permute-start(f32[128,512]{1,0:T(8,128)S(1)} %get-tuple-element.37.own), channel_id=1, source_target_pairs={{1,2},{3,4},{5,6},{7,8},{9,10},{11,12},{13,14},{2,1},{4,3},{6,5},{... | collective-permute-start | bytes 786440 | tf_op jit(solution)/shard_map/ppermute | solution.py:57
  7.0 5.1 %collective-permute-start.1 = (f32[128,512]{1,0:T(8,128)S(1)}, f32[128,512]{1,0:T(8,128)S(1)}, u32[]{:S(2)}, u32[]{:S(2)}) collective-permute-start(f32[128,512]{1,0:T(8,128)S(1)} %get-tuple-element.37.own), channel_id=1, source_target_pairs={{0,1},{2,3},{4,5},{6,7},{8,9},{10,11},{12,13},{14,15},{1,0},{3,2},... | collective-permute-start | bytes 786440 | tf_op jit(solution)/shard_map/ppermute | solution.py:57
  7.1 10.8 %collective-permute-start.2 = (f32[128,512]{1,0:T(8,128)S(1)}, f32[128,512]{1,0:T(8,128)S(1)}, u32[]{:S(2)}, u32[]{:S(2)}) collective-permute-start(f32[128,512]{1,0:T(8,128)S(1)} %get-tuple-element.44.own), channel_id=1, source_target_pairs={{1,2},{3,4},{5,6},{7,8},{9,10},{11,12},{13,14},{2,1},{4,3},{6,5},{... | collective-permute-start | bytes 786440 | tf_op jit(solution)/shard_map/ppermute | solution.py:57
  10.6 7.3 %collective-permute-start.3 = (f32[128,512]{1,0:T(8,128)S(1)}, f32[128,512]{1,0:T(8,128)S(1)}, u32[]{:S(2)}, u32[]{:S(2)}) collective-permute-start(f32[128,512]{1,0:T(8,128)S(1)} %get-tuple-element.44.own), channel_id=1, source_target_pairs={{0,1},{2,3},{4,5},{6,7},{8,9},{10,11},{12,13},{14,15},{1,0},{3,2},... | collective-permute-start | bytes 786440 | tf_op jit(solution)/shard_map/ppermute | solution.py:57
  12.0 5.8 %copy-start.2 = (f32[8,32,512]{2,1,0:T(8,128)S(1)}, f32[8,32,512]{2,1,0:T(8,128)}, u32[]{:S(2)}) copy-start(f32[8,32,512]{2,1,0:T(8,128)} %whole.19) | copy-start | bytes 1572868
  13.3 6.8 %collective-permute-start.4 = (f32[64,512]{1,0:T(8,128)S(1)}, f32[64,512]{1,0:T(8,128)S(1)}, u32[]{:S(2)}, u32[]{:S(2)}) collective-permute-start(f32[64,512]{1,0:T(8,128)S(1)} %get-tuple-element.42.send1), channel_id=1, source_target_pairs={{16,32},{48,64},{80,96},{112,128},{144,160},{176,192},{208,224},{3... | collective-permute-start | bytes 393224 | tf_op jit(solution)/shard_map/ppermute | solution.py:57
  14.0 7.0 %collective-permute-start.5 = (f32[64,512]{1,0:T(8,128)S(1)}, f32[64,512]{1,0:T(8,128)S(1)}, u32[]{:S(2)}, u32[]{:S(2)}) collective-permute-start(f32[64,512]{1,0:T(8,128)S(1)} %get-tuple-element.43.send0), channel_id=1, source_target_pairs={{0,16},{32,48},{64,80},{96,112},{128,144},{160,176},{192,208},{224... | collective-permute-start | bytes 393224 | tf_op jit(solution)/shard_map/ppermute | solution.py:57
  22.3 8.3 %collective-permute-start.6 = (f32[128,512]{1,0:T(8,128)S(1)}, f32[128,512]{1,0:T(8,128)S(1)}, u32[]{:S(2)}, u32[]{:S(2)}) collective-permute-start(f32[128,512]{1,0:T(8,128)S(1)} %shard_map.45.own.rest_0_), channel_id=1, source_target_pairs={{1,2},{3,4},{5,6},{7,8},{9,10},{11,12},{13,14},{2,1},{4,3},{6,5},{... | collective-permute-start | bytes 786440 | tf_op jit(solution)/shard_map/ppermute | solution.py:57
  26.4 4.2 %collective-permute-start.7 = (f32[128,512]{1,0:T(8,128)S(1)}, f32[128,512]{1,0:T(8,128)S(1)}, u32[]{:S(2)}, u32[]{:S(2)}) collective-permute-start(f32[128,512]{1,0:T(8,128)S(1)} %shard_map.45.own.rest_0_), channel_id=1, source_target_pairs={{0,1},{2,3},{4,5},{6,7},{8,9},{10,11},{12,13},{14,15},{1,0},{3,2},... | collective-permute-start | bytes 786440 | tf_op jit(solution)/shard_map/ppermute | solution.py:57
  26.5 11.0 %copy-start.1 = (f32[8,32,512]{2,1,0:T(8,128)S(1)}, f32[8,32,512]{2,1,0:T(8,128)}, u32[]{:S(2)}) copy-start(f32[8,32,512]{2,1,0:T(8,128)} %rest_1_.1) | copy-start | bytes 1572868
  26.5 11.0 %collective-permute-start.8 = (f32[128,512]{1,0:T(8,128)S(1)}, f32[128,512]{1,0:T(8,128)S(1)}, u32[]{:S(2)}, u32[]{:S(2)}) collective-permute-start(f32[128,512]{1,0:T(8,128)S(1)} %get-tuple-element.52.own.rest_0_), channel_id=1, source_target_pairs={{1,2},{3,4},{5,6},{7,8},{9,10},{11,12},{13,14},{2,1},{4,3},{6,5},{... | collective-permute-start | bytes 786440 | tf_op jit(solution)/shard_map/ppermute | solution.py:57
  30.5 7.0 %collective-permute-start.9 = (f32[128,512]{1,0:T(8,128)S(1)}, f32[128,512]{1,0:T(8,128)S(1)}, u32[]{:S(2)}, u32[]{:S(2)}) collective-permute-start(f32[128,512]{1,0:T(8,128)S(1)} %get-tuple-element.52.own.rest_0_), channel_id=1, source_target_pairs={{0,1},{2,3},{4,5},{6,7},{8,9},{10,11},{12,13},{14,15},{1,0},{3,2},... | collective-permute-start | bytes 786440 | tf_op jit(solution)/shard_map/ppermute | solution.py:57
  31.8 7.2 %collective-permute-start.10 = (f32[64,512]{1,0:T(8,128)S(1)}, f32[64,512]{1,0:T(8,128)S(1)}, u32[]{:S(2)}, u32[]{:S(2)}) collective-permute-start(f32[64,512]{1,0:T(8,128)S(1)} %get-tuple-element.50.send1), channel_id=1, source_target_pairs={{16,32},{48,64},{80,96},{112,128},{144,160},{176,192},{208,224},{3... | collective-permute-start | bytes 393224 | tf_op jit(solution)/shard_map/ppermute | solution.py:57
  32.5 8.1 %collective-permute-start.11 = (f32[64,512]{1,0:T(8,128)S(1)}, f32[64,512]{1,0:T(8,128)S(1)}, u32[]{:S(2)}, u32[]{:S(2)}) collective-permute-start(f32[64,512]{1,0:T(8,128)S(1)} %get-tuple-element.51.send0), channel_id=1, source_target_pairs={{0,16},{32,48},{64,80},{96,112},{128,144},{160,176},{192,208},{224... | collective-permute-start | bytes 393224 | tf_op jit(solution)/shard_map/ppermute | solution.py:57
  41.4 9.2 %collective-permute-start.12 = (f32[128,512]{1,0:T(8,128)S(1)}, f32[128,512]{1,0:T(8,128)S(1)}, u32[]{:S(2)}, u32[]{:S(2)}) collective-permute-start(f32[128,512]{1,0:T(8,128)S(1)} %shard_map.48.own), channel_id=1, source_target_pairs={{1,2},{3,4},{5,6},{7,8},{9,10},{11,12},{13,14},{2,1},{4,3},{6,5},{... | collective-permute-start | bytes 786440 | tf_op jit(solution)/shard_map/ppermute | solution.py:57
  46.4 4.2 %collective-permute-start.13 = (f32[128,512]{1,0:T(8,128)S(1)}, f32[128,512]{1,0:T(8,128)S(1)}, u32[]{:S(2)}, u32[]{:S(2)}) collective-permute-start(f32[128,512]{1,0:T(8,128)S(1)} %shard_map.48.own), channel_id=1, source_target_pairs={{0,1},{2,3},{4,5},{6,7},{8,9},{10,11},{12,13},{14,15},{1,0},{3,2},... | collective-permute-start | bytes 786440 | tf_op jit(solution)/shard_map/ppermute | solution.py:57
  46.5 13.2 %collective-permute-start.14 = (f32[128,512]{1,0:T(8,128)S(1)}, f32[128,512]{1,0:T(8,128)S(1)}, u32[]{:S(2)}, u32[]{:S(2)}) collective-permute-start(f32[128,512]{1,0:T(8,128)S(1)} %get-tuple-element.56.own), channel_id=1, source_target_pairs={{1,2},{3,4},{5,6},{7,8},{9,10},{11,12},{13,14},{2,1},{4,3},{6,5},{... | collective-permute-start | bytes 786440 | tf_op jit(solution)/shard_map/ppermute | solution.py:57
  50.5 9.2 %collective-permute-start.15 = (f32[128,512]{1,0:T(8,128)S(1)}, f32[128,512]{1,0:T(8,128)S(1)}, u32[]{:S(2)}, u32[]{:S(2)}) collective-permute-start(f32[128,512]{1,0:T(8,128)S(1)} %get-tuple-element.56.own), channel_id=1, source_target_pairs={{0,1},{2,3},{4,5},{6,7},{8,9},{10,11},{12,13},{14,15},{1,0},{3,2},... | collective-permute-start | bytes 786440 | tf_op jit(solution)/shard_map/ppermute | solution.py:57
  51.8 10.0 %collective-permute-start.16 = (f32[64,512]{1,0:T(8,128)S(1)}, f32[64,512]{1,0:T(8,128)S(1)}, u32[]{:S(2)}, u32[]{:S(2)}) collective-permute-start(f32[64,512]{1,0:T(8,128)S(1)} %get-tuple-element.54.send1), channel_id=1, source_target_pairs={{16,32},{48,64},{80,96},{112,128},{144,160},{176,192},{208,224},{3... | collective-permute-start | bytes 393224 | tf_op jit(solution)/shard_map/ppermute | solution.py:57
  52.5 10.3 %collective-permute-start.17 = (f32[64,512]{1,0:T(8,128)S(1)}, f32[64,512]{1,0:T(8,128)S(1)}, u32[]{:S(2)}, u32[]{:S(2)}) collective-permute-start(f32[64,512]{1,0:T(8,128)S(1)} %get-tuple-element.55.send0), channel_id=1, source_target_pairs={{0,16},{32,48},{64,80},{96,112},{128,144},{160,176},{192,208},{224... | collective-permute-start | bytes 393224 | tf_op jit(solution)/shard_map/ppermute | solution.py:57
  64.2 10.1 %collective-permute-start.18 = (f32[128,512]{1,0:T(8,128)S(1)}, f32[128,512]{1,0:T(8,128)S(1)}, u32[]{:S(2)}, u32[]{:S(2)}) collective-permute-start(f32[128,512]{1,0:T(8,128)S(1)} %shard_map.51.own.rest_0_), channel_id=1, source_target_pairs={{1,2},{3,4},{5,6},{7,8},{9,10},{11,12},{13,14},{2,1},{4,3},{6,5},{... | collective-permute-start | bytes 786440 | tf_op jit(solution)/shard_map/ppermute | solution.py:57
  68.9 5.4 %collective-permute-start.19 = (f32[128,512]{1,0:T(8,128)S(1)}, f32[128,512]{1,0:T(8,128)S(1)}, u32[]{:S(2)}, u32[]{:S(2)}) collective-permute-start(f32[128,512]{1,0:T(8,128)S(1)} %shard_map.51.own.rest_0_), channel_id=1, source_target_pairs={{0,1},{2,3},{4,5},{6,7},{8,9},{10,11},{12,13},{14,15},{1,0},{3,2},... | collective-permute-start | bytes 786440 | tf_op jit(solution)/shard_map/ppermute | solution.py:57
  69.0 13.8 %collective-permute-start.20 = (f32[128,512]{1,0:T(8,128)S(1)}, f32[128,512]{1,0:T(8,128)S(1)}, u32[]{:S(2)}, u32[]{:S(2)}) collective-permute-start(f32[128,512]{1,0:T(8,128)S(1)} %get-tuple-element.60.own.rest_0_), channel_id=1, source_target_pairs={{1,2},{3,4},{5,6},{7,8},{9,10},{11,12},{13,14},{2,1},{4,3},{6,5},{... | collective-permute-start | bytes 786440 | tf_op jit(solution)/shard_map/ppermute | solution.py:57
  74.1 8.6 %collective-permute-start.21 = (f32[128,512]{1,0:T(8,128)S(1)}, f32[128,512]{1,0:T(8,128)S(1)}, u32[]{:S(2)}, u32[]{:S(2)}) collective-permute-start(f32[128,512]{1,0:T(8,128)S(1)} %get-tuple-element.60.own.rest_0_), channel_id=1, source_target_pairs={{0,1},{2,3},{4,5},{6,7},{8,9},{10,11},{12,13},{14,15},{1,0},{3,2},... | collective-permute-start | bytes 786440 | tf_op jit(solution)/shard_map/ppermute | solution.py:57
  75.4 8.9 %collective-permute-start.22 = (f32[64,512]{1,0:T(8,128)S(1)}, f32[64,512]{1,0:T(8,128)S(1)}, u32[]{:S(2)}, u32[]{:S(2)}) collective-permute-start(f32[64,512]{1,0:T(8,128)S(1)} %get-tuple-element.58.send1), channel_id=1, source_target_pairs={{16,32},{48,64},{80,96},{112,128},{144,160},{176,192},{208,224},{3... | collective-permute-start | bytes 393224 | tf_op jit(solution)/shard_map/ppermute | solution.py:57
  76.1 9.7 %collective-permute-start.23 = (f32[64,512]{1,0:T(8,128)S(1)}, f32[64,512]{1,0:T(8,128)S(1)}, u32[]{:S(2)}, u32[]{:S(2)}) collective-permute-start(f32[64,512]{1,0:T(8,128)S(1)} %get-tuple-element.59.send0), channel_id=1, source_target_pairs={{0,16},{32,48},{64,80},{96,112},{128,144},{160,176},{192,208},{224... | collective-permute-start | bytes 393224 | tf_op jit(solution)/shard_map/ppermute | solution.py:57
  86.7 10.0 %collective-permute-start.24 = (f32[128,512]{1,0:T(8,128)S(1)}, f32[128,512]{1,0:T(8,128)S(1)}, u32[]{:S(2)}, u32[]{:S(2)}) collective-permute-start(f32[128,512]{1,0:T(8,128)S(1)} %shard_map.54.own), channel_id=1, source_target_pairs={{1,2},{3,4},{5,6},{7,8},{9,10},{11,12},{13,14},{2,1},{4,3},{6,5},{... | collective-permute-start | bytes 786440 | tf_op jit(solution)/shard_map/ppermute | solution.py:57
  90.3 6.4 %collective-permute-start.25 = (f32[128,512]{1,0:T(8,128)S(1)}, f32[128,512]{1,0:T(8,128)S(1)}, u32[]{:S(2)}, u32[]{:S(2)}) collective-permute-start(f32[128,512]{1,0:T(8,128)S(1)} %shard_map.54.own), channel_id=1, source_target_pairs={{0,1},{2,3},{4,5},{6,7},{8,9},{10,11},{12,13},{14,15},{1,0},{3,2},... | collective-permute-start | bytes 786440 | tf_op jit(solution)/shard_map/ppermute | solution.py:57
  90.4 15.9 %collective-permute-start.26 = (f32[128,512]{1,0:T(8,128)S(1)}, f32[128,512]{1,0:T(8,128)S(1)}, u32[]{:S(2)}, u32[]{:S(2)}) collective-permute-start(f32[128,512]{1,0:T(8,128)S(1)} %get-tuple-element.64.own), channel_id=1, source_target_pairs={{1,2},{3,4},{5,6},{7,8},{9,10},{11,12},{13,14},{2,1},{4,3},{6,5},{... | collective-permute-start | bytes 786440 | tf_op jit(solution)/shard_map/ppermute | solution.py:57
  96.6 9.7 %collective-permute-start.27 = (f32[128,512]{1,0:T(8,128)S(1)}, f32[128,512]{1,0:T(8,128)S(1)}, u32[]{:S(2)}, u32[]{:S(2)}) collective-permute-start(f32[128,512]{1,0:T(8,128)S(1)} %get-tuple-element.64.own), channel_id=1, source_target_pairs={{0,1},{2,3},{4,5},{6,7},{8,9},{10,11},{12,13},{14,15},{1,0},{3,2},... | collective-permute-start | bytes 786440 | tf_op jit(solution)/shard_map/ppermute | solution.py:57
  97.9 10.5 %collective-permute-start.28 = (f32[64,512]{1,0:T(8,128)S(1)}, f32[64,512]{1,0:T(8,128)S(1)}, u32[]{:S(2)}, u32[]{:S(2)}) collective-permute-start(f32[64,512]{1,0:T(8,128)S(1)} %get-tuple-element.62.send1), channel_id=1, source_target_pairs={{16,32},{48,64},{80,96},{112,128},{144,160},{176,192},{208,224},{3... | collective-permute-start | bytes 393224 | tf_op jit(solution)/shard_map/ppermute | solution.py:57
  98.6 10.8 %collective-permute-start.29 = (f32[64,512]{1,0:T(8,128)S(1)}, f32[64,512]{1,0:T(8,128)S(1)}, u32[]{:S(2)}, u32[]{:S(2)}) collective-permute-start(f32[64,512]{1,0:T(8,128)S(1)} %get-tuple-element.63.send0), channel_id=1, source_target_pairs={{0,16},{32,48},{64,80},{96,112},{128,144},{160,176},{192,208},{224... | collective-permute-start | bytes 393224 | tf_op jit(solution)/shard_map/ppermute | solution.py:57
where the time goes:
time: 155 us
  starting transfers between devices  79.3 us (51%)
  blocking collectives  42.9 us (28%)
  Pallas kernels  24.2 us (16%)
  waiting for transfers between devices  5.93 us (4%)
    ppermute x30, starting transfers between devices, swap(): return lax.ppermute(value, axis, pairs + [(j, i) for i, j in pairs])  79.3 us
    all_to_all x1, blocking collectives, step(): lax.all_to_all(sums, ('gx', 'gz'), 0, 0, tiled=True)  42.9 us
    pallas_call x18, Pallas kernels, call(): pl.pallas_call(kernel, out_shape=[jax.ShapeDtypeStruct(shape, dtype) for...  24.2 us
    ppermute x30, waiting for transfers between devices, swap(): return lax.ppermute(value, axis, pairs + [(j, i) for i, j in pairs])  5.93 us
  transfers between devices with their start and end apart: 30, of which 5 were waited for; matrix products, arithmetic and copies ran while one was open for 0% of the time, Pallas kernels for 11%

commit v1 on v0

--- a/solution.py
+++ b/solution.py
@@ -29,11 +29,14 @@
     return jnp.where(jnp.abs(gap) <= HALF, raw, 0.0)
 
 
+def weights(gap):
+    return float(np.exp(-2.0 * gap * gap / (HALF * HALF)) / scale())
+
+
 def inside_mass(cell, whole):
     total = jnp.zeros(cell.shape, jnp.float32)
     for gap in range(-HALF, HALF + 1):
-        share = float(np.exp(-2.0 * gap * gap / (HALF * HALF)) / scale())
-        total += jnp.where((cell + gap >= 0) & (cell + gap < whole), share, 0.0)
+        total += jnp.where((cell + gap >= 0) & (cell + gap < whole), weights(gap), 0.0)
     return total
 
 
@@ -42,9 +45,15 @@
     return high, (value - high.astype(jnp.float32)).astype(jnp.bfloat16)
 
 
-def dot3(left, right):
+def stacked(value):
+    return jnp.concatenate(split(value), axis=0)
+
+
+def product(left, right, right_low):
     dot = functools.partial(jnp.dot, preferred_element_type=jnp.float32)
-    return dot(left[0], right[0]) + (dot(left[0], right[1]) + dot(left[1], right[0]))
+    rows = left.shape[0] // 2
+    both = dot(left, right)
+    return both[:rows] + (both[rows:] + dot(left[:rows], right_low))
 
 
 def iota(shape, dim):
@@ -65,24 +74,16 @@
     return jnp.concatenate([group(ref, at).reshape(-1, ref.shape[2]) for at in which], axis=0)
 
 
-def tables_kernel(depth, where, z_high, z_low, x_high, x_low, side_high, side_low, y_high, y_low):
-    even = where[1]
-    shape = z_high.shape
-    rows = shape[0]
-    row, col = iota(shape, 0), iota(shape, 1)
-    block, cell = col // rows, col % rows
-    far = jnp.where(even == 1, -depth, depth)
-    gap = row // HALF - cell // HALF - jnp.where(block == 0, 0, jnp.where(block == 1, far, -far))
-    z_high[...], z_low[...] = split(jnp.where(row % HALF == cell % HALF, weight(gap), 0.0))
-    shape = x_high.shape
-    row, col = iota(shape, 0), iota(shape, 1)
+def tables_kernel(x_table, first_table, last_table, y_high, y_low):
+    whole = x_table.shape[1]
+    rows = first_table.shape[1]
+    row, col = iota((whole, whole), 0), iota((whole, whole), 1)
     gap = row % HALF - col % HALF + HALF * (row // rows - col // rows)
     same = row % rows // HALF == col % rows // HALF
-    x_high[...], x_low[...] = split(jnp.where(same, weight(gap), 0.0))
-    shape = side_high.shape
-    row, col = iota(shape, 0), iota(shape, 1)
-    gap = row % HALF - col % HALF + jnp.where(row < rows, HALF, -HALF)
-    side_high[...], side_low[...] = split(jnp.where(row % rows // HALF == col // HALF, weight(gap), 0.0))
+    x_table[...] = stacked(jnp.where(same, weight(gap), 0.0))
+    row, col = iota((rows, rows), 0), iota((rows, rows), 1)
+    for ref, shift in ((first_table, HALF), (last_table, -HALF)):
+        ref[...] = stacked(jnp.where(row // HALF == col // HALF, weight(row % HALF - col % HALF + shift), 0.0))
     shape = y_high.shape
     y_high[...], y_low[...] = split(weight(iota(shape, 0) - iota(shape, 1)))
 
@@ -102,21 +103,30 @@
                 ref[start : start + HALF] = rho_prev[z, at * HALF : (at + 1) * HALF, :] / mass
 
 
-def zy(own, far, near, z_high, z_low, y_high, y_low, high, low):
-    rows = z_high.shape[0]
-    results = []
+def zy(even, own, far, near, y_high, y_low, lined):
+    rows, length = own.shape
+    rows //= 2
+    depth = rows // HALF
     for place in range(2):
         span = slice(place * rows, (place + 1) * rows)
-        for block, ref in enumerate((own, far, near)):
-            to = slice((3 * place + block) * rows, (3 * place + block + 1) * rows)
-            high[to], low[to] = split(ref[span])
-        at = slice(3 * place * rows, 3 * (place + 1) * rows)
-        results.append(dot3((z_high[...], z_low[...]), (high[at], low[at])))
-    return dot3(split(jnp.concatenate(results, axis=0)), (y_high[...], y_low[...]))
-
-
-def edge_kernel(where, own, far, near, z_high, z_low, y_high, y_low, send1, send0, high, low):
-    value = zy(own, far, near, z_high, z_low, y_high, y_low, high, low)
+        for at in range(0, length, LANES):
+            lanes = slice(at, at + LANES)
+            far_part, near_part = far[span, lanes], near[span, lanes]
+            before = jnp.where(even == 1, far_part, near_part)
+            after = jnp.where(even == 1, near_part, far_part)
+            line = [part[z * HALF : (z + 1) * HALF] for part in (before, own[span, lanes], after) for z in range(depth)]
+            for z in range(depth):
+                here = z + depth
+                total = weights(0) * line[here]
+                for gap in range(1, HALF + 1):
+                    total += weights(gap) * (line[here - gap] + line[here + gap])
+                to = place * rows + z * HALF
+                lined[to : to + HALF, lanes] = total
+    return product(stacked(lined[...]), y_high[...], y_low[...])
+
+
+def edge_kernel(where, own, far, near, y_high, y_low, send1, send0, lined):
+    value = zy(where[1], own, far, near, y_high, y_low, lined)
     rows = value.shape[0] // 2
     before, after = value[:rows], value[rows:]
     send0[...] = jnp.where(where[0] == 1, after, before)
@@ -144,22 +154,22 @@
     return sum(rows[:, i : i + LANES] for i in range(0, rows.shape[1], LANES))
 
 
-def inner_kernel(kind, started, where, send1, send0, own, far, near, z_high, z_low, y_high, y_low, x_high, x_low, whole, *rest):
+def inner_kernel(kind, started, where, send1, send0, own, far, near, y_high, y_low, x_table, whole, *rest):
     scaling = None
     if started:
         scaling, *rest = rest
     if kind == "last":
-        rho_prev, out, part, sums, high, low, zy_high, zy_low = rest
+        rho_prev, out, part, sums, lined, zy_high, zy_low = rest
     else:
-        out, part, high, low, zy_high, zy_low = rest
-    rows = z_high.shape[0]
-    value = zy(own, far, near, z_high, z_low, y_high, y_low, high, low)
+        out, part, lined, zy_high, zy_low = rest
+    rows = send1.shape[0]
+    value = zy(where[1], own, far, near, y_high, y_low, lined)
     before = jnp.where(where[0] == 1, send1[...], send0[...])
     after = jnp.where(where[0] == 1, send0[...], send1[...])
     zy_high[:rows], zy_low[:rows] = split(before)
     zy_high[rows : 3 * rows], zy_low[rows : 3 * rows] = split(value)
     zy_high[3 * rows :], zy_low[3 * rows :] = split(after)
-    along_x = dot3((x_high[...], x_low[...]), (zy_high[...], zy_low[...]))
+    along_x = product(x_table[...], zy_high[...], zy_low[...])
     part[:rows], part[rows:] = along_x[:rows], along_x[3 * rows :]
     result = finish(kind, along_x[rows : 3 * rows], INNER, whole, scaling)
     out[...] = result
@@ -169,7 +179,7 @@
         sums[:, LANES:] = lane_sums(result)
 
 
-def outer_kernel(kind, started, where, part, recv1, recv0, side_high, side_low, whole, *rest):
+def outer_kernel(kind, started, where, part, recv1, recv0, first_table, last_table, whole, *rest):
     scaling = None
     if started:
         scaling, *rest = rest
@@ -180,8 +190,8 @@
     rows = recv0.shape[0]
     before = split(jnp.where(where[0] == 1, recv1[...], recv0[...]))
     after = split(jnp.where(where[0] == 1, recv0[...], recv1[...]))
-    first = part[:rows] + dot3((side_high[:rows], side_low[:rows]), before)
-    second = part[rows:] + dot3((side_high[rows:], side_low[rows:]), after)
+    first = part[:rows] + product(first_table[...], *before)
+    second = part[rows:] + product(last_table[...], *after)
     result = finish(kind, jnp.concatenate([first, second], axis=0), EDGE, whole, scaling)
     out[...] = result
     if kind == "last":
@@ -224,26 +234,25 @@
     where = jnp.stack([1 - at_x % 2, 1 - at_z % 2, at_x * width, at_z * depth]).astype(jnp.int32)
     rows = depth * HALF
     one, two = (rows, length), (2 * rows, length)
-    zy_scratch = [pltpu.VMEM((6 * rows, length), jnp.bfloat16)] * 2
+    zy_scratch = [pltpu.VMEM((2 * rows, length), jnp.float32)]
     x_scratch = [pltpu.VMEM((4 * rows, length), jnp.bfloat16)] * 2
 
     first = functools.partial(first_kernel, (width * size_x, depth * size_z))
     edge, inner = call(first, (where, rho_prev), [two, two])
-    table_shapes = [(rows, 3 * rows), (4 * rows, 4 * rows), (2 * rows, rows), (length, length)]
-    doubled = [shape for shape in table_shapes for _ in range(2)]
-    tables = call(functools.partial(tables_kernel, depth), (where,), doubled, dtype=jnp.bfloat16)
-    z_table, x_table, side_table, y_table = (tuple(tables[i : i + 2]) for i in range(0, 8, 2))
+    table_shapes = [(8 * rows, 4 * rows), (2 * rows, rows), (2 * rows, rows), (length, length), (length, length)]
+    x_table, *side_table, y_high, y_low = call(tables_kernel, (), table_shapes, scalars=0, dtype=jnp.bfloat16)
+    y_table = (y_high, y_low)
 
     def heat_step(kind, edge, inner, whole, scaling):
         far_edge = swap(edge, "gz", 1)
         near_edge = swap(edge, "gz", 0)
         far_inner = swap(inner, "gz", 1)
         near_inner = swap(inner, "gz", 0)
-        sends = call(edge_kernel, (where, edge, far_edge, near_edge, *z_table, *y_table), [one, one], zy_scratch)
+        sends = call(edge_kernel, (where, edge, far_edge, near_edge, *y_table), [one, one], zy_scratch)
         recv1 = swap(sends[0], "gx", 1)
         recv0 = swap(sends[1], "gx", 0)
         started, last = scaling is not None, kind == "last"
-        inputs = (where, *sends, inner, far_inner, near_inner, *z_table, *y_table, *x_table, whole)
+        inputs = (where, *sends, inner, far_inner, near_inner, *y_table, x_table, whole)
         more = ((scaling[1],) if started else ()) + ((rho_prev,) if last else ())
         shapes = [two, two] + ([(1, 2 * LANES)] if last else [])
         new_inner, part, *sums = call(

time: 155 us -> 154 us (level)
  Pallas kernels: 24.2 us -> 22.4 us
    pallas_call x18, Pallas kernels: 24.2 us -> 22.4 us  [call(): pl.pallas_call(kernel, out_shape=[jax.ShapeDtypeStruct(shape, dtype) for...]
  transfers between devices with their start and end apart: 30 -> 30, of which waited for: 5 -> 5; matrix products, arithmetic and copies ran while one was open for 0% -> 0% of each run, Pallas kernels for 11% -> 10%
where the time goes in v1:
time: 154 us; the launch traced here: 153 us
  starting transfers between devices  79.3 us (51%)
  blocking collectives  42.8 us (28%)
  Pallas kernels  22.4 us (15%)
  waiting for transfers between devices  6.57 us (4%)
    ppermute x30, starting transfers between devices, swap(): return lax.ppermute(value, axis, pairs + [(j, i) for i, j in pairs])  79.3 us
    all_to_all x1, blocking collectives, step(): lax.all_to_all(sums, ('gx', 'gz'), 0, 0, tiled=True)  42.8 us
    pallas_call x18, Pallas kernels, call(): pl.pallas_call(kernel, out_shape=[jax.ShapeDtypeStruct(shape, dtype) for...  22.4 us
    ppermute x30, waiting for transfers between devices, swap(): return lax.ppermute(value, axis, pairs + [(j, i) for i, j in pairs])  6.57 us
  transfers between devices with their start and end apart: 30, of which 5 were waited for; matrix products, arithmetic and copies ran while one was open for 0% of the time, Pallas kernels for 10%

profile of v1, /device:TPU:1, one launch (start us, length us, event | category | flops | bytes accessed | tf_op | source)
XLA Modules:
  0.0 153.5 jit_solution(5076154508578998503)
XLA Ops:
  0.7 1.0 copy-done
  1.8 0.7 shard_map.41
  2.5 4.5 %collective-permute-start = (f32[128,512]{1,0:T(8,128)S(1)}, f32[128,512]{1,0:T(8,128)S(1)}, u32[]{:S(2)}, u32[]{:S(2)}) collective-permute-start(f32[128,512]{1,0:T(8,128)S(1)} %get-tuple-element.34.own), channel_id=1, source_target_pairs={{1,2},{3,4},{5,6},{7,8},{9,10},{11,12},{13,14},{2,1},{4,3},{6,5},{... | collective-permute-start | bytes 786440 | tf_op jit(solution)/shard_map/ppermute | solution.py:66
  7.0 0.1 collective-permute-start.1
  7.1 3.5 %collective-permute-start.2 = (f32[128,512]{1,0:T(8,128)S(1)}, f32[128,512]{1,0:T(8,128)S(1)}, u32[]{:S(2)}, u32[]{:S(2)}) collective-permute-start(f32[128,512]{1,0:T(8,128)S(1)} %get-tuple-element.39.own), channel_id=1, source_target_pairs={{1,2},{3,4},{5,6},{7,8},{9,10},{11,12},{13,14},{2,1},{4,3},{6,5},{... | collective-permute-start | bytes 786440 | tf_op jit(solution)/shard_map/ppermute | solution.py:66
  10.6 0.1 collective-permute-start.3
  10.7 0.8 shard_map.42
  11.5 1.1 shard_map.43
  12.6 0.7 collective-permute-start.4
  13.2 3.9 %collective-permute-start.5 = (f32[64,512]{1,0:T(8,128)S(1)}, f32[64,512]{1,0:T(8,128)S(1)}, u32[]{:S(2)}, u32[]{:S(2)}) collective-permute-start(f32[64,512]{1,0:T(8,128)S(1)} %get-tuple-element.38.send0), channel_id=1, source_target_pairs={{0,16},{32,48},{64,80},{96,112},{128,144},{160,176},{192,208},{224... | collective-permute-start | bytes 393224 | tf_op jit(solution)/shard_map/ppermute | solution.py:66
  17.2 2.0 %shard_map.44 = (f32[128,512]{1,0:T(8,128)S(1)}, f32[128,512]{1,0:T(8,128)S(1)}) custom-call(s32[4]{0:T(128)S(1)} %pad_add_fusion.where, f32[64,512]{1,0:T(8,128)S(1)} %get-tuple-element.37.send1, f32[64,512]{1,0:T(8,128)S(1)} %get-tuple-element.38.send0, f32[128,512]{1,0:T(8,128)S(1)} %get-tuple-element.39.own, f32[128,512]{1,0:T(8,128)S(1)} %collective-permute-done.2.far, ...), custom_call_target="tpu_custom_call" | custom-call | tf_op jit(solution)/shard_map/pallas_call | solution.py:220
  19.2 1.1 collective-permute-done.5.recv0
  20.3 1.3 shard_map.45.own.rest_0_
  21.6 4.1 %collective-permute-start.6 = (f32[128,512]{1,0:T(8,128)S(1)}, f32[128,512]{1,0:T(8,128)S(1)}, u32[]{:S(2)}, u32[]{:S(2)}) collective-permute-start(f32[128,512]{1,0:T(8,128)S(1)} %shard_map.45.own.rest_0_), channel_id=1, source_target_pairs={{1,2},{3,4},{5,6},{7,8},{9,10},{11,12},{13,14},{2,1},{4,3},{6,5},{... | collective-permute-start | bytes 786440 | tf_op jit(solution)/shard_map/ppermute | solution.py:66
  25.9 3.9 %collective-permute-start.8 = (f32[128,512]{1,0:T(8,128)S(1)}, f32[128,512]{1,0:T(8,128)S(1)}, u32[]{:S(2)}, u32[]{:S(2)}) collective-permute-start(f32[128,512]{1,0:T(8,128)S(1)} %get-tuple-element.46.own.rest_0_), channel_id=1, source_target_pairs={{1,2},{3,4},{5,6},{7,8},{9,10},{11,12},{13,14},{2,1},{4,3},{6,5},{... | collective-permute-start | bytes 786440 | tf_op jit(solution)/shard_map/ppermute | solution.py:66
  29.9 1.1 shard_map.46
  31.0 0.7 collective-permute-start.10
  31.7 5.0 %collective-permute-start.11 = (f32[64,512]{1,0:T(8,128)S(1)}, f32[64,512]{1,0:T(8,128)S(1)}, u32[]{:S(2)}, u32[]{:S(2)}) collective-permute-start(f32[64,512]{1,0:T(8,128)S(1)} %get-tuple-element.45.send0), channel_id=1, source_target_pairs={{0,16},{32,48},{64,80},{96,112},{128,144},{160,176},{192,208},{224... | collective-permute-start | bytes 393224 | tf_op jit(solution)/shard_map/ppermute | solution.py:66
  36.6 1.4 shard_map.47
  38.1 1.6 %collective-permute-done.11.recv0 = f32[64,512]{1,0:T(8,128)S(1)} collective-permute-done((f32[64,512]{1,0:T(8,128)S(1)}, f32[64,512]{1,0:T(8,128)S(1)}, u32[]{:S(2)}, u32[]{:S(2)}) %collective-permute-start.11) | collective-permute-done | bytes 131104 | tf_op jit(solution)/shard_map/ppermute | solution.py:66
  39.7 0.8 shard_map.48.own
  40.6 5.3 %collective-permute-start.12 = (f32[128,512]{1,0:T(8,128)S(1)}, f32[128,512]{1,0:T(8,128)S(1)}, u32[]{:S(2)}, u32[]{:S(2)}) collective-permute-start(f32[128,512]{1,0:T(8,128)S(1)} %shard_map.48.own), channel_id=1, source_target_pairs={{1,2},{3,4},{5,6},{7,8},{9,10},{11,12},{13,14},{2,1},{4,3},{6,5},{... | collective-permute-start | bytes 786440 | tf_op jit(solution)/shard_map/ppermute | solution.py:66
  46.0 3.9 %collective-permute-start.14 = (f32[128,512]{1,0:T(8,128)S(1)}, f32[128,512]{1,0:T(8,128)S(1)}, u32[]{:S(2)}, u32[]{:S(2)}) collective-permute-start(f32[128,512]{1,0:T(8,128)S(1)} %get-tuple-element.50.own), channel_id=1, source_target_pairs={{1,2},{3,4},{5,6},{7,8},{9,10},{11,12},{13,14},{2,1},{4,3},{6,5},{... | collective-permute-start | bytes 786440 | tf_op jit(solution)/shard_map/ppermute | solution.py:66
  49.9 1.1 shard_map.49
  51.0 0.7 collective-permute-start.16
  51.7 7.0 %collective-permute-start.17 = (f32[64,512]{1,0:T(8,128)S(1)}, f32[64,512]{1,0:T(8,128)S(1)}, u32[]{:S(2)}, u32[]{:S(2)}) collective-permute-start(f32[64,512]{1,0:T(8,128)S(1)} %get-tuple-element.49.send0), channel_id=1, source_target_pairs={{0,16},{32,48},{64,80},{96,112},{128,144},{160,176},{192,208},{224... | collective-permute-start | bytes 393224 | tf_op jit(solution)/shard_map/ppermute | solution.py:66
  58.7 2.0 %shard_map.50 = (f32[128,512]{1,0:T(8,128)S(1)}, f32[128,512]{1,0:T(8,128)S(1)}) custom-call(s32[4]{0:T(128)S(1)} %pad_add_fusion.where, f32[64,512]{1,0:T(8,128)S(1)} %get-tuple-element.48.send1, f32[64,512]{1,0:T(8,128)S(1)} %get-tuple-element.49.send0, f32[128,512]{1,0:T(8,128)S(1)} %get-tuple-element.50.own, f32[128,512]{1,0:T(8,128)S(1)} %collective-permute-done.14.far, ...), custom_call_target="tpu_custom_call" | custom-call | tf_op jit(solution)/shard_map/pallas_call | solution.py:220
  60.7 1.1 collective-permute-done.17.recv0
  61.8 1.3 shard_map.51.own.rest_0_
  63.2 4.7 %collective-permute-start.18 = (f32[128,512]{1,0:T(8,128)S(1)}, f32[128,512]{1,0:T(8,128)S(1)}, u32[]{:S(2)}, u32[]{:S(2)}) collective-permute-start(f32[128,512]{1,0:T(8,128)S(1)} %shard_map.51.own.rest_0_), channel_id=1, source_target_pairs={{1,2},{3,4},{5,6},{7,8},{9,10},{11,12},{13,14},{2,1},{4,3},{6,5},{... | collective-permute-start | bytes 786440 | tf_op jit(solution)/shard_map/ppermute | solution.py:66
  68.0 5.2 %collective-permute-start.20 = (f32[128,512]{1,0:T(8,128)S(1)}, f32[128,512]{1,0:T(8,128)S(1)}, u32[]{:S(2)}, u32[]{:S(2)}) collective-permute-start(f32[128,512]{1,0:T(8,128)S(1)} %get-tuple-element.54.own.rest_0_), channel_id=1, source_target_pairs={{1,2},{3,4},{5,6},{7,8},{9,10},{11,12},{13,14},{2,1},{4,3},{6,5},{... | collective-permute-start | bytes 786440 | tf_op jit(solution)/shard_map/ppermute | solution.py:66
  73.2 1.1 shard_map.52
  74.3 0.7 collective-permute-start.22
  75.0 6.6 %collective-permute-start.23 = (f32[64,512]{1,0:T(8,128)S(1)}, f32[64,512]{1,0:T(8,128)S(1)}, u32[]{:S(2)}, u32[]{:S(2)}) collective-permute-start(f32[64,512]{1,0:T(8,128)S(1)} %get-tuple-element.53.send0), channel_id=1, source_target_pairs={{0,16},{32,48},{64,80},{96,112},{128,144},{160,176},{192,208},{224... | collective-permute-start | bytes 393224 | tf_op jit(solution)/shard_map/ppermute | solution.py:66
  81.6 1.5 shard_map.53
  83.1 1.6 %collective-permute-done.23.recv0 = f32[64,512]{1,0:T(8,128)S(1)} collective-permute-done((f32[64,512]{1,0:T(8,128)S(1)}, f32[64,512]{1,0:T(8,128)S(1)}, u32[]{:S(2)}, u32[]{:S(2)}) %collective-permute-start.23) | collective-permute-done | bytes 131104 | tf_op jit(solution)/shard_map/ppermute | solution.py:66
  84.7 0.8 shard_map.54.own
  85.6 3.7 %collective-permute-start.24 = (f32[128,512]{1,0:T(8,128)S(1)}, f32[128,512]{1,0:T(8,128)S(1)}, u32[]{:S(2)}, u32[]{:S(2)}) collective-permute-start(f32[128,512]{1,0:T(8,128)S(1)} %shard_map.54.own), channel_id=1, source_target_pairs={{1,2},{3,4},{5,6},{7,8},{9,10},{11,12},{13,14},{2,1},{4,3},{6,5},{... | collective-permute-start | bytes 786440 | tf_op jit(solution)/shard_map/ppermute | solution.py:66
  89.4 6.1 %collective-permute-start.26 = (f32[128,512]{1,0:T(8,128)S(1)}, f32[128,512]{1,0:T(8,128)S(1)}, u32[]{:S(2)}, u32[]{:S(2)}) collective-permute-start(f32[128,512]{1,0:T(8,128)S(1)} %get-tuple-element.58.own), channel_id=1, source_target_pairs={{1,2},{3,4},{5,6},{7,8},{9,10},{11,12},{13,14},{2,1},{4,3},{6,5},{... | collective-permute-start | bytes 786440 | tf_op jit(solution)/shard_map/ppermute | solution.py:66
  95.6 1.1 shard_map.55
  96.7 0.7 collective-permute-start.28
  97.3 7.7 %collective-permute-start.29 = (f32[64,512]{1,0:T(8,128)S(1)}, f32[64,512]{1,0:T(8,128)S(1)}, u32[]{:S(2)}, u32[]{:S(2)}) collective-permute-start(f32[64,512]{1,0:T(8,128)S(1)} %get-tuple-element.57.send0), channel_id=1, source_target_pairs={{0,16},{32,48},{64,80},{96,112},{128,144},{160,176},{192,208},{224... | collective-permute-start | bytes 393224 | tf_op jit(solution)/shard_map/ppermute | solution.py:66
  105.1 2.0 %shard_map.56 = (f32[128,512]{1,0:T(8,128)S(1)}, f32[128,512]{1,0:T(8,128)S(1)}, f32[1,256]{1,0:T(1,128)S(1)}) custom-call(s32[4]{0:T(128)S(1)} %pad_add_fusion.where, f32[64,512]{1,0:T(8,128)S(1)} %get-tuple-element.56.send1, f32[64,512]{1,0:T(8,128)S(1)} %get-tuple-element.57.send0, f32[128,512]{1,0:T(8,128)S(1)} %get-tuple-element.58.own, ...), custom_call_target="tpu_custom_call" | custom-call | tf_op jit(solution)/shard_map/pallas_call | solution.py:220
  107.1 1.1 collective-permute-done.29.recv0
  108.2 1.3 shard_map.57
  109.5 0.1 broadcast_in_dim.9
  109.7 42.8 %all_to_all.5 = f32[256,1,256]{2,1,0:T(1,128)S(1)} all-to-all(f32[256,1,256]{2,1,0:T(1,128)S(1)} %broadcast_in_dim.9), channel_id=1, replica_groups=mesh['gx'=16,'gz'=16] {'gx','gz'}, dimensions={0} | all-to-all | bytes 524288 | tf_op jit(solution)/shard_map/all_to_all | solution.py:280
  152.5 1.0 shard_map.58
  (40 shorter events, 0.9 us)
Async XLA Ops:
  0.7 1.0 copy-start
  2.5 9.0 %collective-permute-start = (f32[128,512]{1,0:T(8,128)S(1)}, f32[128,512]{1,0:T(8,128)S(1)}, u32[]{:S(2)}, u32[]{:S(2)}) collective-permute-start(f32[128,512]{1,0:T(8,128)S(1)} %get-tuple-element.34.own), channel_id=1, source_target_pairs={{1,2},{3,4},{5,6},{7,8},{9,10},{11,12},{13,14},{2,1},{4,3},{6,5},{... | collective-permute-start | bytes 786440 | tf_op jit(solution)/shard_map/ppermute | solution.py:66
  7.0 4.5 %collective-permute-start.1 = (f32[128,512]{1,0:T(8,128)S(1)}, f32[128,512]{1,0:T(8,128)S(1)}, u32[]{:S(2)}, u32[]{:S(2)}) collective-permute-start(f32[128,512]{1,0:T(8,128)S(1)} %get-tuple-element.34.own), channel_id=1, source_target_pairs={{0,1},{2,3},{4,5},{6,7},{8,9},{10,11},{12,13},{14,15},{1,0},{3,2},... | collective-permute-start | bytes 786440 | tf_op jit(solution)/shard_map/ppermute | solution.py:66
  7.1 10.1 %collective-permute-start.2 = (f32[128,512]{1,0:T(8,128)S(1)}, f32[128,512]{1,0:T(8,128)S(1)}, u32[]{:S(2)}, u32[]{:S(2)}) collective-permute-start(f32[128,512]{1,0:T(8,128)S(1)} %get-tuple-element.39.own), channel_id=1, source_target_pairs={{1,2},{3,4},{5,6},{7,8},{9,10},{11,12},{13,14},{2,1},{4,3},{6,5},{... | collective-permute-start | bytes 786440 | tf_op jit(solution)/shard_map/ppermute | solution.py:66
  10.6 6.6 %collective-permute-start.3 = (f32[128,512]{1,0:T(8,128)S(1)}, f32[128,512]{1,0:T(8,128)S(1)}, u32[]{:S(2)}, u32[]{:S(2)}) collective-permute-start(f32[128,512]{1,0:T(8,128)S(1)} %get-tuple-element.39.own), channel_id=1, source_target_pairs={{0,1},{2,3},{4,5},{6,7},{8,9},{10,11},{12,13},{14,15},{1,0},{3,2},... | collective-permute-start | bytes 786440 | tf_op jit(solution)/shard_map/ppermute | solution.py:66
  11.5 5.7 %copy-start.2 = (f32[8,32,512]{2,1,0:T(8,128)S(1)}, f32[8,32,512]{2,1,0:T(8,128)}, u32[]{:S(2)}) copy-start(f32[8,32,512]{2,1,0:T(8,128)} %whole.19) | copy-start | bytes 1572868
  12.6 6.6 %collective-permute-start.4 = (f32[64,512]{1,0:T(8,128)S(1)}, f32[64,512]{1,0:T(8,128)S(1)}, u32[]{:S(2)}, u32[]{:S(2)}) collective-permute-start(f32[64,512]{1,0:T(8,128)S(1)} %get-tuple-element.37.send1), channel_id=1, source_target_pairs={{16,32},{48,64},{80,96},{112,128},{144,160},{176,192},{208,224},{3... | collective-permute-start | bytes 393224 | tf_op jit(solution)/shard_map/ppermute | solution.py:66
  13.2 7.0 %collective-permute-start.5 = (f32[64,512]{1,0:T(8,128)S(1)}, f32[64,512]{1,0:T(8,128)S(1)}, u32[]{:S(2)}, u32[]{:S(2)}) collective-permute-start(f32[64,512]{1,0:T(8,128)S(1)} %get-tuple-element.38.send0), channel_id=1, source_target_pairs={{0,16},{32,48},{64,80},{96,112},{128,144},{160,176},{192,208},{224... | collective-permute-start | bytes 393224 | tf_op jit(solution)/shard_map/ppermute | solution.py:66
  21.6 8.2 %collective-permute-start.6 = (f32[128,512]{1,0:T(8,128)S(1)}, f32[128,512]{1,0:T(8,128)S(1)}, u32[]{:S(2)}, u32[]{:S(2)}) collective-permute-start(f32[128,512]{1,0:T(8,128)S(1)} %shard_map.45.own.rest_0_), channel_id=1, source_target_pairs={{1,2},{3,4},{5,6},{7,8},{9,10},{11,12},{13,14},{2,1},{4,3},{6,5},{... | collective-permute-start | bytes 786440 | tf_op jit(solution)/shard_map/ppermute | solution.py:66
  25.8 4.1 %collective-permute-start.7 = (f32[128,512]{1,0:T(8,128)S(1)}, f32[128,512]{1,0:T(8,128)S(1)}, u32[]{:S(2)}, u32[]{:S(2)}) collective-permute-start(f32[128,512]{1,0:T(8,128)S(1)} %shard_map.45.own.rest_0_), channel_id=1, source_target_pairs={{0,1},{2,3},{4,5},{6,7},{8,9},{10,11},{12,13},{14,15},{1,0},{3,2},... | collective-permute-start | bytes 786440 | tf_op jit(solution)/shard_map/ppermute | solution.py:66
  25.9 10.8 %copy-start.1 = (f32[8,32,512]{2,1,0:T(8,128)S(1)}, f32[8,32,512]{2,1,0:T(8,128)}, u32[]{:S(2)}) copy-start(f32[8,32,512]{2,1,0:T(8,128)} %rest_1_.1) | copy-start | bytes 1572868
  25.9 10.8 %collective-permute-start.8 = (f32[128,512]{1,0:T(8,128)S(1)}, f32[128,512]{1,0:T(8,128)S(1)}, u32[]{:S(2)}, u32[]{:S(2)}) collective-permute-start(f32[128,512]{1,0:T(8,128)S(1)} %get-tuple-element.46.own.rest_0_), channel_id=1, source_target_pairs={{1,2},{3,4},{5,6},{7,8},{9,10},{11,12},{13,14},{2,1},{4,3},{6,5},{... | collective-permute-start | bytes 786440 | tf_op jit(solution)/shard_map/ppermute | solution.py:66
  29.8 6.9 %collective-permute-start.9 = (f32[128,512]{1,0:T(8,128)S(1)}, f32[128,512]{1,0:T(8,128)S(1)}, u32[]{:S(2)}, u32[]{:S(2)}) collective-permute-start(f32[128,512]{1,0:T(8,128)S(1)} %get-tuple-element.46.own.rest_0_), channel_id=1, source_target_pairs={{0,1},{2,3},{4,5},{6,7},{8,9},{10,11},{12,13},{14,15},{1,0},{3,2},... | collective-permute-start | bytes 786440 | tf_op jit(solution)/shard_map/ppermute | solution.py:66
  31.0 7.1 %collective-permute-start.10 = (f32[64,512]{1,0:T(8,128)S(1)}, f32[64,512]{1,0:T(8,128)S(1)}, u32[]{:S(2)}, u32[]{:S(2)}) collective-permute-start(f32[64,512]{1,0:T(8,128)S(1)} %get-tuple-element.44.send1), channel_id=1, source_target_pairs={{16,32},{48,64},{80,96},{112,128},{144,160},{176,192},{208,224},{3... | collective-permute-start | bytes 393224 | tf_op jit(solution)/shard_map/ppermute | solution.py:66
  31.7 8.1 %collective-permute-start.11 = (f32[64,512]{1,0:T(8,128)S(1)}, f32[64,512]{1,0:T(8,128)S(1)}, u32[]{:S(2)}, u32[]{:S(2)}) collective-permute-start(f32[64,512]{1,0:T(8,128)S(1)} %get-tuple-element.45.send0), channel_id=1, source_target_pairs={{0,16},{32,48},{64,80},{96,112},{128,144},{160,176},{192,208},{224... | collective-permute-start | bytes 393224 | tf_op jit(solution)/shard_map/ppermute | solution.py:66
  40.6 9.4 %collective-permute-start.12 = (f32[128,512]{1,0:T(8,128)S(1)}, f32[128,512]{1,0:T(8,128)S(1)}, u32[]{:S(2)}, u32[]{:S(2)}) collective-permute-start(f32[128,512]{1,0:T(8,128)S(1)} %shard_map.48.own), channel_id=1, source_target_pairs={{1,2},{3,4},{5,6},{7,8},{9,10},{11,12},{13,14},{2,1},{4,3},{6,5},{... | collective-permute-start | bytes 786440 | tf_op jit(solution)/shard_map/ppermute | solution.py:66
  45.9 4.1 %collective-permute-start.13 = (f32[128,512]{1,0:T(8,128)S(1)}, f32[128,512]{1,0:T(8,128)S(1)}, u32[]{:S(2)}, u32[]{:S(2)}) collective-permute-start(f32[128,512]{1,0:T(8,128)S(1)} %shard_map.48.own), channel_id=1, source_target_pairs={{0,1},{2,3},{4,5},{6,7},{8,9},{10,11},{12,13},{14,15},{1,0},{3,2},... | collective-permute-start | bytes 786440 | tf_op jit(solution)/shard_map/ppermute | solution.py:66
  46.0 12.8 %collective-permute-start.14 = (f32[128,512]{1,0:T(8,128)S(1)}, f32[128,512]{1,0:T(8,128)S(1)}, u32[]{:S(2)}, u32[]{:S(2)}) collective-permute-start(f32[128,512]{1,0:T(8,128)S(1)} %get-tuple-element.50.own), channel_id=1, source_target_pairs={{1,2},{3,4},{5,6},{7,8},{9,10},{11,12},{13,14},{2,1},{4,3},{6,5},{... | collective-permute-start | bytes 786440 | tf_op jit(solution)/shard_map/ppermute | solution.py:66
  49.8 8.9 %collective-permute-start.15 = (f32[128,512]{1,0:T(8,128)S(1)}, f32[128,512]{1,0:T(8,128)S(1)}, u32[]{:S(2)}, u32[]{:S(2)}) collective-permute-start(f32[128,512]{1,0:T(8,128)S(1)} %get-tuple-element.50.own), channel_id=1, source_target_pairs={{0,1},{2,3},{4,5},{6,7},{8,9},{10,11},{12,13},{14,15},{1,0},{3,2},... | collective-permute-start | bytes 786440 | tf_op jit(solution)/shard_map/ppermute | solution.py:66
  51.0 9.7 %collective-permute-start.16 = (f32[64,512]{1,0:T(8,128)S(1)}, f32[64,512]{1,0:T(8,128)S(1)}, u32[]{:S(2)}, u32[]{:S(2)}) collective-permute-start(f32[64,512]{1,0:T(8,128)S(1)} %get-tuple-element.48.send1), channel_id=1, source_target_pairs={{16,32},{48,64},{80,96},{112,128},{144,160},{176,192},{208,224},{3... | collective-permute-start | bytes 393224 | tf_op jit(solution)/shard_map/ppermute | solution.py:66
  51.7 10.1 %collective-permute-start.17 = (f32[64,512]{1,0:T(8,128)S(1)}, f32[64,512]{1,0:T(8,128)S(1)}, u32[]{:S(2)}, u32[]{:S(2)}) collective-permute-start(f32[64,512]{1,0:T(8,128)S(1)} %get-tuple-element.49.send0), channel_id=1, source_target_pairs={{0,16},{32,48},{64,80},{96,112},{128,144},{160,176},{192,208},{224... | collective-permute-start | bytes 393224 | tf_op jit(solution)/shard_map/ppermute | solution.py:66
  63.2 10.1 %collective-permute-start.18 = (f32[128,512]{1,0:T(8,128)S(1)}, f32[128,512]{1,0:T(8,128)S(1)}, u32[]{:S(2)}, u32[]{:S(2)}) collective-permute-start(f32[128,512]{1,0:T(8,128)S(1)} %shard_map.51.own.rest_0_), channel_id=1, source_target_pairs={{1,2},{3,4},{5,6},{7,8},{9,10},{11,12},{13,14},{2,1},{4,3},{6,5},{... | collective-permute-start | bytes 786440 | tf_op jit(solution)/shard_map/ppermute | solution.py:66
  67.8 5.4 %collective-permute-start.19 = (f32[128,512]{1,0:T(8,128)S(1)}, f32[128,512]{1,0:T(8,128)S(1)}, u32[]{:S(2)}, u32[]{:S(2)}) collective-permute-start(f32[128,512]{1,0:T(8,128)S(1)} %shard_map.51.own.rest_0_), channel_id=1, source_target_pairs={{0,1},{2,3},{4,5},{6,7},{8,9},{10,11},{12,13},{14,15},{1,0},{3,2},... | collective-permute-start | bytes 786440 | tf_op jit(solution)/shard_map/ppermute | solution.py:66
  68.0 13.7 %collective-permute-start.20 = (f32[128,512]{1,0:T(8,128)S(1)}, f32[128,512]{1,0:T(8,128)S(1)}, u32[]{:S(2)}, u32[]{:S(2)}) collective-permute-start(f32[128,512]{1,0:T(8,128)S(1)} %get-tuple-element.54.own.rest_0_), channel_id=1, source_target_pairs={{1,2},{3,4},{5,6},{7,8},{9,10},{11,12},{13,14},{2,1},{4,3},{6,5},{... | collective-permute-start | bytes 786440 | tf_op jit(solution)/shard_map/ppermute | solution.py:66
  73.1 8.5 %collective-permute-start.21 = (f32[128,512]{1,0:T(8,128)S(1)}, f32[128,512]{1,0:T(8,128)S(1)}, u32[]{:S(2)}, u32[]{:S(2)}) collective-permute-start(f32[128,512]{1,0:T(8,128)S(1)} %get-tuple-element.54.own.rest_0_), channel_id=1, source_target_pairs={{0,1},{2,3},{4,5},{6,7},{8,9},{10,11},{12,13},{14,15},{1,0},{3,2},... | collective-permute-start | bytes 786440 | tf_op jit(solution)/shard_map/ppermute | solution.py:66
  74.3 8.8 %collective-permute-start.22 = (f32[64,512]{1,0:T(8,128)S(1)}, f32[64,512]{1,0:T(8,128)S(1)}, u32[]{:S(2)}, u32[]{:S(2)}) collective-permute-start(f32[64,512]{1,0:T(8,128)S(1)} %get-tuple-element.52.send1), channel_id=1, source_target_pairs={{16,32},{48,64},{80,96},{112,128},{144,160},{176,192},{208,224},{3... | collective-permute-start | bytes 393224 | tf_op jit(solution)/shard_map/ppermute | solution.py:66
  75.0 9.7 %collective-permute-start.23 = (f32[64,512]{1,0:T(8,128)S(1)}, f32[64,512]{1,0:T(8,128)S(1)}, u32[]{:S(2)}, u32[]{:S(2)}) collective-permute-start(f32[64,512]{1,0:T(8,128)S(1)} %get-tuple-element.53.send0), channel_id=1, source_target_pairs={{0,16},{32,48},{64,80},{96,112},{128,144},{160,176},{192,208},{224... | collective-permute-start | bytes 393224 | tf_op jit(solution)/shard_map/ppermute | solution.py:66
  85.6 10.0 %collective-permute-start.24 = (f32[128,512]{1,0:T(8,128)S(1)}, f32[128,512]{1,0:T(8,128)S(1)}, u32[]{:S(2)}, u32[]{:S(2)}) collective-permute-start(f32[128,512]{1,0:T(8,128)S(1)} %shard_map.54.own), channel_id=1, source_target_pairs={{1,2},{3,4},{5,6},{7,8},{9,10},{11,12},{13,14},{2,1},{4,3},{6,5},{... | collective-permute-start | bytes 786440 | tf_op jit(solution)/shard_map/ppermute | solution.py:66
  89.3 6.3 %collective-permute-start.25 = (f32[128,512]{1,0:T(8,128)S(1)}, f32[128,512]{1,0:T(8,128)S(1)}, u32[]{:S(2)}, u32[]{:S(2)}) collective-permute-start(f32[128,512]{1,0:T(8,128)S(1)} %shard_map.54.own), channel_id=1, source_target_pairs={{0,1},{2,3},{4,5},{6,7},{8,9},{10,11},{12,13},{14,15},{1,0},{3,2},... | collective-permute-start | bytes 786440 | tf_op jit(solution)/shard_map/ppermute | solution.py:66
  89.4 15.7 %collective-permute-start.26 = (f32[128,512]{1,0:T(8,128)S(1)}, f32[128,512]{1,0:T(8,128)S(1)}, u32[]{:S(2)}, u32[]{:S(2)}) collective-permute-start(f32[128,512]{1,0:T(8,128)S(1)} %get-tuple-element.58.own), channel_id=1, source_target_pairs={{1,2},{3,4},{5,6},{7,8},{9,10},{11,12},{13,14},{2,1},{4,3},{6,5},{... | collective-permute-start | bytes 786440 | tf_op jit(solution)/shard_map/ppermute | solution.py:66
  95.5 9.6 %collective-permute-start.27 = (f32[128,512]{1,0:T(8,128)S(1)}, f32[128,512]{1,0:T(8,128)S(1)}, u32[]{:S(2)}, u32[]{:S(2)}) collective-permute-start(f32[128,512]{1,0:T(8,128)S(1)} %get-tuple-element.58.own), channel_id=1, source_target_pairs={{0,1},{2,3},{4,5},{6,7},{8,9},{10,11},{12,13},{14,15},{1,0},{3,2},... | collective-permute-start | bytes 786440 | tf_op jit(solution)/shard_map/ppermute | solution.py:66
  96.7 10.4 %collective-permute-start.28 = (f32[64,512]{1,0:T(8,128)S(1)}, f32[64,512]{1,0:T(8,128)S(1)}, u32[]{:S(2)}, u32[]{:S(2)}) collective-permute-start(f32[64,512]{1,0:T(8,128)S(1)} %get-tuple-element.56.send1), channel_id=1, source_target_pairs={{16,32},{48,64},{80,96},{112,128},{144,160},{176,192},{208,224},{3... | collective-permute-start | bytes 393224 | tf_op jit(solution)/shard_map/ppermute | solution.py:66
  97.3 10.8 %collective-permute-start.29 = (f32[64,512]{1,0:T(8,128)S(1)}, f32[64,512]{1,0:T(8,128)S(1)}, u32[]{:S(2)}, u32[]{:S(2)}) collective-permute-start(f32[64,512]{1,0:T(8,128)S(1)} %get-tuple-element.57.send0), channel_id=1, source_target_pairs={{0,16},{32,48},{64,80},{96,112},{128,144},{160,176},{192,208},{224... | collective-permute-start | bytes 393224 | tf_op jit(solution)/shard_map/ppermute | solution.py:66

commit v2 on v1

--- a/solution.py
+++ b/solution.py
@@ -64,6 +64,12 @@
     size = lax.axis_size(axis)
     pairs = [(i, i + 1) for i in range(first, size - 1, 2)]
     return lax.ppermute(value, axis, pairs + [(j, i) for i, j in pairs])
+
+
+def gather_pairs(value, axis):
+    size = lax.axis_size(axis)
+    pairs = [[i, (i + 1) % size] for i in range(1, size, 2)]
+    return lax.all_gather(value, axis, axis_index_groups=pairs, tiled=True)
 
 
 def group(ref, at):
@@ -103,8 +109,11 @@
                 ref[start : start + HALF] = rho_prev[z, at * HALF : (at + 1) * HALF, :] / mass
 
 
-def zy(even, own, far, near, y_high, y_low, lined):
+def zy(where, own, far, near, y_high, y_low, lined):
+    even = where[1]
     rows, length = own.shape
+    paired = far.shape[0] > rows
+    whole = rows
     rows //= 2
     depth = rows // HALF
     for place in range(2):
@@ -112,6 +121,9 @@
         for at in range(0, length, LANES):
             lanes = slice(at, at + LANES)
             far_part, near_part = far[span, lanes], near[span, lanes]
+            if paired:
+                second = far[whole + place * rows : whole + (place + 1) * rows, lanes]
+                far_part = jnp.where(where[4] == 1, jnp.where(even == 1, far_part, second), 0.0)
             before = jnp.where(even == 1, far_part, near_part)
             after = jnp.where(even == 1, near_part, far_part)
             line = [part[z * HALF : (z + 1) * HALF] for part in (before, own[span, lanes], after) for z in range(depth)]
@@ -126,7 +138,7 @@
 
 
 def edge_kernel(where, own, far, near, y_high, y_low, send1, send0, lined):
-    value = zy(where[1], own, far, near, y_high, y_low, lined)
+    value = zy(where, own, far, near, y_high, y_low, lined)
     rows = value.shape[0] // 2
     before, after = value[:rows], value[rows:]
     send0[...] = jnp.where(where[0] == 1, after, before)
@@ -163,7 +175,7 @@
     else:
         out, part, lined, zy_high, zy_low = rest
     rows = send1.shape[0]
-    value = zy(where[1], own, far, near, y_high, y_low, lined)
+    value = zy(where, own, far, near, y_high, y_low, lined)
     before = jnp.where(where[0] == 1, send1[...], send0[...])
     after = jnp.where(where[0] == 1, send0[...], send1[...])
     zy_high[:rows], zy_low[:rows] = split(before)
@@ -231,7 +243,8 @@
     depth, width, length = rho_prev.shape
     at_x, at_z = lax.axis_index("gx"), lax.axis_index("gz")
     size_x, size_z = lax.axis_size("gx"), lax.axis_size("gz")
-    where = jnp.stack([1 - at_x % 2, 1 - at_z % 2, at_x * width, at_z * depth]).astype(jnp.int32)
+    inside = (at_z > 0) & (at_z < size_z - 1)
+    where = jnp.stack([1 - at_x % 2, 1 - at_z % 2, at_x * width, at_z * depth, inside]).astype(jnp.int32)
     rows = depth * HALF
     one, two = (rows, length), (2 * rows, length)
     zy_scratch = [pltpu.VMEM((2 * rows, length), jnp.float32)]
@@ -244,8 +257,8 @@
     y_table = (y_high, y_low)
 
     def heat_step(kind, edge, inner, whole, scaling):
-        far_edge = swap(edge, "gz", 1)
         near_edge = swap(edge, "gz", 0)
+        far_edge = gather_pairs(edge, "gz")
         far_inner = swap(inner, "gz", 1)
         near_inner = swap(inner, "gz", 0)
         sends = call(edge_kernel, (where, edge, far_edge, near_edge, *y_table), [one, one], zy_scratch)

time: 154 us -> 169 us (1.097)
  blocking collectives: 42.8 us -> 84.5 us
  starting transfers between devices: 79.3 us -> 53.9 us
    all_gather x0 -> x5, blocking collectives: none -> 42.8 us  [gather_pairs(): return lax.all_gather(value, axis, axis_index_groups=pairs, tiled=True)]
    ppermute x30 -> x25, starting transfers between devices: 79.3 us -> 53.9 us  [swap(): return lax.ppermute(value, axis, pairs + [(j, i) for i, j in pairs])]
    ppermute x30 -> x25, waiting for transfers between devices: 6.57 us -> 5.09 us  [swap(): return lax.ppermute(value, axis, pairs + [(j, i) for i, j in pairs])]
  transfers between devices with their start and end apart: 30 -> 25, of which waited for: 5 -> 5; matrix products, arithmetic and copies ran while one was open for 0% -> 0% of each run, Pallas kernels for 10% -> 9%
where the time goes in v2:
time: 169 us; the launch traced here: 168 us
  blocking collectives  84.5 us (50%)
  starting transfers between devices  53.9 us (32%)
  Pallas kernels  22.5 us (13%)
  waiting for transfers between devices  5.09 us (3%)
    ppermute x25, starting transfers between devices, swap(): return lax.ppermute(value, axis, pairs + [(j, i) for i, j in pairs])  53.9 us
    all_gather x5, blocking collectives, gather_pairs(): return lax.all_gather(value, axis, axis_index_groups=pairs, tiled=True)  42.8 us
    all_to_all x1, blocking collectives, step(): lax.all_to_all(sums, ('gx', 'gz'), 0, 0, tiled=True)  41.6 us
    pallas_call x18, Pallas kernels, call(): pl.pallas_call(kernel, out_shape=[jax.ShapeDtypeStruct(shape, dtype) for...  22.5 us
    ppermute x25, waiting for transfers between devices, swap(): return lax.ppermute(value, axis, pairs + [(j, i) for i, j in pairs])  5.09 us
  transfers between devices with their start and end apart: 25, of which 5 were waited for; matrix products, arithmetic and copies ran while one was open for 0% of the time, Pallas kernels for 9%

profile of v2, /device:TPU:1, one launch (start us, length us, event | category | flops | bytes accessed | tf_op | source)
XLA Modules:
  0.0 168.3 jit_solution(15423070185630278056)
XLA Ops:
  0.7 1.0 copy-done
  1.8 0.7 shard_map.41
  2.5 3.3 %collective-permute-start = (f32[128,512]{1,0:T(8,128)S(1)}, f32[128,512]{1,0:T(8,128)S(1)}, u32[]{:S(2)}, u32[]{:S(2)}) collective-permute-start(f32[128,512]{1,0:T(8,128)S(1)} %get-tuple-element.34.own), channel_id=1, source_target_pairs={{0,1},{2,3},{4,5},{6,7},{8,9},{10,11},{12,13},{14,15},{1,0},{3,2},... | collective-permute-start | bytes 786440 | tf_op jit(solution)/shard_map/ppermute | solution.py:66
  5.8 1.9 %collective-permute-start.1 = (f32[128,512]{1,0:T(8,128)S(1)}, f32[128,512]{1,0:T(8,128)S(1)}, u32[]{:S(2)}, u32[]{:S(2)}) collective-permute-start(f32[128,512]{1,0:T(8,128)S(1)} %get-tuple-element.39.own), channel_id=1, source_target_pairs={{1,2},{3,4},{5,6},{7,8},{9,10},{11,12},{13,14},{2,1},{4,3},{6,5},{... | collective-permute-start | bytes 786440 | tf_op jit(solution)/shard_map/ppermute | solution.py:66
  7.8 0.8 shard_map.42
  8.6 8.0 %all_gather.15.far = f32[256,512]{1,0:T(8,128)S(1)} all-gather(f32[128,512]{1,0:T(8,128)S(1)} %get-tuple-element.34.own), channel_id=1, replica_groups={{1,2},{3,4},{5,6},{7,8},{9,10},{11,12},{13,14},{15,0},{17,18},{19,20},{..., dimensions={0}, use_global_device_ids=true | all-gather | bytes 786432 | tf_op jit(solution)/shard_map/all_gather | solution.py:72
  16.5 1.1 shard_map.43
  17.7 0.7 collective-permute-start.3
  18.3 2.2 %collective-permute-start.4 = (f32[64,512]{1,0:T(8,128)S(1)}, f32[64,512]{1,0:T(8,128)S(1)}, u32[]{:S(2)}, u32[]{:S(2)}) collective-permute-start(f32[64,512]{1,0:T(8,128)S(1)} %get-tuple-element.38.send0), channel_id=1, source_target_pairs={{0,16},{32,48},{64,80},{96,112},{128,144},{160,176},{192,208},{224... | collective-permute-start | bytes 393224 | tf_op jit(solution)/shard_map/ppermute | solution.py:66
  20.6 2.0 %shard_map.44 = (f32[128,512]{1,0:T(8,128)S(1)}, f32[128,512]{1,0:T(8,128)S(1)}) custom-call(s32[5]{0:T(128)S(1)} %stack.27.where, f32[64,512]{1,0:T(8,128)S(1)} %get-tuple-element.37.send1, f32[64,512]{1,0:T(8,128)S(1)} %get-tuple-element.38.send0, f32[128,512]{1,0:T(8,128)S(1)} %get-tuple-element.39.own, f32[128,512]{1,0:T(8,128)S(1)} %collective-permute-done.1.far, ...), custom_call_target="tpu_custom_call" | custom-call | tf_op jit(solution)/shard_map/pallas_call | solution.py:232
  22.9 1.3 shard_map.45.own.rest_0_
  24.3 3.4 %collective-permute-start.5 = (f32[128,512]{1,0:T(8,128)S(1)}, f32[128,512]{1,0:T(8,128)S(1)}, u32[]{:S(2)}, u32[]{:S(2)}) collective-permute-start(f32[128,512]{1,0:T(8,128)S(1)} %shard_map.45.own.rest_0_), channel_id=1, source_target_pairs={{0,1},{2,3},{4,5},{6,7},{8,9},{10,11},{12,13},{14,15},{1,0},{3,2},... | collective-permute-start | bytes 786440 | tf_op jit(solution)/shard_map/ppermute | solution.py:66
  27.7 1.9 %collective-permute-start.6 = (f32[128,512]{1,0:T(8,128)S(1)}, f32[128,512]{1,0:T(8,128)S(1)}, u32[]{:S(2)}, u32[]{:S(2)}) collective-permute-start(f32[128,512]{1,0:T(8,128)S(1)} %get-tuple-element.46.own.rest_0_), channel_id=1, source_target_pairs={{1,2},{3,4},{5,6},{7,8},{9,10},{11,12},{13,14},{2,1},{4,3},{6,5},{... | collective-permute-start | bytes 786440 | tf_op jit(solution)/shard_map/ppermute | solution.py:66
  29.7 8.7 %all_gather.16.far = f32[256,512]{1,0:T(8,128)S(1)} all-gather(f32[128,512]{1,0:T(8,128)S(1)} %shard_map.45.own.rest_0_), channel_id=1, replica_groups={{1,2},{3,4},{5,6},{7,8},{9,10},{11,12},{13,14},{15,0},{17,18},{19,20},{..., dimensions={0}, use_global_device_ids=true | all-gather | bytes 786432 | tf_op jit(solution)/shard_map/all_gather | solution.py:72
  38.4 1.1 shard_map.46
  39.5 0.7 collective-permute-start.8
  40.2 5.0 %collective-permute-start.9 = (f32[64,512]{1,0:T(8,128)S(1)}, f32[64,512]{1,0:T(8,128)S(1)}, u32[]{:S(2)}, u32[]{:S(2)}) collective-permute-start(f32[64,512]{1,0:T(8,128)S(1)} %get-tuple-element.45.send0), channel_id=1, source_target_pairs={{0,16},{32,48},{64,80},{96,112},{128,144},{160,176},{192,208},{224... | collective-permute-start | bytes 393224 | tf_op jit(solution)/shard_map/ppermute | solution.py:66
  45.2 1.4 shard_map.47
  46.6 1.7 %collective-permute-done.9.recv0 = f32[64,512]{1,0:T(8,128)S(1)} collective-permute-done((f32[64,512]{1,0:T(8,128)S(1)}, f32[64,512]{1,0:T(8,128)S(1)}, u32[]{:S(2)}, u32[]{:S(2)}) %collective-permute-start.9) | collective-permute-done | bytes 131104 | tf_op jit(solution)/shard_map/ppermute | solution.py:66
  48.4 0.8 shard_map.48.own
  49.2 1.3 collective-permute-start.10
  50.5 1.9 %collective-permute-start.11 = (f32[128,512]{1,0:T(8,128)S(1)}, f32[128,512]{1,0:T(8,128)S(1)}, u32[]{:S(2)}, u32[]{:S(2)}) collective-permute-start(f32[128,512]{1,0:T(8,128)S(1)} %get-tuple-element.50.own), channel_id=1, source_target_pairs={{1,2},{3,4},{5,6},{7,8},{9,10},{11,12},{13,14},{2,1},{4,3},{6,5},{... | collective-permute-start | bytes 786440 | tf_op jit(solution)/shard_map/ppermute | solution.py:66
  52.5 8.7 %all_gather.17.far = f32[256,512]{1,0:T(8,128)S(1)} all-gather(f32[128,512]{1,0:T(8,128)S(1)} %shard_map.48.own), channel_id=1, replica_groups={{1,2},{3,4},{5,6},{7,8},{9,10},{11,12},{13,14},{15,0},{17,18},{19,20},{..., dimensions={0}, use_global_device_ids=true | all-gather | bytes 786432 | tf_op jit(solution)/shard_map/all_gather | solution.py:72
  61.2 1.1 shard_map.49
  62.3 0.7 collective-permute-start.13
  63.0 7.2 %collective-permute-start.14 = (f32[64,512]{1,0:T(8,128)S(1)}, f32[64,512]{1,0:T(8,128)S(1)}, u32[]{:S(2)}, u32[]{:S(2)}) collective-permute-start(f32[64,512]{1,0:T(8,128)S(1)} %get-tuple-element.49.send0), channel_id=1, source_target_pairs={{0,16},{32,48},{64,80},{96,112},{128,144},{160,176},{192,208},{224... | collective-permute-start | bytes 393224 | tf_op jit(solution)/shard_map/ppermute | solution.py:66
  70.1 2.0 %shard_map.50 = (f32[128,512]{1,0:T(8,128)S(1)}, f32[128,512]{1,0:T(8,128)S(1)}) custom-call(s32[5]{0:T(128)S(1)} %stack.27.where, f32[64,512]{1,0:T(8,128)S(1)} %get-tuple-element.48.send1, f32[64,512]{1,0:T(8,128)S(1)} %get-tuple-element.49.send0, f32[128,512]{1,0:T(8,128)S(1)} %get-tuple-element.50.own, f32[128,512]{1,0:T(8,128)S(1)} %collective-permute-done.11.far, ...), custom_call_target="tpu_custom_call" | custom-call | tf_op jit(solution)/shard_map/pallas_call | solution.py:232
  72.2 0.8 collective-permute-done.14.recv0
  73.0 1.3 shard_map.51.own.rest_0_
  74.3 1.7 collective-permute-start.15
  76.0 1.9 %collective-permute-start.16 = (f32[128,512]{1,0:T(8,128)S(1)}, f32[128,512]{1,0:T(8,128)S(1)}, u32[]{:S(2)}, u32[]{:S(2)}) collective-permute-start(f32[128,512]{1,0:T(8,128)S(1)} %get-tuple-element.54.own.rest_0_), channel_id=1, source_target_pairs={{1,2},{3,4},{5,6},{7,8},{9,10},{11,12},{13,14},{2,1},{4,3},{6,5},{... | collective-permute-start | bytes 786440 | tf_op jit(solution)/shard_map/ppermute | solution.py:66
  78.0 8.8 %all_gather.18.far = f32[256,512]{1,0:T(8,128)S(1)} all-gather(f32[128,512]{1,0:T(8,128)S(1)} %shard_map.51.own.rest_0_), channel_id=1, replica_groups={{1,2},{3,4},{5,6},{7,8},{9,10},{11,12},{13,14},{15,0},{17,18},{19,20},{..., dimensions={0}, use_global_device_ids=true | all-gather | bytes 786432 | tf_op jit(solution)/shard_map/all_gather | solution.py:72
  86.8 1.1 shard_map.52
  87.9 0.7 collective-permute-start.18
  88.6 7.8 %collective-permute-start.19 = (f32[64,512]{1,0:T(8,128)S(1)}, f32[64,512]{1,0:T(8,128)S(1)}, u32[]{:S(2)}, u32[]{:S(2)}) collective-permute-start(f32[64,512]{1,0:T(8,128)S(1)} %get-tuple-element.53.send0), channel_id=1, source_target_pairs={{0,16},{32,48},{64,80},{96,112},{128,144},{160,176},{192,208},{224... | collective-permute-start | bytes 393224 | tf_op jit(solution)/shard_map/ppermute | solution.py:66
  96.4 1.4 shard_map.53
  97.9 1.4 collective-permute-done.19.recv0
  99.3 0.8 shard_map.54.own
  100.1 1.7 %collective-permute-start.20 = (f32[128,512]{1,0:T(8,128)S(1)}, f32[128,512]{1,0:T(8,128)S(1)}, u32[]{:S(2)}, u32[]{:S(2)}) collective-permute-start(f32[128,512]{1,0:T(8,128)S(1)} %shard_map.54.own), channel_id=1, source_target_pairs={{0,1},{2,3},{4,5},{6,7},{8,9},{10,11},{12,13},{14,15},{1,0},{3,2},... | collective-permute-start | bytes 786440 | tf_op jit(solution)/shard_map/ppermute | solution.py:66
  101.8 1.9 %collective-permute-start.21 = (f32[128,512]{1,0:T(8,128)S(1)}, f32[128,512]{1,0:T(8,128)S(1)}, u32[]{:S(2)}, u32[]{:S(2)}) collective-permute-start(f32[128,512]{1,0:T(8,128)S(1)} %get-tuple-element.58.own), channel_id=1, source_target_pairs={{1,2},{3,4},{5,6},{7,8},{9,10},{11,12},{13,14},{2,1},{4,3},{6,5},{... | collective-permute-start | bytes 786440 | tf_op jit(solution)/shard_map/ppermute | solution.py:66
  103.8 8.8 %all_gather.19.far = f32[256,512]{1,0:T(8,128)S(1)} all-gather(f32[128,512]{1,0:T(8,128)S(1)} %shard_map.54.own), channel_id=1, replica_groups={{1,2},{3,4},{5,6},{7,8},{9,10},{11,12},{13,14},{15,0},{17,18},{19,20},{..., dimensions={0}, use_global_device_ids=true | all-gather | bytes 786432 | tf_op jit(solution)/shard_map/all_gather | solution.py:72
  112.6 1.1 shard_map.55
  114.4 7.0 %collective-permute-start.24 = (f32[64,512]{1,0:T(8,128)S(1)}, f32[64,512]{1,0:T(8,128)S(1)}, u32[]{:S(2)}, u32[]{:S(2)}) collective-permute-start(f32[64,512]{1,0:T(8,128)S(1)} %get-tuple-element.57.send0), channel_id=1, source_target_pairs={{0,16},{32,48},{64,80},{96,112},{128,144},{160,176},{192,208},{224... | collective-permute-start | bytes 393224 | tf_op jit(solution)/shard_map/ppermute | solution.py:66
  121.3 2.0 %shard_map.56 = (f32[128,512]{1,0:T(8,128)S(1)}, f32[128,512]{1,0:T(8,128)S(1)}, f32[1,256]{1,0:T(1,128)S(1)}) custom-call(s32[5]{0:T(128)S(1)} %stack.27.where, f32[64,512]{1,0:T(8,128)S(1)} %get-tuple-element.56.send1, f32[64,512]{1,0:T(8,128)S(1)} %get-tuple-element.57.send0, f32[128,512]{1,0:T(8,128)S(1)} %get-tuple-element.58.own, ...), custom_call_target="tpu_custom_call" | custom-call | tf_op jit(solution)/shard_map/pallas_call | solution.py:232
  123.3 0.8 collective-permute-done.24.recv0
  124.1 1.3 shard_map.57
  125.6 41.6 %all_to_all.5 = f32[256,1,256]{2,1,0:T(1,128)S(1)} all-to-all(f32[256,1,256]{2,1,0:T(1,128)S(1)} %broadcast_in_dim.9), channel_id=1, replica_groups=mesh['gx'=16,'gz'=16] {'gx','gz'}, dimensions={0} | all-to-all | bytes 524288 | tf_op jit(solution)/shard_map/all_to_all | solution.py:293
  167.3 1.0 shard_map.58
  (35 shorter events, 1.7 us)
Async XLA Ops:
  0.7 1.0 copy-start
  2.5 14.1 %collective-permute-start = (f32[128,512]{1,0:T(8,128)S(1)}, f32[128,512]{1,0:T(8,128)S(1)}, u32[]{:S(2)}, u32[]{:S(2)}) collective-permute-start(f32[128,512]{1,0:T(8,128)S(1)} %get-tuple-element.34.own), channel_id=1, source_target_pairs={{0,1},{2,3},{4,5},{6,7},{8,9},{10,11},{12,13},{14,15},{1,0},{3,2},... | collective-permute-start | bytes 786440 | tf_op jit(solution)/shard_map/ppermute | solution.py:66
  5.8 14.8 %collective-permute-start.1 = (f32[128,512]{1,0:T(8,128)S(1)}, f32[128,512]{1,0:T(8,128)S(1)}, u32[]{:S(2)}, u32[]{:S(2)}) collective-permute-start(f32[128,512]{1,0:T(8,128)S(1)} %get-tuple-element.39.own), channel_id=1, source_target_pairs={{1,2},{3,4},{5,6},{7,8},{9,10},{11,12},{13,14},{2,1},{4,3},{6,5},{... | collective-permute-start | bytes 786440 | tf_op jit(solution)/shard_map/ppermute | solution.py:66
  7.7 12.9 %collective-permute-start.2 = (f32[128,512]{1,0:T(8,128)S(1)}, f32[128,512]{1,0:T(8,128)S(1)}, u32[]{:S(2)}, u32[]{:S(2)}) collective-permute-start(f32[128,512]{1,0:T(8,128)S(1)} %get-tuple-element.39.own), channel_id=1, source_target_pairs={{0,1},{2,3},{4,5},{6,7},{8,9},{10,11},{12,13},{14,15},{1,0},{3,2},... | collective-permute-start | bytes 786440 | tf_op jit(solution)/shard_map/ppermute | solution.py:66
  16.5 4.0 %copy-start.2 = (f32[8,32,512]{2,1,0:T(8,128)S(1)}, f32[8,32,512]{2,1,0:T(8,128)}, u32[]{:S(2)}) copy-start(f32[8,32,512]{2,1,0:T(8,128)} %whole.19) | copy-start | bytes 1572868
  17.7 4.9 %collective-permute-start.3 = (f32[64,512]{1,0:T(8,128)S(1)}, f32[64,512]{1,0:T(8,128)S(1)}, u32[]{:S(2)}, u32[]{:S(2)}) collective-permute-start(f32[64,512]{1,0:T(8,128)S(1)} %get-tuple-element.37.send1), channel_id=1, source_target_pairs={{16,32},{48,64},{80,96},{112,128},{144,160},{176,192},{208,224},{3... | collective-permute-start | bytes 393224 | tf_op jit(solution)/shard_map/ppermute | solution.py:66
  18.3 4.6 %collective-permute-start.4 = (f32[64,512]{1,0:T(8,128)S(1)}, f32[64,512]{1,0:T(8,128)S(1)}, u32[]{:S(2)}, u32[]{:S(2)}) collective-permute-start(f32[64,512]{1,0:T(8,128)S(1)} %get-tuple-element.38.send0), channel_id=1, source_target_pairs={{0,16},{32,48},{64,80},{96,112},{128,144},{160,176},{192,208},{224... | collective-permute-start | bytes 393224 | tf_op jit(solution)/shard_map/ppermute | solution.py:66
  24.3 14.1 %collective-permute-start.5 = (f32[128,512]{1,0:T(8,128)S(1)}, f32[128,512]{1,0:T(8,128)S(1)}, u32[]{:S(2)}, u32[]{:S(2)}) collective-permute-start(f32[128,512]{1,0:T(8,128)S(1)} %shard_map.45.own.rest_0_), channel_id=1, source_target_pairs={{0,1},{2,3},{4,5},{6,7},{8,9},{10,11},{12,13},{14,15},{1,0},{3,2},... | collective-permute-start | bytes 786440 | tf_op jit(solution)/shard_map/ppermute | solution.py:66
  27.7 17.5 %collective-permute-start.6 = (f32[128,512]{1,0:T(8,128)S(1)}, f32[128,512]{1,0:T(8,128)S(1)}, u32[]{:S(2)}, u32[]{:S(2)}) collective-permute-start(f32[128,512]{1,0:T(8,128)S(1)} %get-tuple-element.46.own.rest_0_), channel_id=1, source_target_pairs={{1,2},{3,4},{5,6},{7,8},{9,10},{11,12},{13,14},{2,1},{4,3},{6,5},{... | collective-permute-start | bytes 786440 | tf_op jit(solution)/shard_map/ppermute | solution.py:66
  29.6 15.5 %collective-permute-start.7 = (f32[128,512]{1,0:T(8,128)S(1)}, f32[128,512]{1,0:T(8,128)S(1)}, u32[]{:S(2)}, u32[]{:S(2)}) collective-permute-start(f32[128,512]{1,0:T(8,128)S(1)} %get-tuple-element.46.own.rest_0_), channel_id=1, source_target_pairs={{0,1},{2,3},{4,5},{6,7},{8,9},{10,11},{12,13},{14,15},{1,0},{3,2},... | collective-permute-start | bytes 786440 | tf_op jit(solution)/shard_map/ppermute | solution.py:66
  38.4 6.8 %copy-start.1 = (f32[8,32,512]{2,1,0:T(8,128)S(1)}, f32[8,32,512]{2,1,0:T(8,128)}, u32[]{:S(2)}) copy-start(f32[8,32,512]{2,1,0:T(8,128)} %rest_1_.1) | copy-start | bytes 1572868
  39.5 7.1 %collective-permute-start.8 = (f32[64,512]{1,0:T(8,128)S(1)}, f32[64,512]{1,0:T(8,128)S(1)}, u32[]{:S(2)}, u32[]{:S(2)}) collective-permute-start(f32[64,512]{1,0:T(8,128)S(1)} %get-tuple-element.44.send1), channel_id=1, source_target_pairs={{16,32},{48,64},{80,96},{112,128},{144,160},{176,192},{208,224},{3... | collective-permute-start | bytes 393224 | tf_op jit(solution)/shard_map/ppermute | solution.py:66
  40.2 8.2 %collective-permute-start.9 = (f32[64,512]{1,0:T(8,128)S(1)}, f32[64,512]{1,0:T(8,128)S(1)}, u32[]{:S(2)}, u32[]{:S(2)}) collective-permute-start(f32[64,512]{1,0:T(8,128)S(1)} %get-tuple-element.45.send0), channel_id=1, source_target_pairs={{0,16},{32,48},{64,80},{96,112},{128,144},{160,176},{192,208},{224... | collective-permute-start | bytes 393224 | tf_op jit(solution)/shard_map/ppermute | solution.py:66
  49.2 12.0 %collective-permute-start.10 = (f32[128,512]{1,0:T(8,128)S(1)}, f32[128,512]{1,0:T(8,128)S(1)}, u32[]{:S(2)}, u32[]{:S(2)}) collective-permute-start(f32[128,512]{1,0:T(8,128)S(1)} %shard_map.48.own), channel_id=1, source_target_pairs={{0,1},{2,3},{4,5},{6,7},{8,9},{10,11},{12,13},{14,15},{1,0},{3,2},... | collective-permute-start | bytes 786440 | tf_op jit(solution)/shard_map/ppermute | solution.py:66
  50.5 19.6 %collective-permute-start.11 = (f32[128,512]{1,0:T(8,128)S(1)}, f32[128,512]{1,0:T(8,128)S(1)}, u32[]{:S(2)}, u32[]{:S(2)}) collective-permute-start(f32[128,512]{1,0:T(8,128)S(1)} %get-tuple-element.50.own), channel_id=1, source_target_pairs={{1,2},{3,4},{5,6},{7,8},{9,10},{11,12},{13,14},{2,1},{4,3},{6,5},{... | collective-permute-start | bytes 786440 | tf_op jit(solution)/shard_map/ppermute | solution.py:66
  52.4 17.7 %collective-permute-start.12 = (f32[128,512]{1,0:T(8,128)S(1)}, f32[128,512]{1,0:T(8,128)S(1)}, u32[]{:S(2)}, u32[]{:S(2)}) collective-permute-start(f32[128,512]{1,0:T(8,128)S(1)} %get-tuple-element.50.own), channel_id=1, source_target_pairs={{0,1},{2,3},{4,5},{6,7},{8,9},{10,11},{12,13},{14,15},{1,0},{3,2},... | collective-permute-start | bytes 786440 | tf_op jit(solution)/shard_map/ppermute | solution.py:66
  62.3 9.9 %collective-permute-start.13 = (f32[64,512]{1,0:T(8,128)S(1)}, f32[64,512]{1,0:T(8,128)S(1)}, u32[]{:S(2)}, u32[]{:S(2)}) collective-permute-start(f32[64,512]{1,0:T(8,128)S(1)} %get-tuple-element.48.send1), channel_id=1, source_target_pairs={{16,32},{48,64},{80,96},{112,128},{144,160},{176,192},{208,224},{3... | collective-permute-start | bytes 393224 | tf_op jit(solution)/shard_map/ppermute | solution.py:66
  63.0 10.0 %collective-permute-start.14 = (f32[64,512]{1,0:T(8,128)S(1)}, f32[64,512]{1,0:T(8,128)S(1)}, u32[]{:S(2)}, u32[]{:S(2)}) collective-permute-start(f32[64,512]{1,0:T(8,128)S(1)} %get-tuple-element.49.send0), channel_id=1, source_target_pairs={{0,16},{32,48},{64,80},{96,112},{128,144},{160,176},{192,208},{224... | collective-permute-start | bytes 393224 | tf_op jit(solution)/shard_map/ppermute | solution.py:66
  74.3 12.5 %collective-permute-start.15 = (f32[128,512]{1,0:T(8,128)S(1)}, f32[128,512]{1,0:T(8,128)S(1)}, u32[]{:S(2)}, u32[]{:S(2)}) collective-permute-start(f32[128,512]{1,0:T(8,128)S(1)} %shard_map.51.own.rest_0_), channel_id=1, source_target_pairs={{0,1},{2,3},{4,5},{6,7},{8,9},{10,11},{12,13},{14,15},{1,0},{3,2},... | collective-permute-start | bytes 786440 | tf_op jit(solution)/shard_map/ppermute | solution.py:66
  76.0 20.4 %collective-permute-start.16 = (f32[128,512]{1,0:T(8,128)S(1)}, f32[128,512]{1,0:T(8,128)S(1)}, u32[]{:S(2)}, u32[]{:S(2)}) collective-permute-start(f32[128,512]{1,0:T(8,128)S(1)} %get-tuple-element.54.own.rest_0_), channel_id=1, source_target_pairs={{1,2},{3,4},{5,6},{7,8},{9,10},{11,12},{13,14},{2,1},{4,3},{6,5},{... | collective-permute-start | bytes 786440 | tf_op jit(solution)/shard_map/ppermute | solution.py:66
  77.9 18.5 %collective-permute-start.17 = (f32[128,512]{1,0:T(8,128)S(1)}, f32[128,512]{1,0:T(8,128)S(1)}, u32[]{:S(2)}, u32[]{:S(2)}) collective-permute-start(f32[128,512]{1,0:T(8,128)S(1)} %get-tuple-element.54.own.rest_0_), channel_id=1, source_target_pairs={{0,1},{2,3},{4,5},{6,7},{8,9},{10,11},{12,13},{14,15},{1,0},{3,2},... | collective-permute-start | bytes 786440 | tf_op jit(solution)/shard_map/ppermute | solution.py:66
  87.9 10.0 %collective-permute-start.18 = (f32[64,512]{1,0:T(8,128)S(1)}, f32[64,512]{1,0:T(8,128)S(1)}, u32[]{:S(2)}, u32[]{:S(2)}) collective-permute-start(f32[64,512]{1,0:T(8,128)S(1)} %get-tuple-element.52.send1), channel_id=1, source_target_pairs={{16,32},{48,64},{80,96},{112,128},{144,160},{176,192},{208,224},{3... | collective-permute-start | bytes 393224 | tf_op jit(solution)/shard_map/ppermute | solution.py:66
  88.6 10.7 %collective-permute-start.19 = (f32[64,512]{1,0:T(8,128)S(1)}, f32[64,512]{1,0:T(8,128)S(1)}, u32[]{:S(2)}, u32[]{:S(2)}) collective-permute-start(f32[64,512]{1,0:T(8,128)S(1)} %get-tuple-element.53.send0), channel_id=1, source_target_pairs={{0,16},{32,48},{64,80},{96,112},{128,144},{160,176},{192,208},{224... | collective-permute-start | bytes 393224 | tf_op jit(solution)/shard_map/ppermute | solution.py:66
  100.1 12.5 %collective-permute-start.20 = (f32[128,512]{1,0:T(8,128)S(1)}, f32[128,512]{1,0:T(8,128)S(1)}, u32[]{:S(2)}, u32[]{:S(2)}) collective-permute-start(f32[128,512]{1,0:T(8,128)S(1)} %shard_map.54.own), channel_id=1, source_target_pairs={{0,1},{2,3},{4,5},{6,7},{8,9},{10,11},{12,13},{14,15},{1,0},{3,2},... | collective-permute-start | bytes 786440 | tf_op jit(solution)/shard_map/ppermute | solution.py:66
  101.8 19.5 %collective-permute-start.21 = (f32[128,512]{1,0:T(8,128)S(1)}, f32[128,512]{1,0:T(8,128)S(1)}, u32[]{:S(2)}, u32[]{:S(2)}) collective-permute-start(f32[128,512]{1,0:T(8,128)S(1)} %get-tuple-element.58.own), channel_id=1, source_target_pairs={{1,2},{3,4},{5,6},{7,8},{9,10},{11,12},{13,14},{2,1},{4,3},{6,5},{... | collective-permute-start | bytes 786440 | tf_op jit(solution)/shard_map/ppermute | solution.py:66
  103.7 17.6 %collective-permute-start.22 = (f32[128,512]{1,0:T(8,128)S(1)}, f32[128,512]{1,0:T(8,128)S(1)}, u32[]{:S(2)}, u32[]{:S(2)}) collective-permute-start(f32[128,512]{1,0:T(8,128)S(1)} %get-tuple-element.58.own), channel_id=1, source_target_pairs={{0,1},{2,3},{4,5},{6,7},{8,9},{10,11},{12,13},{14,15},{1,0},{3,2},... | collective-permute-start | bytes 786440 | tf_op jit(solution)/shard_map/ppermute | solution.py:66
  113.7 9.6 %collective-permute-start.23 = (f32[64,512]{1,0:T(8,128)S(1)}, f32[64,512]{1,0:T(8,128)S(1)}, u32[]{:S(2)}, u32[]{:S(2)}) collective-permute-start(f32[64,512]{1,0:T(8,128)S(1)} %get-tuple-element.56.send1), channel_id=1, source_target_pairs={{16,32},{48,64},{80,96},{112,128},{144,160},{176,192},{208,224},{3... | collective-permute-start | bytes 393224 | tf_op jit(solution)/shard_map/ppermute | solution.py:66
  114.4 9.8 %collective-permute-start.24 = (f32[64,512]{1,0:T(8,128)S(1)}, f32[64,512]{1,0:T(8,128)S(1)}, u32[]{:S(2)}, u32[]{:S(2)}) collective-permute-start(f32[64,512]{1,0:T(8,128)S(1)} %get-tuple-element.57.send0), channel_id=1, source_target_pairs={{0,16},{32,48},{64,80},{96,112},{128,144},{160,176},{192,208},{224... | collective-permute-start | bytes 393224 | tf_op jit(solution)/shard_map/ppermute | solution.py:66

commit v3 on v1

v3 whole, which is shorter than its diff:
```python
import functools

import jax
import jax.numpy as jnp
import numpy as np
from jax import lax
from jax.experimental import pallas as pl
from jax.experimental.pallas import tpu as pltpu
from jax.sharding import PartitionSpec as P


HALF = 8
ITERS = 3
NEWTON = 6
LANES = 128


GROUPS = 4


def scale():
    offsets = np.arange(-HALF, HALF + 1)
    return float(np.sum(np.exp(-2.0 * offsets * offsets / (HALF * HALF))))


def weight(gap):
    gap = gap.astype(jnp.float32)
    raw = jnp.exp(-2.0 * gap * gap / (HALF * HALF)) / scale()
    return jnp.where(jnp.abs(gap) <= HALF, raw, 0.0)


def weights(gap):
    return float(np.exp(-2.0 * gap * gap / (HALF * HALF)) / scale())


def inside_mass(cell, whole):
    total = jnp.zeros(cell.shape, jnp.float32)
    for gap in range(-HALF, HALF + 1):
        total += jnp.where((cell + gap >= 0) & (cell + gap < whole), weights(gap), 0.0)
    return total


def split(value):
    high = value.astype(jnp.bfloat16)
    return high, (value - high.astype(jnp.float32)).astype(jnp.bfloat16)


def stacked(value):
    return jnp.concatenate(split(value), axis=0)


def product(left, right, right_low):
    dot = functools.partial(jnp.dot, preferred_element_type=jnp.float32)
    rows = left.shape[0] // 2
    both = dot(left, right)
    return both[:rows] + (both[rows:] + dot(left[:rows], right_low))


def iota(shape, dim):
    return lax.broadcasted_iota(jnp.int32, shape, dim)


def swap(value, axis, first):
    size = lax.axis_size(axis)
    pairs = [(i, i + 1) for i in range(first, size - 1, 2)]
    return lax.ppermute(value, axis, pairs + [(j, i) for i, j in pairs])


def cells(where, at):
    start = jnp.where(where[0] == 1, at, GROUPS - 1 - at) * HALF
    return pl.ds(pl.multiple_of(start, HALF), HALF)


def tables_kernel(where, x_table, first_table, last_table, y_high, y_low):
    sign = jnp.where(where[0] == 1, 1, -1)
    whole = x_table.shape[1]
    rows = first_table.shape[1]
    row, col = iota((whole, whole), 0), iota((whole, whole), 1)
    gap = row % HALF - col % HALF + sign * HALF * (row // rows - col // rows)
    same = row % rows // HALF == col % rows // HALF
    x_table[...] = stacked(jnp.where(same, weight(gap), 0.0))
    row, col = iota((rows, rows), 0), iota((rows, rows), 1)
    for ref, shift in ((first_table, sign * HALF), (last_table, -sign * HALF)):
        ref[...] = stacked(jnp.where(row // HALF == col // HALF, weight(row % HALF - col % HALF + shift), 0.0))
    shape = y_high.shape
    y_high[...], y_low[...] = split(weight(iota(shape, 0) - iota(shape, 1)))


def order_kernel(where, rho_prev, potential, rho_ordered, potential_ordered):
    depth, _, length = rho_prev.shape
    rows = depth * HALF
    for source, ref in ((rho_prev, rho_ordered), (potential, potential_ordered)):
        for at in range(GROUPS):
            ref[at * rows : (at + 1) * rows] = source[:, cells(where, at), :].reshape(rows, length)


def first_kernel(sizes, where, rho_prev, first, rest):
    depth, _, length = rho_prev.shape
    whole_x, whole_z = sizes
    mass_z = inside_mass(where[3] + iota((depth, LANES), 0), whole_z)
    mass_y = inside_mass(iota((1, length), 1), length)
    rows = depth * HALF
    for at in range(GROUPS):
        span = cells(where, at)
        mass_x = inside_mass(where[2] + span.start + iota((HALF, LANES), 0), whole_x)
        ref, base = (rest, (at - 1) * rows) if at else (first, 0)
        for z in range(depth):
            mass = (mass_x[:, :1] * mass_z[z : z + 1, :1]) * mass_y
            start = base + z * HALF
            ref[start : start + HALF] = rho_prev[z, span, :] / mass


def zy(depth, where, own, far, near, y_high, y_low, lined):
    even = where[1]
    length = own.shape[1]
    rows = depth * HALF
    for start in range(0, own.shape[0], rows):
        span = slice(start, start + rows)
        for at in range(0, length, LANES):
            lanes = slice(at, at + LANES)
            far_part, near_part = far[span, lanes], near[span, lanes]
            before = jnp.where(even == 1, far_part, near_part)
            after = jnp.where(even == 1, near_part, far_part)
            line = [part[z * HALF : (z + 1) * HALF] for part in (before, own[span, lanes], after) for z in range(depth)]
            for z in range(depth):
                here = z + depth
                total = weights(0) * line[here]
                for gap in range(1, HALF + 1):
                    total += weights(gap) * (line[here - gap] + line[here + gap])
                to = start + z * HALF
                lined[to : to + HALF, lanes] = total
    return product(stacked(lined[...]), y_high[...], y_low[...])


def zy_first_kernel(depth, where, own, far, near, y_high, y_low, out, lined):
    out[...] = zy(depth, where, own, far, near, y_high, y_low, lined)


def zy_rest_kernel(depth, where, own, far, near, y_high, y_low, inner, last, lined):
    value = zy(depth, where, own, far, near, y_high, y_low, lined)
    rows = last.shape[0]
    inner[...], last[...] = value[:-rows], value[-rows:]


def prox(target):
    current = target
    for _ in range(NEWTON):
        grown = 0.5 * jnp.exp(current)
        current = (grown * (current - 1.0) + target) / (1.0 + grown)
    return jnp.exp(current)


def finish(kind, value, span, whole, scaling):
    if kind == "dual":
        return whole[span] / value
    inner = value if scaling is None else scaling[...] * value
    rho = prox(jnp.log(inner) - whole[span])
    return rho if kind == "last" else rho / value


def lane_sums(value):
    rows = jnp.sum(value, axis=0, keepdims=True)
    return sum(rows[:, i : i + LANES] for i in range(0, rows.shape[1], LANES))


def rest_kernel(kind, started, first, inner, last, recv0, x_table, last_table, whole, *rest):
    scaling = None
    if started:
        scaling, *rest = rest
    if kind == "last":
        rho_prev, out, part, sums, high, low = rest
    else:
        out, part, high, low = rest
    rows = first.shape[0]
    at = 0
    for ref in (first, inner, last):
        span = slice(at, at + ref.shape[0])
        high[span], low[span] = split(ref[...])
        at = span.stop
    along_x = product(x_table[...], high[...], low[...])
    part[...] = along_x[:rows]
    final = along_x[3 * rows :] + product(last_table[...], *split(recv0[...]))
    value = jnp.concatenate([along_x[rows : 3 * rows], final], axis=0)
    result = finish(kind, value, slice(rows, 4 * rows), whole, scaling)
    out[...] = result
    if kind == "last":
        sums[:, :LANES] = lane_sums(rho_prev[...])
        sums[:, LANES:] = lane_sums(result)


def first_group_kernel(kind, started, part, recv1, first_table, whole, *rest):
    scaling = None
    if started:
        scaling, *rest = rest
    if kind == "last":
        sums_rest, out, sums = rest
    else:
        (out,) = rest
    value = part[...] + product(first_table[...], *split(recv1[...]))
    result = finish(kind, value, slice(0, value.shape[0]), whole, scaling)
    out[...] = result
    if kind == "last":
        sums[...] = sums_rest[...]
        sums[:, LANES:] += lane_sums(result)


def scale_kernel(where, first, rest, sums, out, ratio):
    totals = jnp.sum(sums[...], axis=0, keepdims=True)
    mass_prev, mass_new = jnp.sum(totals[:, :LANES]), jnp.sum(totals[:, LANES:])
    ones = jnp.ones((1, LANES), jnp.float32)
    prev, new = mass_prev * ones, mass_new * ones
    ratio[...] = new / prev
    factor = (prev / new)[:, :1]
    depth, _, length = out.shape
    rows = first.shape[0]
    for at in range(GROUPS):
        value = rest[(at - 1) * rows : at * rows] if at else first[...]
        out[:, cells(where, at), :] = (value * factor).reshape(depth, HALF, length)


def call(kernel, inputs, shapes, scratch=(), scalars=1, dtype=jnp.float32):
    specs = [pl.BlockSpec(memory_space=pltpu.SMEM)] * scalars
    specs += [pl.BlockSpec(memory_space=pltpu.VMEM)] * (len(inputs) - scalars)
    return pl.pallas_call(
        kernel,
        out_shape=[jax.ShapeDtypeStruct(shape, dtype) for shape in shapes],
        in_specs=specs,
        out_specs=[pl.BlockSpec(memory_space=pltpu.VMEM)] * len(shapes),
        scratch_shapes=scratch,
        compiler_params=pltpu.CompilerParams(vmem_limit_bytes=20 << 20),
    )(*inputs)


def step(rho_prev, potential):
    depth, width, length = rho_prev.shape
    at_x, at_z = lax.axis_index("gx"), lax.axis_index("gz")
    size_x, size_z = lax.axis_size("gx"), lax.axis_size("gz")
    where = jnp.stack([1 - at_x % 2, 1 - at_z % 2, at_x * width, at_z * depth]).astype(jnp.int32)
    rows = depth * HALF
    one, three, whole = (rows, length), (3 * rows, length), (4 * rows, length)
    halves = [pltpu.VMEM(whole, jnp.bfloat16)] * 2

    start = functools.partial(first_kernel, (width * size_x, depth * size_z))
    first, rest = call(start, (where, rho_prev), [one, three])
    table_shapes = [(8 * rows, 4 * rows), (2 * rows, rows), (2 * rows, rows), (length, length), (length, length)]
    x_table, first_table, last_table, *y_table = call(tables_kernel, (where,), table_shapes, dtype=jnp.bfloat16)
    rho_ordered, potential_ordered = call(order_kernel, (where, rho_prev, potential), [whole, whole])

    def heat_step(kind, first, rest, whole, scaling):
        started, last = scaling is not None, kind == "last"
        far = swap(first, "gz", 1)
        near = swap(first, "gz", 0)
        far_rest = swap(rest, "gz", 1)
        near_rest = swap(rest, "gz", 0)
        inner, send0 = call(
            functools.partial(zy_rest_kernel, depth),
            (where, rest, far_rest, near_rest, *y_table),
            [(2 * rows, length), one],
            [pltpu.VMEM(three, jnp.float32)],
        )
        recv0 = swap(send0, "gx", 0)
        (send1,) = call(
            functools.partial(zy_first_kernel, depth),
            (where, first, far, near, *y_table),
            [one],
            [pltpu.VMEM(one, jnp.float32)],
        )
        recv1 = swap(send1, "gx", 1)
        more = ((scaling[1],) if started else ()) + ((rho_ordered,) if last else ())
        total = [(1, 2 * LANES)] if last else []
        new_rest, part, *sums = call(
            functools.partial(rest_kernel, kind, started),
            (send1, inner, send0, recv0, x_table, last_table, whole, *more),
            [three, one] + total,
            halves,
            0,
        )
        more = ((scaling[0],) if started else ()) + tuple(sums)
        new_first, *sums = call(
            functools.partial(first_group_kernel, kind, started),
            (part, recv1, first_table, whole, *more),
            [one] + total,
            scalars=0,
        )
        return new_first, new_rest, *sums

    scaling = None
    for sweep in range(ITERS):
        if sweep:
            first, rest = heat_step("dual", first, rest, rho_ordered, None)
        if sweep < ITERS - 1:
            first, rest = scaling = heat_step("scaling", first, rest, potential_ordered, scaling)
        else:
            first, rest, sums = heat_step("last", first, rest, potential_ordered, scaling)
    everyone = size_x * size_z
    sums = jnp.broadcast_to(sums[None], (everyone, 1, 2 * LANES))
    sums = lax.all_to_all(sums, ("gx", "gz"), 0, 0, tiled=True).reshape(everyone, 2 * LANES)
    rho_next, ratio = call(scale_kernel, (where, first, rest, sums), [(depth, width, length), (1, LANES)])
    return rho_next, ratio[0, :1]


def solution(mesh):
    return jax.shard_map(
        step,
        mesh=mesh,
        in_specs=(P("gz", "gx", None), P("gz", "gx", None)),
        out_specs=(P("gz", "gx", None), P()),
        check_vma=False,
    )
```

time: 154 us -> 177 us (1.15)
  starting transfers between devices: 79.3 us -> 89.3 us
  waiting for transfers between devices: 6.57 us -> 15.9 us
  blocking collectives: 42.8 us -> 47.2 us
    ppermute x30, starting transfers between devices: 79.3 us -> 89.3 us  [swap(): return lax.ppermute(value, axis, pairs + [(j, i) for i, j in pairs])]
    ppermute x30, waiting for transfers between devices: 6.57 us -> 15.9 us  [swap(): return lax.ppermute(value, axis, pairs + [(j, i) for i, j in pairs])]
    all_to_all x1, blocking collectives: 42.8 us -> 47.2 us  [step(): lax.all_to_all(sums, ('gx', 'gz'), 0, 0, tiled=True)]
    pallas_call x18 -> x24, Pallas kernels: 22.4 us -> 21.6 us  [call(): pl.pallas_call(kernel, out_shape=[jax.ShapeDtypeStruct(shape, dtype) for...]
  transfers between devices with their start and end apart: 30 -> 30, of which waited for: 5 -> 9; matrix products, arithmetic and copies ran while one was open for 0% -> 0% of each run, Pallas kernels for 10% -> 9%
where the time goes in v3:
time: 177 us; the launch traced here: 176 us
  starting transfers between devices  89.3 us (50%)
  blocking collectives  47.2 us (27%)
  Pallas kernels  21.6 us (12%)
  waiting for transfers between devices  15.9 us (9%)
    ppermute x30, starting transfers between devices, swap(): return lax.ppermute(value, axis, pairs + [(j, i) for i, j in pairs])  89.3 us
    all_to_all x1, blocking collectives, step(): lax.all_to_all(sums, ('gx', 'gz'), 0, 0, tiled=True)  47.2 us
    pallas_call x24, Pallas kernels, call(): pl.pallas_call(kernel, out_shape=[jax.ShapeDtypeStruct(shape, dtype) for...  21.6 us
    ppermute x30, waiting for transfers between devices, swap(): return lax.ppermute(value, axis, pairs + [(j, i) for i, j in pairs])  15.9 us
  transfers between devices with their start and end apart: 30, of which 9 were waited for; matrix products, arithmetic and copies ran while one was open for 0% of the time, Pallas kernels for 9%

profile of v3, /device:TPU:1, one launch (start us, length us, event | category | flops | bytes accessed | tf_op | source)
XLA Modules:
  0.0 176.4 jit_solution(17648347694017989374)
XLA Ops:
  0.7 1.0 copy-done
  1.8 0.7 shard_map.41
  2.5 4.5 %collective-permute-start.2 = (f32[192,512]{1,0:T(8,128)S(1)}, f32[192,512]{1,0:T(8,128)S(1)}, u32[]{:S(2)}, u32[]{:S(2)}) collective-permute-start(f32[192,512]{1,0:T(8,128)S(1)} %get-tuple-element.39.own), channel_id=1, source_target_pairs={{1,2},{3,4},{5,6},{7,8},{9,10},{11,12},{13,14},{2,1},{4,3},{6,5},{... | collective-permute-start | bytes 1179656 | tf_op jit(solution)/shard_map/ppermute | solution.py:66
  7.1 3.5 %collective-permute-start = (f32[64,512]{1,0:T(8,128)S(1)}, f32[64,512]{1,0:T(8,128)S(1)}, u32[]{:S(2)}, u32[]{:S(2)}) collective-permute-start(f32[64,512]{1,0:T(8,128)S(1)} %get-tuple-element.36.own), channel_id=1, source_target_pairs={{1,2},{3,4},{5,6},{7,8},{9,10},{11,12},{13,14},{2,1},{4,3},{6,5},{... | collective-permute-start | bytes 393224 | tf_op jit(solution)/shard_map/ppermute | solution.py:66
  10.7 1.3 shard_map.42
  12.4 1.2 shard_map.44
  13.7 1.4 collective-permute-start.4
  15.1 0.6 shard_map.45
  15.7 0.9 shard_map.43.first
  16.6 2.1 %collective-permute-done.4.recv0 = f32[64,512]{1,0:T(8,128)S(1)} collective-permute-done((f32[64,512]{1,0:T(8,128)S(1)}, f32[64,512]{1,0:T(8,128)S(1)}, u32[]{:S(2)}, u32[]{:S(2)}) %collective-permute-start.4) | collective-permute-done | bytes 131104 | tf_op jit(solution)/shard_map/ppermute | solution.py:66
  18.7 1.3 shard_map.46
  20.0 4.3 %collective-permute-start.8 = (f32[192,512]{1,0:T(8,128)S(1)}, f32[192,512]{1,0:T(8,128)S(1)}, u32[]{:S(2)}, u32[]{:S(2)}) collective-permute-start(f32[192,512]{1,0:T(8,128)S(1)} %get-tuple-element.47.own.rest_0_), channel_id=1, source_target_pairs={{1,2},{3,4},{5,6},{7,8},{9,10},{11,12},{13,14},{2,1},{4,3},{6,5},{... | collective-permute-start | bytes 1179656 | tf_op jit(solution)/shard_map/ppermute | solution.py:66
  24.3 0.7 collective-permute-start.5
  25.5 3.5 %collective-permute-start.6 = (f32[64,512]{1,0:T(8,128)S(1)}, f32[64,512]{1,0:T(8,128)S(1)}, u32[]{:S(2)}, u32[]{:S(2)}) collective-permute-start(f32[64,512]{1,0:T(8,128)S(1)} %shard_map.47.own.rest_0_), channel_id=1, source_target_pairs={{1,2},{3,4},{5,6},{7,8},{9,10},{11,12},{13,14},{2,1},{4,3},{6,5},{... | collective-permute-start | bytes 393224 | tf_op jit(solution)/shard_map/ppermute | solution.py:66
  29.1 0.6 collective-permute-done.8.far
  29.7 1.3 shard_map.49
  31.0 7.5 %collective-permute-start.10 = (f32[64,512]{1,0:T(8,128)S(1)}, f32[64,512]{1,0:T(8,128)S(1)}, u32[]{:S(2)}, u32[]{:S(2)}) collective-permute-start(f32[64,512]{1,0:T(8,128)S(1)} %get-tuple-element.49.last), channel_id=1, source_target_pairs={{0,16},{32,48},{64,80},{96,112},{128,144},{160,176},{192,208},{224... | collective-permute-start | bytes 393224 | tf_op jit(solution)/shard_map/ppermute | solution.py:66
  38.4 0.9 shard_map.48.first
  39.3 2.5 %collective-permute-done.10.recv0 = f32[64,512]{1,0:T(8,128)S(1)} collective-permute-done((f32[64,512]{1,0:T(8,128)S(1)}, f32[64,512]{1,0:T(8,128)S(1)}, u32[]{:S(2)}, u32[]{:S(2)}) %collective-permute-start.10) | collective-permute-done | bytes 131104 | tf_op jit(solution)/shard_map/ppermute | solution.py:66
  42.2 3.6 %collective-permute-start.14 = (f32[192,512]{1,0:T(8,128)S(1)}, f32[192,512]{1,0:T(8,128)S(1)}, u32[]{:S(2)}, u32[]{:S(2)}) collective-permute-start(f32[192,512]{1,0:T(8,128)S(1)} %get-tuple-element.52.own), channel_id=1, source_target_pairs={{1,2},{3,4},{5,6},{7,8},{9,10},{11,12},{13,14},{2,1},{4,3},{6,5},{... | collective-permute-start | bytes 1179656 | tf_op jit(solution)/shard_map/ppermute | solution.py:66
  46.0 0.7 collective-permute-start.11
  46.9 5.5 %collective-permute-start.12 = (f32[64,512]{1,0:T(8,128)S(1)}, f32[64,512]{1,0:T(8,128)S(1)}, u32[]{:S(2)}, u32[]{:S(2)}) collective-permute-start(f32[64,512]{1,0:T(8,128)S(1)} %shard_map.51.own), channel_id=1, source_target_pairs={{1,2},{3,4},{5,6},{7,8},{9,10},{11,12},{13,14},{2,1},{4,3},{6,5},{... | collective-permute-start | bytes 393224 | tf_op jit(solution)/shard_map/ppermute | solution.py:66
  52.5 1.3 shard_map.53
  53.8 11.6 %collective-permute-start.16 = (f32[64,512]{1,0:T(8,128)S(1)}, f32[64,512]{1,0:T(8,128)S(1)}, u32[]{:S(2)}, u32[]{:S(2)}) collective-permute-start(f32[64,512]{1,0:T(8,128)S(1)} %get-tuple-element.54.last), channel_id=1, source_target_pairs={{0,16},{32,48},{64,80},{96,112},{128,144},{160,176},{192,208},{224... | collective-permute-start | bytes 393224 | tf_op jit(solution)/shard_map/ppermute | solution.py:66
  65.4 0.9 shard_map.52.first
  66.3 2.5 %collective-permute-done.16.recv0 = f32[64,512]{1,0:T(8,128)S(1)} collective-permute-done((f32[64,512]{1,0:T(8,128)S(1)}, f32[64,512]{1,0:T(8,128)S(1)}, u32[]{:S(2)}, u32[]{:S(2)}) %collective-permute-start.16) | collective-permute-done | bytes 131104 | tf_op jit(solution)/shard_map/ppermute | solution.py:66
  68.8 1.2 shard_map.54
  70.1 6.5 %collective-permute-start.20 = (f32[192,512]{1,0:T(8,128)S(1)}, f32[192,512]{1,0:T(8,128)S(1)}, u32[]{:S(2)}, u32[]{:S(2)}) collective-permute-start(f32[192,512]{1,0:T(8,128)S(1)} %get-tuple-element.56.own.rest_0_), channel_id=1, source_target_pairs={{1,2},{3,4},{5,6},{7,8},{9,10},{11,12},{13,14},{2,1},{4,3},{6,5},{... | collective-permute-start | bytes 1179656 | tf_op jit(solution)/shard_map/ppermute | solution.py:66
  76.7 0.7 collective-permute-start.17
  77.9 2.4 %collective-permute-start.18 = (f32[64,512]{1,0:T(8,128)S(1)}, f32[64,512]{1,0:T(8,128)S(1)}, u32[]{:S(2)}, u32[]{:S(2)}) collective-permute-start(f32[64,512]{1,0:T(8,128)S(1)} %shard_map.55.own.rest_0_), channel_id=1, source_target_pairs={{1,2},{3,4},{5,6},{7,8},{9,10},{11,12},{13,14},{2,1},{4,3},{6,5},{... | collective-permute-start | bytes 393224 | tf_op jit(solution)/shard_map/ppermute | solution.py:66
  80.4 1.6 collective-permute-done.20.far
  82.0 1.3 shard_map.57
  83.3 10.9 %collective-permute-start.22 = (f32[64,512]{1,0:T(8,128)S(1)}, f32[64,512]{1,0:T(8,128)S(1)}, u32[]{:S(2)}, u32[]{:S(2)}) collective-permute-start(f32[64,512]{1,0:T(8,128)S(1)} %get-tuple-element.58.last), channel_id=1, source_target_pairs={{0,16},{32,48},{64,80},{96,112},{128,144},{160,176},{192,208},{224... | collective-permute-start | bytes 393224 | tf_op jit(solution)/shard_map/ppermute | solution.py:66
  94.2 0.9 shard_map.56.first
  95.1 2.5 %collective-permute-done.22.recv0 = f32[64,512]{1,0:T(8,128)S(1)} collective-permute-done((f32[64,512]{1,0:T(8,128)S(1)}, f32[64,512]{1,0:T(8,128)S(1)}, u32[]{:S(2)}, u32[]{:S(2)}) %collective-permute-start.22) | collective-permute-done | bytes 131104 | tf_op jit(solution)/shard_map/ppermute | solution.py:66
  98.0 7.0 %collective-permute-start.26 = (f32[192,512]{1,0:T(8,128)S(1)}, f32[192,512]{1,0:T(8,128)S(1)}, u32[]{:S(2)}, u32[]{:S(2)}) collective-permute-start(f32[192,512]{1,0:T(8,128)S(1)} %get-tuple-element.60.own), channel_id=1, source_target_pairs={{1,2},{3,4},{5,6},{7,8},{9,10},{11,12},{13,14},{2,1},{4,3},{6,5},{... | collective-permute-start | bytes 1179656 | tf_op jit(solution)/shard_map/ppermute | solution.py:66
  105.1 0.7 collective-permute-start.23
  106.0 2.4 %collective-permute-start.24 = (f32[64,512]{1,0:T(8,128)S(1)}, f32[64,512]{1,0:T(8,128)S(1)}, u32[]{:S(2)}, u32[]{:S(2)}) collective-permute-start(f32[64,512]{1,0:T(8,128)S(1)} %shard_map.59.own), channel_id=1, source_target_pairs={{1,2},{3,4},{5,6},{7,8},{9,10},{11,12},{13,14},{2,1},{4,3},{6,5},{... | collective-permute-start | bytes 393224 | tf_op jit(solution)/shard_map/ppermute | solution.py:66
  108.5 2.0 %collective-permute-done.26.far = f32[192,512]{1,0:T(8,128)S(1)} collective-permute-done((f32[192,512]{1,0:T(8,128)S(1)}, f32[192,512]{1,0:T(8,128)S(1)}, u32[]{:S(2)}, u32[]{:S(2)}) %collective-permute-start.26) | collective-permute-done | bytes 393248 | tf_op jit(solution)/shard_map/ppermute | solution.py:66
  110.4 1.3 shard_map.61
  111.7 10.6 %collective-permute-start.28 = (f32[64,512]{1,0:T(8,128)S(1)}, f32[64,512]{1,0:T(8,128)S(1)}, u32[]{:S(2)}, u32[]{:S(2)}) collective-permute-start(f32[64,512]{1,0:T(8,128)S(1)} %get-tuple-element.62.last), channel_id=1, source_target_pairs={{0,16},{32,48},{64,80},{96,112},{128,144},{160,176},{192,208},{224... | collective-permute-start | bytes 393224 | tf_op jit(solution)/shard_map/ppermute | solution.py:66
  122.3 0.9 shard_map.60.first
  123.3 0.7 collective-permute-start.29
  123.9 1.8 %collective-permute-done.28.recv0 = f32[64,512]{1,0:T(8,128)S(1)} collective-permute-done((f32[64,512]{1,0:T(8,128)S(1)}, f32[64,512]{1,0:T(8,128)S(1)}, u32[]{:S(2)}, u32[]{:S(2)}) %collective-permute-start.28) | collective-permute-done | bytes 131104 | tf_op jit(solution)/shard_map/ppermute | solution.py:66
  125.7 1.2 shard_map.62
  127.0 0.5 shard_map.63
  127.6 47.2 %all_to_all.5 = f32[256,1,256]{2,1,0:T(1,128)S(1)} all-to-all(f32[256,1,256]{2,1,0:T(1,128)S(1)} %broadcast_in_dim.9), channel_id=1, replica_groups=mesh['gx'=16,'gz'=16] {'gx','gz'}, dimensions={0} | all-to-all | bytes 524288 | tf_op jit(solution)/shard_map/all_to_all | solution.py:297
  174.9 1.5 shard_map.64
  (46 shorter events, 3.9 us)
Async XLA Ops:
  0.7 1.0 copy-start
  2.5 10.0 %collective-permute-start.2 = (f32[192,512]{1,0:T(8,128)S(1)}, f32[192,512]{1,0:T(8,128)S(1)}, u32[]{:S(2)}, u32[]{:S(2)}) collective-permute-start(f32[192,512]{1,0:T(8,128)S(1)} %get-tuple-element.39.own), channel_id=1, source_target_pairs={{1,2},{3,4},{5,6},{7,8},{9,10},{11,12},{13,14},{2,1},{4,3},{6,5},{... | collective-permute-start | bytes 1179656 | tf_op jit(solution)/shard_map/ppermute | solution.py:66
  7.0 5.4 %collective-permute-start.3 = (f32[192,512]{1,0:T(8,128)S(1)}, f32[192,512]{1,0:T(8,128)S(1)}, u32[]{:S(2)}, u32[]{:S(2)}) collective-permute-start(f32[192,512]{1,0:T(8,128)S(1)} %get-tuple-element.39.own), channel_id=1, source_target_pairs={{0,1},{2,3},{4,5},{6,7},{8,9},{10,11},{12,13},{14,15},{1,0},{3,2},... | collective-permute-start | bytes 1179656 | tf_op jit(solution)/shard_map/ppermute | solution.py:66
  7.1 8.6 %collective-permute-start = (f32[64,512]{1,0:T(8,128)S(1)}, f32[64,512]{1,0:T(8,128)S(1)}, u32[]{:S(2)}, u32[]{:S(2)}) collective-permute-start(f32[64,512]{1,0:T(8,128)S(1)} %get-tuple-element.36.own), channel_id=1, source_target_pairs={{1,2},{3,4},{5,6},{7,8},{9,10},{11,12},{13,14},{2,1},{4,3},{6,5},{... | collective-permute-start | bytes 393224 | tf_op jit(solution)/shard_map/ppermute | solution.py:66
  10.6 5.1 %collective-permute-start.1 = (f32[64,512]{1,0:T(8,128)S(1)}, f32[64,512]{1,0:T(8,128)S(1)}, u32[]{:S(2)}, u32[]{:S(2)}) collective-permute-start(f32[64,512]{1,0:T(8,128)S(1)} %get-tuple-element.36.own), channel_id=1, source_target_pairs={{0,1},{2,3},{4,5},{6,7},{8,9},{10,11},{12,13},{14,15},{1,0},{3,2},... | collective-permute-start | bytes 393224 | tf_op jit(solution)/shard_map/ppermute | solution.py:66
  12.4 2.6 %copy-start.1 = (f32[8,32,512]{2,1,0:T(8,128)S(1)}, f32[8,32,512]{2,1,0:T(8,128)}, u32[]{:S(2)}) copy-start(f32[8,32,512]{2,1,0:T(8,128)} %rho_prev.3) | copy-start | bytes 1572868
  12.4 2.6 %copy-start.2 = (f32[8,32,512]{2,1,0:T(8,128)S(1)}, f32[8,32,512]{2,1,0:T(8,128)}, u32[]{:S(2)}) copy-start(f32[8,32,512]{2,1,0:T(8,128)} %potential.1) | copy-start | bytes 1572868
  13.7 5.0 %collective-permute-start.4 = (f32[64,512]{1,0:T(8,128)S(1)}, f32[64,512]{1,0:T(8,128)S(1)}, u32[]{:S(2)}, u32[]{:S(2)}) collective-permute-start(f32[64,512]{1,0:T(8,128)S(1)} %get-tuple-element.41.last), channel_id=1, source_target_pairs={{0,16},{32,48},{64,80},{96,112},{128,144},{160,176},{192,208},{224... | collective-permute-start | bytes 393224 | tf_op jit(solution)/shard_map/ppermute | solution.py:66
  20.0 9.7 %collective-permute-start.8 = (f32[192,512]{1,0:T(8,128)S(1)}, f32[192,512]{1,0:T(8,128)S(1)}, u32[]{:S(2)}, u32[]{:S(2)}) collective-permute-start(f32[192,512]{1,0:T(8,128)S(1)} %get-tuple-element.47.own.rest_0_), channel_id=1, source_target_pairs={{1,2},{3,4},{5,6},{7,8},{9,10},{11,12},{13,14},{2,1},{4,3},{6,5},{... | collective-permute-start | bytes 1179656 | tf_op jit(solution)/shard_map/ppermute | solution.py:66
  24.2 5.4 %collective-permute-start.9 = (f32[192,512]{1,0:T(8,128)S(1)}, f32[192,512]{1,0:T(8,128)S(1)}, u32[]{:S(2)}, u32[]{:S(2)}) collective-permute-start(f32[192,512]{1,0:T(8,128)S(1)} %get-tuple-element.47.own.rest_0_), channel_id=1, source_target_pairs={{0,1},{2,3},{4,5},{6,7},{8,9},{10,11},{12,13},{14,15},{1,0},{3,2},... | collective-permute-start | bytes 1179656 | tf_op jit(solution)/shard_map/ppermute | solution.py:66
  24.3 0.7 collective-permute-start.5
  25.5 12.9 %collective-permute-start.6 = (f32[64,512]{1,0:T(8,128)S(1)}, f32[64,512]{1,0:T(8,128)S(1)}, u32[]{:S(2)}, u32[]{:S(2)}) collective-permute-start(f32[64,512]{1,0:T(8,128)S(1)} %shard_map.47.own.rest_0_), channel_id=1, source_target_pairs={{1,2},{3,4},{5,6},{7,8},{9,10},{11,12},{13,14},{2,1},{4,3},{6,5},{... | collective-permute-start | bytes 393224 | tf_op jit(solution)/shard_map/ppermute | solution.py:66
  29.0 9.4 %collective-permute-start.7 = (f32[64,512]{1,0:T(8,128)S(1)}, f32[64,512]{1,0:T(8,128)S(1)}, u32[]{:S(2)}, u32[]{:S(2)}) collective-permute-start(f32[64,512]{1,0:T(8,128)S(1)} %shard_map.47.own.rest_0_), channel_id=1, source_target_pairs={{0,1},{2,3},{4,5},{6,7},{8,9},{10,11},{12,13},{14,15},{1,0},{3,2},... | collective-permute-start | bytes 393224 | tf_op jit(solution)/shard_map/ppermute | solution.py:66
  31.0 10.8 %collective-permute-start.10 = (f32[64,512]{1,0:T(8,128)S(1)}, f32[64,512]{1,0:T(8,128)S(1)}, u32[]{:S(2)}, u32[]{:S(2)}) collective-permute-start(f32[64,512]{1,0:T(8,128)S(1)} %get-tuple-element.49.last), channel_id=1, source_target_pairs={{0,16},{32,48},{64,80},{96,112},{128,144},{160,176},{192,208},{224... | collective-permute-start | bytes 393224 | tf_op jit(solution)/shard_map/ppermute | solution.py:66
  42.2 10.3 %collective-permute-start.14 = (f32[192,512]{1,0:T(8,128)S(1)}, f32[192,512]{1,0:T(8,128)S(1)}, u32[]{:S(2)}, u32[]{:S(2)}) collective-permute-start(f32[192,512]{1,0:T(8,128)S(1)} %get-tuple-element.52.own), channel_id=1, source_target_pairs={{1,2},{3,4},{5,6},{7,8},{9,10},{11,12},{13,14},{2,1},{4,3},{6,5},{... | collective-permute-start | bytes 1179656 | tf_op jit(solution)/shard_map/ppermute | solution.py:66
  45.9 6.6 %collective-permute-start.15 = (f32[192,512]{1,0:T(8,128)S(1)}, f32[192,512]{1,0:T(8,128)S(1)}, u32[]{:S(2)}, u32[]{:S(2)}) collective-permute-start(f32[192,512]{1,0:T(8,128)S(1)} %get-tuple-element.52.own), channel_id=1, source_target_pairs={{0,1},{2,3},{4,5},{6,7},{8,9},{10,11},{12,13},{14,15},{1,0},{3,2},... | collective-permute-start | bytes 1179656 | tf_op jit(solution)/shard_map/ppermute | solution.py:66
  46.0 0.7 collective-permute-start.11
  46.9 18.5 %collective-permute-start.12 = (f32[64,512]{1,0:T(8,128)S(1)}, f32[64,512]{1,0:T(8,128)S(1)}, u32[]{:S(2)}, u32[]{:S(2)}) collective-permute-start(f32[64,512]{1,0:T(8,128)S(1)} %shard_map.51.own), channel_id=1, source_target_pairs={{1,2},{3,4},{5,6},{7,8},{9,10},{11,12},{13,14},{2,1},{4,3},{6,5},{... | collective-permute-start | bytes 393224 | tf_op jit(solution)/shard_map/ppermute | solution.py:66
  52.4 13.0 %collective-permute-start.13 = (f32[64,512]{1,0:T(8,128)S(1)}, f32[64,512]{1,0:T(8,128)S(1)}, u32[]{:S(2)}, u32[]{:S(2)}) collective-permute-start(f32[64,512]{1,0:T(8,128)S(1)} %shard_map.51.own), channel_id=1, source_target_pairs={{0,1},{2,3},{4,5},{6,7},{8,9},{10,11},{12,13},{14,15},{1,0},{3,2},... | collective-permute-start | bytes 393224 | tf_op jit(solution)/shard_map/ppermute | solution.py:66
  53.8 15.0 %collective-permute-start.16 = (f32[64,512]{1,0:T(8,128)S(1)}, f32[64,512]{1,0:T(8,128)S(1)}, u32[]{:S(2)}, u32[]{:S(2)}) collective-permute-start(f32[64,512]{1,0:T(8,128)S(1)} %get-tuple-element.54.last), channel_id=1, source_target_pairs={{0,16},{32,48},{64,80},{96,112},{128,144},{160,176},{192,208},{224... | collective-permute-start | bytes 393224 | tf_op jit(solution)/shard_map/ppermute | solution.py:66
  70.1 12.0 %collective-permute-start.20 = (f32[192,512]{1,0:T(8,128)S(1)}, f32[192,512]{1,0:T(8,128)S(1)}, u32[]{:S(2)}, u32[]{:S(2)}) collective-permute-start(f32[192,512]{1,0:T(8,128)S(1)} %get-tuple-element.56.own.rest_0_), channel_id=1, source_target_pairs={{1,2},{3,4},{5,6},{7,8},{9,10},{11,12},{13,14},{2,1},{4,3},{6,5},{... | collective-permute-start | bytes 1179656 | tf_op jit(solution)/shard_map/ppermute | solution.py:66
  76.6 5.4 %collective-permute-start.21 = (f32[192,512]{1,0:T(8,128)S(1)}, f32[192,512]{1,0:T(8,128)S(1)}, u32[]{:S(2)}, u32[]{:S(2)}) collective-permute-start(f32[192,512]{1,0:T(8,128)S(1)} %get-tuple-element.56.own.rest_0_), channel_id=1, source_target_pairs={{0,1},{2,3},{4,5},{6,7},{8,9},{10,11},{12,13},{14,15},{1,0},{3,2},... | collective-permute-start | bytes 1179656 | tf_op jit(solution)/shard_map/ppermute | solution.py:66
  76.7 0.7 collective-permute-start.17
  77.9 16.3 %collective-permute-start.18 = (f32[64,512]{1,0:T(8,128)S(1)}, f32[64,512]{1,0:T(8,128)S(1)}, u32[]{:S(2)}, u32[]{:S(2)}) collective-permute-start(f32[64,512]{1,0:T(8,128)S(1)} %shard_map.55.own.rest_0_), channel_id=1, source_target_pairs={{1,2},{3,4},{5,6},{7,8},{9,10},{11,12},{13,14},{2,1},{4,3},{6,5},{... | collective-permute-start | bytes 393224 | tf_op jit(solution)/shard_map/ppermute | solution.py:66
  80.3 13.9 %collective-permute-start.19 = (f32[64,512]{1,0:T(8,128)S(1)}, f32[64,512]{1,0:T(8,128)S(1)}, u32[]{:S(2)}, u32[]{:S(2)}) collective-permute-start(f32[64,512]{1,0:T(8,128)S(1)} %shard_map.55.own.rest_0_), channel_id=1, source_target_pairs={{0,1},{2,3},{4,5},{6,7},{8,9},{10,11},{12,13},{14,15},{1,0},{3,2},... | collective-permute-start | bytes 393224 | tf_op jit(solution)/shard_map/ppermute | solution.py:66
  83.3 14.3 %collective-permute-start.22 = (f32[64,512]{1,0:T(8,128)S(1)}, f32[64,512]{1,0:T(8,128)S(1)}, u32[]{:S(2)}, u32[]{:S(2)}) collective-permute-start(f32[64,512]{1,0:T(8,128)S(1)} %get-tuple-element.58.last), channel_id=1, source_target_pairs={{0,16},{32,48},{64,80},{96,112},{128,144},{160,176},{192,208},{224... | collective-permute-start | bytes 393224 | tf_op jit(solution)/shard_map/ppermute | solution.py:66
  98.0 12.4 %collective-permute-start.26 = (f32[192,512]{1,0:T(8,128)S(1)}, f32[192,512]{1,0:T(8,128)S(1)}, u32[]{:S(2)}, u32[]{:S(2)}) collective-permute-start(f32[192,512]{1,0:T(8,128)S(1)} %get-tuple-element.60.own), channel_id=1, source_target_pairs={{1,2},{3,4},{5,6},{7,8},{9,10},{11,12},{13,14},{2,1},{4,3},{6,5},{... | collective-permute-start | bytes 1179656 | tf_op jit(solution)/shard_map/ppermute | solution.py:66
  105.0 5.4 %collective-permute-start.27 = (f32[192,512]{1,0:T(8,128)S(1)}, f32[192,512]{1,0:T(8,128)S(1)}, u32[]{:S(2)}, u32[]{:S(2)}) collective-permute-start(f32[192,512]{1,0:T(8,128)S(1)} %get-tuple-element.60.own), channel_id=1, source_target_pairs={{0,1},{2,3},{4,5},{6,7},{8,9},{10,11},{12,13},{14,15},{1,0},{3,2},... | collective-permute-start | bytes 1179656 | tf_op jit(solution)/shard_map/ppermute | solution.py:66
  105.1 0.7 collective-permute-start.23
  106.0 16.4 %collective-permute-start.24 = (f32[64,512]{1,0:T(8,128)S(1)}, f32[64,512]{1,0:T(8,128)S(1)}, u32[]{:S(2)}, u32[]{:S(2)}) collective-permute-start(f32[64,512]{1,0:T(8,128)S(1)} %shard_map.59.own), channel_id=1, source_target_pairs={{1,2},{3,4},{5,6},{7,8},{9,10},{11,12},{13,14},{2,1},{4,3},{6,5},{... | collective-permute-start | bytes 393224 | tf_op jit(solution)/shard_map/ppermute | solution.py:66
  108.4 14.0 %collective-permute-start.25 = (f32[64,512]{1,0:T(8,128)S(1)}, f32[64,512]{1,0:T(8,128)S(1)}, u32[]{:S(2)}, u32[]{:S(2)}) collective-permute-start(f32[64,512]{1,0:T(8,128)S(1)} %shard_map.59.own), channel_id=1, source_target_pairs={{0,1},{2,3},{4,5},{6,7},{8,9},{10,11},{12,13},{14,15},{1,0},{3,2},... | collective-permute-start | bytes 393224 | tf_op jit(solution)/shard_map/ppermute | solution.py:66
  111.7 14.0 %collective-permute-start.28 = (f32[64,512]{1,0:T(8,128)S(1)}, f32[64,512]{1,0:T(8,128)S(1)}, u32[]{:S(2)}, u32[]{:S(2)}) collective-permute-start(f32[64,512]{1,0:T(8,128)S(1)} %get-tuple-element.62.last), channel_id=1, source_target_pairs={{0,16},{32,48},{64,80},{96,112},{128,144},{160,176},{192,208},{224... | collective-permute-start | bytes 393224 | tf_op jit(solution)/shard_map/ppermute | solution.py:66
  123.3 3.7 %collective-permute-start.29 = (f32[64,512]{1,0:T(8,128)S(1)}, f32[64,512]{1,0:T(8,128)S(1)}, u32[]{:S(2)}, u32[]{:S(2)}) collective-permute-start(f32[64,512]{1,0:T(8,128)S(1)} %shard_map.60.first), channel_id=1, source_target_pairs={{16,32},{48,64},{80,96},{112,128},{144,160},{176,192},{208,224},{3... | collective-permute-start | bytes 393224 | tf_op jit(solution)/shard_map/ppermute | solution.py:66

commit v4 on v3

--- a/solution.py
+++ b/solution.py
@@ -71,7 +71,7 @@
     return pl.ds(pl.multiple_of(start, HALF), HALF)
 
 
-def tables_kernel(where, x_table, first_table, last_table, y_high, y_low):
+def tables_kernel(where, x_table, first_table, last_table, y_high, y_low, across_high, across_low):
     sign = jnp.where(where[0] == 1, 1, -1)
     whole = x_table.shape[1]
     rows = first_table.shape[1]
@@ -83,7 +83,33 @@
     for ref, shift in ((first_table, sign * HALF), (last_table, -sign * HALF)):
         ref[...] = stacked(jnp.where(row // HALF == col // HALF, weight(row % HALF - col % HALF + shift), 0.0))
     shape = y_high.shape
-    y_high[...], y_low[...] = split(weight(iota(shape, 0) - iota(shape, 1)))
+    row, col = iota(shape, 0), iota(shape, 1)
+    y_high[...], y_low[...] = split(weight(row - col))
+    other = (row < shape[0] // 2) != (col < shape[0] // 2)
+    across_high[...], across_low[...] = split(jnp.where(other, weight(row - col), 0.0))
+
+
+def along_y(value, y_high, y_low, across_high, across_low):
+    dot = functools.partial(jnp.dot, preferred_element_type=jnp.float32)
+    rows, length = value.shape
+    half, quarter = length // 2, length // 4
+    high, low = split(value)
+    left, right, middle = slice(0, half), slice(half, length), slice(quarter, half + quarter)
+    highs = jnp.concatenate([high[:, left], high[:, right]], axis=0)
+    lows = jnp.concatenate([low[:, left], low[:, right]], axis=0)
+    both = dot(jnp.concatenate([highs, lows], axis=0), y_high[...])
+    inside = both[: 2 * rows] + (both[2 * rows :] + dot(highs, y_low[...]))
+    both = dot(jnp.concatenate([high[:, middle], low[:, middle]], axis=0), across_high[...])
+    across = both[:rows] + (both[rows:] + dot(high[:, middle], across_low[...]))
+    return jnp.concatenate(
+        [
+            inside[:rows, :quarter],
+            inside[:rows, quarter:] + across[:, :quarter],
+            inside[rows:, :quarter] + across[:, quarter:],
+            inside[rows:, quarter:],
+        ],
+        axis=1,
+    )
 
 
 def order_kernel(where, rho_prev, potential, rho_ordered, potential_ordered):
@@ -94,23 +120,21 @@
             ref[at * rows : (at + 1) * rows] = source[:, cells(where, at), :].reshape(rows, length)
 
 
-def first_kernel(sizes, where, rho_prev, first, rest):
+def first_kernel(sizes, which, where, rho_prev, out):
     depth, _, length = rho_prev.shape
     whole_x, whole_z = sizes
     mass_z = inside_mass(where[3] + iota((depth, LANES), 0), whole_z)
     mass_y = inside_mass(iota((1, length), 1), length)
-    rows = depth * HALF
-    for at in range(GROUPS):
+    for place, at in enumerate(which):
         span = cells(where, at)
         mass_x = inside_mass(where[2] + span.start + iota((HALF, LANES), 0), whole_x)
-        ref, base = (rest, (at - 1) * rows) if at else (first, 0)
         for z in range(depth):
             mass = (mass_x[:, :1] * mass_z[z : z + 1, :1]) * mass_y
-            start = base + z * HALF
-            ref[start : start + HALF] = rho_prev[z, span, :] / mass
-
-
-def zy(depth, where, own, far, near, y_high, y_low, lined):
+            start = (place * depth + z) * HALF
+            out[start : start + HALF] = rho_prev[z, span, :] / mass
+
+
+def zy(depth, where, own, far, near, y_tables, lined):
     even = where[1]
     length = own.shape[1]
     rows = depth * HALF
@@ -129,17 +153,19 @@
                     total += weights(gap) * (line[here - gap] + line[here + gap])
                 to = start + z * HALF
                 lined[to : to + HALF, lanes] = total
-    return product(stacked(lined[...]), y_high[...], y_low[...])
-
-
-def zy_first_kernel(depth, where, own, far, near, y_high, y_low, out, lined):
-    out[...] = zy(depth, where, own, far, near, y_high, y_low, lined)
-
-
-def zy_rest_kernel(depth, where, own, far, near, y_high, y_low, inner, last, lined):
-    value = zy(depth, where, own, far, near, y_high, y_low, lined)
+    return along_y(lined[...], *y_tables)
+
+
+def zy_one_kernel(depth, where, own, far, near, *rest):
+    *y_tables, out, lined = rest
+    out[...] = zy(depth, where, own, far, near, y_tables, lined)
+
+
+def zy_two_kernel(depth, where, own, far, near, *rest):
+    *y_tables, out, last, lined = rest
+    value = zy(depth, where, own, far, near, y_tables, lined)
     rows = last.shape[0]
-    inner[...], last[...] = value[:-rows], value[-rows:]
+    out[...], last[...] = value[:-rows], value[-rows:]
 
 
 def prox(target):
@@ -213,9 +239,10 @@
     factor = (prev / new)[:, :1]
     depth, _, length = out.shape
     rows = first.shape[0]
+    parts = [first] + [rest.at[at * rows : (at + 1) * rows] for at in range(GROUPS - 1)]
     for at in range(GROUPS):
-        value = rest[(at - 1) * rows : at * rows] if at else first[...]
-        out[:, cells(where, at), :] = (value * factor).reshape(depth, HALF, length)
+        value = jnp.where(where[0] == 1, parts[at][...], parts[GROUPS - 1 - at][...])
+        out[:, at * HALF : (at + 1) * HALF, :] = (value * factor).reshape(depth, HALF, length)
 
 
 def call(kernel, inputs, shapes, scratch=(), scalars=1, dtype=jnp.float32):
@@ -237,34 +264,31 @@
     size_x, size_z = lax.axis_size("gx"), lax.axis_size("gz")
     where = jnp.stack([1 - at_x % 2, 1 - at_z % 2, at_x * width, at_z * depth]).astype(jnp.int32)
     rows = depth * HALF
-    one, three, whole = (rows, length), (3 * rows, length), (4 * rows, length)
+    one, two, three, whole = ((count * rows, length) for count in (1, 2, 3, 4))
     halves = [pltpu.VMEM(whole, jnp.bfloat16)] * 2
 
     start = functools.partial(first_kernel, (width * size_x, depth * size_z))
-    first, rest = call(start, (where, rho_prev), [one, three])
-    table_shapes = [(8 * rows, 4 * rows), (2 * rows, rows), (2 * rows, rows), (length, length), (length, length)]
+    (first,) = call(functools.partial(start, (0, GROUPS - 1)), (where, rho_prev), [two])
+    (rest,) = call(functools.partial(start, range(1, GROUPS - 1)), (where, rho_prev), [two])
+    y_shapes = [(length // 2, length // 2)] * 4
+    table_shapes = [(8 * rows, 4 * rows), (2 * rows, rows), (2 * rows, rows), *y_shapes]
     x_table, first_table, last_table, *y_table = call(tables_kernel, (where,), table_shapes, dtype=jnp.bfloat16)
     rho_ordered, potential_ordered = call(order_kernel, (where, rho_prev, potential), [whole, whole])
 
-    def heat_step(kind, first, rest, whole, scaling):
+    def heat_step(turn, kind, first, rest, whole, scaling):
         started, last = scaling is not None, kind == "last"
         far = swap(first, "gz", 1)
         near = swap(first, "gz", 0)
         far_rest = swap(rest, "gz", 1)
         near_rest = swap(rest, "gz", 0)
-        inner, send0 = call(
-            functools.partial(zy_rest_kernel, depth),
-            (where, rest, far_rest, near_rest, *y_table),
-            [(2 * rows, length), one],
-            [pltpu.VMEM(three, jnp.float32)],
-        )
+        kernel, shapes = (zy_one_kernel, [one]) if turn else (zy_two_kernel, [one, one])
+        inputs = (where, first, far, near, *y_table)
+        send1, *last_group = call(functools.partial(kernel, depth), inputs, shapes, [pltpu.VMEM(first.shape, jnp.float32)])
+        kernel, shapes = (zy_two_kernel, [two, one]) if turn else (zy_one_kernel, [two])
+        inputs = (where, rest, far_rest, near_rest, *y_table)
+        inner, *more = call(functools.partial(kernel, depth), inputs, shapes, [pltpu.VMEM(rest.shape, jnp.float32)])
+        (send0,) = last_group or more
         recv0 = swap(send0, "gx", 0)
-        (send1,) = call(
-            functools.partial(zy_first_kernel, depth),
-            (where, first, far, near, *y_table),
-            [one],
-            [pltpu.VMEM(one, jnp.float32)],
-        )
         recv1 = swap(send1, "gx", 1)
         more = ((scaling[1],) if started else ()) + ((rho_ordered,) if last else ())
         total = [(1, 2 * LANES)] if last else []
@@ -287,11 +311,11 @@
     scaling = None
     for sweep in range(ITERS):
         if sweep:
-            first, rest = heat_step("dual", first, rest, rho_ordered, None)
+            first, rest = heat_step(2 * sweep - 1, "dual", first, rest, rho_ordered, None)
         if sweep < ITERS - 1:
-            first, rest = scaling = heat_step("scaling", first, rest, potential_ordered, scaling)
+            first, rest = scaling = heat_step(2 * sweep, "scaling", first, rest, potential_ordered, scaling)
         else:
-            first, rest, sums = heat_step("last", first, rest, potential_ordered, scaling)
+            first, rest, sums = heat_step(2 * sweep, "last", first, rest, potential_ordered, scaling)
     everyone = size_x * size_z
     sums = jnp.broadcast_to(sums[None], (everyone, 1, 2 * LANES))
     sums = lax.all_to_all(sums, ("gx", "gz"), 0, 0, tiled=True).reshape(everyone, 2 * LANES)

time: 177 us -> 177 us (level)
    pallas_call x24 -> x25, Pallas kernels: 21.6 us -> 21.5 us  [call(): pl.pallas_call(kernel, out_shape=[jax.ShapeDtypeStruct(shape, dtype) for...]
where the time goes in v4:
time: 177 us; the launch traced here: 176 us
  starting transfers between devices  89.3 us (50%)
  blocking collectives  48 us (27%)
  Pallas kernels  21.5 us (12%)
  waiting for transfers between devices  14.9 us (8%)
    ppermute x30, starting transfers between devices, swap(): return lax.ppermute(value, axis, pairs + [(j, i) for i, j in pairs])  89.3 us
    all_to_all x1, blocking collectives, step(): lax.all_to_all(sums, ('gx', 'gz'), 0, 0, tiled=True)  48 us
    pallas_call x25, Pallas kernels, call(): pl.pallas_call(kernel, out_shape=[jax.ShapeDtypeStruct(shape, dtype) for...  21.5 us
    ppermute x30, waiting for transfers between devices, swap(): return lax.ppermute(value, axis, pairs + [(j, i) for i, j in pairs])  14.9 us
  transfers between devices with their start and end apart: 30, of which 9 were waited for; matrix products, arithmetic and copies ran while one was open for 0% of the time, Pallas kernels for 9%

profile of v4, /device:TPU:1, one launch (start us, length us, event | category | flops | bytes accessed | tf_op | source)
XLA Modules:
  0.0 176.1 jit_solution(17017964243278931116)
XLA Ops:
  0.7 1.0 copy-done
  1.8 0.6 shard_map.41.own
  2.4 4.5 %collective-permute-start = (f32[128,512]{1,0:T(8,128)S(1)}, f32[128,512]{1,0:T(8,128)S(1)}, u32[]{:S(2)}, u32[]{:S(2)}) collective-permute-start(f32[128,512]{1,0:T(8,128)S(1)} %shard_map.41.own), channel_id=1, source_target_pairs={{1,2},{3,4},{5,6},{7,8},{9,10},{11,12},{13,14},{2,1},{4,3},{6,5},{... | collective-permute-start | bytes 786440 | tf_op jit(solution)/shard_map/ppermute | solution.py:66
  7.0 0.6 shard_map.44.own
  7.7 3.5 %collective-permute-start.2 = (f32[128,512]{1,0:T(8,128)S(1)}, f32[128,512]{1,0:T(8,128)S(1)}, u32[]{:S(2)}, u32[]{:S(2)}) collective-permute-start(f32[128,512]{1,0:T(8,128)S(1)} %shard_map.44.own), channel_id=1, source_target_pairs={{1,2},{3,4},{5,6},{7,8},{9,10},{11,12},{13,14},{2,1},{4,3},{6,5},{... | collective-permute-start | bytes 786440 | tf_op jit(solution)/shard_map/ppermute | solution.py:66
  11.3 0.9 shard_map.42
  12.2 1.1 shard_map.43
  13.3 1.4 collective-permute-start.4
  14.7 0.6 shard_map.46
  15.4 1.1 shard_map.45.inner
  16.4 1.5 collective-permute-done.4.recv0
  18.0 1.3 shard_map.47
  19.2 4.1 %collective-permute-start.8 = (f32[192,512]{1,0:T(8,128)S(1)}, f32[192,512]{1,0:T(8,128)S(1)}, u32[]{:S(2)}, u32[]{:S(2)}) collective-permute-start(f32[192,512]{1,0:T(8,128)S(1)} %get-tuple-element.47.own.rest_0_), channel_id=1, source_target_pairs={{1,2},{3,4},{5,6},{7,8},{9,10},{11,12},{13,14},{2,1},{4,3},{6,5},{... | collective-permute-start | bytes 1179656 | tf_op jit(solution)/shard_map/ppermute | solution.py:66
  23.4 0.7 collective-permute-start.5
  24.6 3.8 %collective-permute-start.6 = (f32[64,512]{1,0:T(8,128)S(1)}, f32[64,512]{1,0:T(8,128)S(1)}, u32[]{:S(2)}, u32[]{:S(2)}) collective-permute-start(f32[64,512]{1,0:T(8,128)S(1)} %shard_map.48.own.rest_0_), channel_id=1, source_target_pairs={{1,2},{3,4},{5,6},{7,8},{9,10},{11,12},{13,14},{2,1},{4,3},{6,5},{... | collective-permute-start | bytes 393224 | tf_op jit(solution)/shard_map/ppermute | solution.py:66
  28.7 1.3 shard_map.50
  30.0 7.8 %collective-permute-start.10 = (f32[64,512]{1,0:T(8,128)S(1)}, f32[64,512]{1,0:T(8,128)S(1)}, u32[]{:S(2)}, u32[]{:S(2)}) collective-permute-start(f32[64,512]{1,0:T(8,128)S(1)} %get-tuple-element.49.last), channel_id=1, source_target_pairs={{0,16},{32,48},{64,80},{96,112},{128,144},{160,176},{192,208},{224... | collective-permute-start | bytes 393224 | tf_op jit(solution)/shard_map/ppermute | solution.py:66
  37.9 0.9 shard_map.49.first
  38.7 2.5 %collective-permute-done.10.recv0 = f32[64,512]{1,0:T(8,128)S(1)} collective-permute-done((f32[64,512]{1,0:T(8,128)S(1)}, f32[64,512]{1,0:T(8,128)S(1)}, u32[]{:S(2)}, u32[]{:S(2)}) %collective-permute-start.10) | collective-permute-done | bytes 131104 | tf_op jit(solution)/shard_map/ppermute | solution.py:66
  41.7 4.5 %collective-permute-start.14 = (f32[192,512]{1,0:T(8,128)S(1)}, f32[192,512]{1,0:T(8,128)S(1)}, u32[]{:S(2)}, u32[]{:S(2)}) collective-permute-start(f32[192,512]{1,0:T(8,128)S(1)} %get-tuple-element.52.own), channel_id=1, source_target_pairs={{1,2},{3,4},{5,6},{7,8},{9,10},{11,12},{13,14},{2,1},{4,3},{6,5},{... | collective-permute-start | bytes 1179656 | tf_op jit(solution)/shard_map/ppermute | solution.py:66
  46.3 0.7 collective-permute-start.11
  47.2 4.2 %collective-permute-start.12 = (f32[64,512]{1,0:T(8,128)S(1)}, f32[64,512]{1,0:T(8,128)S(1)}, u32[]{:S(2)}, u32[]{:S(2)}) collective-permute-start(f32[64,512]{1,0:T(8,128)S(1)} %shard_map.52.own), channel_id=1, source_target_pairs={{1,2},{3,4},{5,6},{7,8},{9,10},{11,12},{13,14},{2,1},{4,3},{6,5},{... | collective-permute-start | bytes 393224 | tf_op jit(solution)/shard_map/ppermute | solution.py:66
  51.7 1.3 shard_map.54
  52.9 11.2 %collective-permute-start.16 = (f32[64,512]{1,0:T(8,128)S(1)}, f32[64,512]{1,0:T(8,128)S(1)}, u32[]{:S(2)}, u32[]{:S(2)}) collective-permute-start(f32[64,512]{1,0:T(8,128)S(1)} %get-tuple-element.54.last), channel_id=1, source_target_pairs={{0,16},{32,48},{64,80},{96,112},{128,144},{160,176},{192,208},{224... | collective-permute-start | bytes 393224 | tf_op jit(solution)/shard_map/ppermute | solution.py:66
  64.2 0.9 shard_map.53.first
  65.0 2.5 %collective-permute-done.16.recv0 = f32[64,512]{1,0:T(8,128)S(1)} collective-permute-done((f32[64,512]{1,0:T(8,128)S(1)}, f32[64,512]{1,0:T(8,128)S(1)}, u32[]{:S(2)}, u32[]{:S(2)}) %collective-permute-start.16) | collective-permute-done | bytes 131104 | tf_op jit(solution)/shard_map/ppermute | solution.py:66
  67.5 1.2 shard_map.55
  68.8 6.7 %collective-permute-start.20 = (f32[192,512]{1,0:T(8,128)S(1)}, f32[192,512]{1,0:T(8,128)S(1)}, u32[]{:S(2)}, u32[]{:S(2)}) collective-permute-start(f32[192,512]{1,0:T(8,128)S(1)} %get-tuple-element.56.own.rest_0_), channel_id=1, source_target_pairs={{1,2},{3,4},{5,6},{7,8},{9,10},{11,12},{13,14},{2,1},{4,3},{6,5},{... | collective-permute-start | bytes 1179656 | tf_op jit(solution)/shard_map/ppermute | solution.py:66
  75.6 0.7 collective-permute-start.17
  76.3 0.5 shard_map.56.own.rest_0_
  76.8 2.4 %collective-permute-start.18 = (f32[64,512]{1,0:T(8,128)S(1)}, f32[64,512]{1,0:T(8,128)S(1)}, u32[]{:S(2)}, u32[]{:S(2)}) collective-permute-start(f32[64,512]{1,0:T(8,128)S(1)} %shard_map.56.own.rest_0_), channel_id=1, source_target_pairs={{1,2},{3,4},{5,6},{7,8},{9,10},{11,12},{13,14},{2,1},{4,3},{6,5},{... | collective-permute-start | bytes 393224 | tf_op jit(solution)/shard_map/ppermute | solution.py:66
  79.3 1.6 collective-permute-done.20.far
  81.0 1.3 shard_map.58
  82.2 10.9 %collective-permute-start.22 = (f32[64,512]{1,0:T(8,128)S(1)}, f32[64,512]{1,0:T(8,128)S(1)}, u32[]{:S(2)}, u32[]{:S(2)}) collective-permute-start(f32[64,512]{1,0:T(8,128)S(1)} %get-tuple-element.58.last), channel_id=1, source_target_pairs={{0,16},{32,48},{64,80},{96,112},{128,144},{160,176},{192,208},{224... | collective-permute-start | bytes 393224 | tf_op jit(solution)/shard_map/ppermute | solution.py:66
  93.1 0.9 shard_map.57.first
  94.0 2.5 %collective-permute-done.22.recv0 = f32[64,512]{1,0:T(8,128)S(1)} collective-permute-done((f32[64,512]{1,0:T(8,128)S(1)}, f32[64,512]{1,0:T(8,128)S(1)}, u32[]{:S(2)}, u32[]{:S(2)}) %collective-permute-start.22) | collective-permute-done | bytes 131104 | tf_op jit(solution)/shard_map/ppermute | solution.py:66
  96.9 7.0 %collective-permute-start.26 = (f32[192,512]{1,0:T(8,128)S(1)}, f32[192,512]{1,0:T(8,128)S(1)}, u32[]{:S(2)}, u32[]{:S(2)}) collective-permute-start(f32[192,512]{1,0:T(8,128)S(1)} %get-tuple-element.60.own), channel_id=1, source_target_pairs={{1,2},{3,4},{5,6},{7,8},{9,10},{11,12},{13,14},{2,1},{4,3},{6,5},{... | collective-permute-start | bytes 1179656 | tf_op jit(solution)/shard_map/ppermute | solution.py:66
  104.0 0.7 collective-permute-start.23
  104.9 2.4 %collective-permute-start.24 = (f32[64,512]{1,0:T(8,128)S(1)}, f32[64,512]{1,0:T(8,128)S(1)}, u32[]{:S(2)}, u32[]{:S(2)}) collective-permute-start(f32[64,512]{1,0:T(8,128)S(1)} %shard_map.60.own), channel_id=1, source_target_pairs={{1,2},{3,4},{5,6},{7,8},{9,10},{11,12},{13,14},{2,1},{4,3},{6,5},{... | collective-permute-start | bytes 393224 | tf_op jit(solution)/shard_map/ppermute | solution.py:66
  107.4 2.0 %collective-permute-done.26.far = f32[192,512]{1,0:T(8,128)S(1)} collective-permute-done((f32[192,512]{1,0:T(8,128)S(1)}, f32[192,512]{1,0:T(8,128)S(1)}, u32[]{:S(2)}, u32[]{:S(2)}) %collective-permute-start.26) | collective-permute-done | bytes 393248 | tf_op jit(solution)/shard_map/ppermute | solution.py:66
  109.4 1.3 shard_map.62
  110.6 10.6 %collective-permute-start.28 = (f32[64,512]{1,0:T(8,128)S(1)}, f32[64,512]{1,0:T(8,128)S(1)}, u32[]{:S(2)}, u32[]{:S(2)}) collective-permute-start(f32[64,512]{1,0:T(8,128)S(1)} %get-tuple-element.62.last), channel_id=1, source_target_pairs={{0,16},{32,48},{64,80},{96,112},{128,144},{160,176},{192,208},{224... | collective-permute-start | bytes 393224 | tf_op jit(solution)/shard_map/ppermute | solution.py:66
  121.3 0.9 shard_map.61.first
  122.2 0.7 collective-permute-start.29
  122.8 1.8 %collective-permute-done.28.recv0 = f32[64,512]{1,0:T(8,128)S(1)} collective-permute-done((f32[64,512]{1,0:T(8,128)S(1)}, f32[64,512]{1,0:T(8,128)S(1)}, u32[]{:S(2)}, u32[]{:S(2)}) %collective-permute-start.28) | collective-permute-done | bytes 131104 | tf_op jit(solution)/shard_map/ppermute | solution.py:66
  124.7 1.2 shard_map.63
  126.6 48.0 %all_to_all.5 = f32[256,1,256]{2,1,0:T(1,128)S(1)} all-to-all(f32[256,1,256]{2,1,0:T(1,128)S(1)} %broadcast_in_dim.9), channel_id=1, replica_groups=mesh['gx'=16,'gz'=16] {'gx','gz'}, dimensions={0} | all-to-all | bytes 524288 | tf_op jit(solution)/shard_map/all_to_all | solution.py:321
  174.6 1.5 shard_map.65
  (47 shorter events, 3.9 us)
Async XLA Ops:
  0.7 1.0 copy-start
  2.4 9.8 %collective-permute-start = (f32[128,512]{1,0:T(8,128)S(1)}, f32[128,512]{1,0:T(8,128)S(1)}, u32[]{:S(2)}, u32[]{:S(2)}) collective-permute-start(f32[128,512]{1,0:T(8,128)S(1)} %shard_map.41.own), channel_id=1, source_target_pairs={{1,2},{3,4},{5,6},{7,8},{9,10},{11,12},{13,14},{2,1},{4,3},{6,5},{... | collective-permute-start | bytes 786440 | tf_op jit(solution)/shard_map/ppermute | solution.py:66
  6.9 5.3 %collective-permute-start.1 = (f32[128,512]{1,0:T(8,128)S(1)}, f32[128,512]{1,0:T(8,128)S(1)}, u32[]{:S(2)}, u32[]{:S(2)}) collective-permute-start(f32[128,512]{1,0:T(8,128)S(1)} %shard_map.41.own), channel_id=1, source_target_pairs={{0,1},{2,3},{4,5},{6,7},{8,9},{10,11},{12,13},{14,15},{1,0},{3,2},... | collective-permute-start | bytes 786440 | tf_op jit(solution)/shard_map/ppermute | solution.py:66
  7.7 7.7 %collective-permute-start.2 = (f32[128,512]{1,0:T(8,128)S(1)}, f32[128,512]{1,0:T(8,128)S(1)}, u32[]{:S(2)}, u32[]{:S(2)}) collective-permute-start(f32[128,512]{1,0:T(8,128)S(1)} %shard_map.44.own), channel_id=1, source_target_pairs={{1,2},{3,4},{5,6},{7,8},{9,10},{11,12},{13,14},{2,1},{4,3},{6,5},{... | collective-permute-start | bytes 786440 | tf_op jit(solution)/shard_map/ppermute | solution.py:66
  11.2 4.2 %collective-permute-start.3 = (f32[128,512]{1,0:T(8,128)S(1)}, f32[128,512]{1,0:T(8,128)S(1)}, u32[]{:S(2)}, u32[]{:S(2)}) collective-permute-start(f32[128,512]{1,0:T(8,128)S(1)} %shard_map.44.own), channel_id=1, source_target_pairs={{0,1},{2,3},{4,5},{6,7},{8,9},{10,11},{12,13},{14,15},{1,0},{3,2},... | collective-permute-start | bytes 786440 | tf_op jit(solution)/shard_map/ppermute | solution.py:66
  12.2 2.5 %copy-start.1 = (f32[8,32,512]{2,1,0:T(8,128)S(1)}, f32[8,32,512]{2,1,0:T(8,128)}, u32[]{:S(2)}) copy-start(f32[8,32,512]{2,1,0:T(8,128)} %rho_prev.5) | copy-start | bytes 1572868
  12.2 2.5 %copy-start.2 = (f32[8,32,512]{2,1,0:T(8,128)S(1)}, f32[8,32,512]{2,1,0:T(8,128)}, u32[]{:S(2)}) copy-start(f32[8,32,512]{2,1,0:T(8,128)} %potential.1) | copy-start | bytes 1572868
  13.3 4.7 %collective-permute-start.4 = (f32[64,512]{1,0:T(8,128)S(1)}, f32[64,512]{1,0:T(8,128)S(1)}, u32[]{:S(2)}, u32[]{:S(2)}) collective-permute-start(f32[64,512]{1,0:T(8,128)S(1)} %get-tuple-element.41.last), channel_id=1, source_target_pairs={{0,16},{32,48},{64,80},{96,112},{128,144},{160,176},{192,208},{224... | collective-permute-start | bytes 393224 | tf_op jit(solution)/shard_map/ppermute | solution.py:66
  19.2 9.5 %collective-permute-start.8 = (f32[192,512]{1,0:T(8,128)S(1)}, f32[192,512]{1,0:T(8,128)S(1)}, u32[]{:S(2)}, u32[]{:S(2)}) collective-permute-start(f32[192,512]{1,0:T(8,128)S(1)} %get-tuple-element.47.own.rest_0_), channel_id=1, source_target_pairs={{1,2},{3,4},{5,6},{7,8},{9,10},{11,12},{13,14},{2,1},{4,3},{6,5},{... | collective-permute-start | bytes 1179656 | tf_op jit(solution)/shard_map/ppermute | solution.py:66
  23.3 5.4 %collective-permute-start.9 = (f32[192,512]{1,0:T(8,128)S(1)}, f32[192,512]{1,0:T(8,128)S(1)}, u32[]{:S(2)}, u32[]{:S(2)}) collective-permute-start(f32[192,512]{1,0:T(8,128)S(1)} %get-tuple-element.47.own.rest_0_), channel_id=1, source_target_pairs={{0,1},{2,3},{4,5},{6,7},{8,9},{10,11},{12,13},{14,15},{1,0},{3,2},... | collective-permute-start | bytes 1179656 | tf_op jit(solution)/shard_map/ppermute | solution.py:66
  23.4 0.7 collective-permute-start.5
  24.6 13.2 %collective-permute-start.6 = (f32[64,512]{1,0:T(8,128)S(1)}, f32[64,512]{1,0:T(8,128)S(1)}, u32[]{:S(2)}, u32[]{:S(2)}) collective-permute-start(f32[64,512]{1,0:T(8,128)S(1)} %shard_map.48.own.rest_0_), channel_id=1, source_target_pairs={{1,2},{3,4},{5,6},{7,8},{9,10},{11,12},{13,14},{2,1},{4,3},{6,5},{... | collective-permute-start | bytes 393224 | tf_op jit(solution)/shard_map/ppermute | solution.py:66
  28.4 9.4 %collective-permute-start.7 = (f32[64,512]{1,0:T(8,128)S(1)}, f32[64,512]{1,0:T(8,128)S(1)}, u32[]{:S(2)}, u32[]{:S(2)}) collective-permute-start(f32[64,512]{1,0:T(8,128)S(1)} %shard_map.48.own.rest_0_), channel_id=1, source_target_pairs={{0,1},{2,3},{4,5},{6,7},{8,9},{10,11},{12,13},{14,15},{1,0},{3,2},... | collective-permute-start | bytes 393224 | tf_op jit(solution)/shard_map/ppermute | solution.py:66
  30.0 11.2 %collective-permute-start.10 = (f32[64,512]{1,0:T(8,128)S(1)}, f32[64,512]{1,0:T(8,128)S(1)}, u32[]{:S(2)}, u32[]{:S(2)}) collective-permute-start(f32[64,512]{1,0:T(8,128)S(1)} %get-tuple-element.49.last), channel_id=1, source_target_pairs={{0,16},{32,48},{64,80},{96,112},{128,144},{160,176},{192,208},{224... | collective-permute-start | bytes 393224 | tf_op jit(solution)/shard_map/ppermute | solution.py:66
  41.7 10.0 %collective-permute-start.14 = (f32[192,512]{1,0:T(8,128)S(1)}, f32[192,512]{1,0:T(8,128)S(1)}, u32[]{:S(2)}, u32[]{:S(2)}) collective-permute-start(f32[192,512]{1,0:T(8,128)S(1)} %get-tuple-element.52.own), channel_id=1, source_target_pairs={{1,2},{3,4},{5,6},{7,8},{9,10},{11,12},{13,14},{2,1},{4,3},{6,5},{... | collective-permute-start | bytes 1179656 | tf_op jit(solution)/shard_map/ppermute | solution.py:66
  46.2 5.4 %collective-permute-start.15 = (f32[192,512]{1,0:T(8,128)S(1)}, f32[192,512]{1,0:T(8,128)S(1)}, u32[]{:S(2)}, u32[]{:S(2)}) collective-permute-start(f32[192,512]{1,0:T(8,128)S(1)} %get-tuple-element.52.own), channel_id=1, source_target_pairs={{0,1},{2,3},{4,5},{6,7},{8,9},{10,11},{12,13},{14,15},{1,0},{3,2},... | collective-permute-start | bytes 1179656 | tf_op jit(solution)/shard_map/ppermute | solution.py:66
  46.3 0.7 collective-permute-start.11
  47.2 17.0 %collective-permute-start.12 = (f32[64,512]{1,0:T(8,128)S(1)}, f32[64,512]{1,0:T(8,128)S(1)}, u32[]{:S(2)}, u32[]{:S(2)}) collective-permute-start(f32[64,512]{1,0:T(8,128)S(1)} %shard_map.52.own), channel_id=1, source_target_pairs={{1,2},{3,4},{5,6},{7,8},{9,10},{11,12},{13,14},{2,1},{4,3},{6,5},{... | collective-permute-start | bytes 393224 | tf_op jit(solution)/shard_map/ppermute | solution.py:66
  51.4 12.7 %collective-permute-start.13 = (f32[64,512]{1,0:T(8,128)S(1)}, f32[64,512]{1,0:T(8,128)S(1)}, u32[]{:S(2)}, u32[]{:S(2)}) collective-permute-start(f32[64,512]{1,0:T(8,128)S(1)} %shard_map.52.own), channel_id=1, source_target_pairs={{0,1},{2,3},{4,5},{6,7},{8,9},{10,11},{12,13},{14,15},{1,0},{3,2},... | collective-permute-start | bytes 393224 | tf_op jit(solution)/shard_map/ppermute | solution.py:66
  52.9 14.6 %collective-permute-start.16 = (f32[64,512]{1,0:T(8,128)S(1)}, f32[64,512]{1,0:T(8,128)S(1)}, u32[]{:S(2)}, u32[]{:S(2)}) collective-permute-start(f32[64,512]{1,0:T(8,128)S(1)} %get-tuple-element.54.last), channel_id=1, source_target_pairs={{0,16},{32,48},{64,80},{96,112},{128,144},{160,176},{192,208},{224... | collective-permute-start | bytes 393224 | tf_op jit(solution)/shard_map/ppermute | solution.py:66
  68.8 12.2 %collective-permute-start.20 = (f32[192,512]{1,0:T(8,128)S(1)}, f32[192,512]{1,0:T(8,128)S(1)}, u32[]{:S(2)}, u32[]{:S(2)}) collective-permute-start(f32[192,512]{1,0:T(8,128)S(1)} %get-tuple-element.56.own.rest_0_), channel_id=1, source_target_pairs={{1,2},{3,4},{5,6},{7,8},{9,10},{11,12},{13,14},{2,1},{4,3},{6,5},{... | collective-permute-start | bytes 1179656 | tf_op jit(solution)/shard_map/ppermute | solution.py:66
  75.5 5.4 %collective-permute-start.21 = (f32[192,512]{1,0:T(8,128)S(1)}, f32[192,512]{1,0:T(8,128)S(1)}, u32[]{:S(2)}, u32[]{:S(2)}) collective-permute-start(f32[192,512]{1,0:T(8,128)S(1)} %get-tuple-element.56.own.rest_0_), channel_id=1, source_target_pairs={{0,1},{2,3},{4,5},{6,7},{8,9},{10,11},{12,13},{14,15},{1,0},{3,2},... | collective-permute-start | bytes 1179656 | tf_op jit(solution)/shard_map/ppermute | solution.py:66
  75.6 0.7 collective-permute-start.17
  76.8 16.3 %collective-permute-start.18 = (f32[64,512]{1,0:T(8,128)S(1)}, f32[64,512]{1,0:T(8,128)S(1)}, u32[]{:S(2)}, u32[]{:S(2)}) collective-permute-start(f32[64,512]{1,0:T(8,128)S(1)} %shard_map.56.own.rest_0_), channel_id=1, source_target_pairs={{1,2},{3,4},{5,6},{7,8},{9,10},{11,12},{13,14},{2,1},{4,3},{6,5},{... | collective-permute-start | bytes 393224 | tf_op jit(solution)/shard_map/ppermute | solution.py:66
  79.2 13.9 %collective-permute-start.19 = (f32[64,512]{1,0:T(8,128)S(1)}, f32[64,512]{1,0:T(8,128)S(1)}, u32[]{:S(2)}, u32[]{:S(2)}) collective-permute-start(f32[64,512]{1,0:T(8,128)S(1)} %shard_map.56.own.rest_0_), channel_id=1, source_target_pairs={{0,1},{2,3},{4,5},{6,7},{8,9},{10,11},{12,13},{14,15},{1,0},{3,2},... | collective-permute-start | bytes 393224 | tf_op jit(solution)/shard_map/ppermute | solution.py:66
  82.2 14.3 %collective-permute-start.22 = (f32[64,512]{1,0:T(8,128)S(1)}, f32[64,512]{1,0:T(8,128)S(1)}, u32[]{:S(2)}, u32[]{:S(2)}) collective-permute-start(f32[64,512]{1,0:T(8,128)S(1)} %get-tuple-element.58.last), channel_id=1, source_target_pairs={{0,16},{32,48},{64,80},{96,112},{128,144},{160,176},{192,208},{224... | collective-permute-start | bytes 393224 | tf_op jit(solution)/shard_map/ppermute | solution.py:66
  96.9 12.4 %collective-permute-start.26 = (f32[192,512]{1,0:T(8,128)S(1)}, f32[192,512]{1,0:T(8,128)S(1)}, u32[]{:S(2)}, u32[]{:S(2)}) collective-permute-start(f32[192,512]{1,0:T(8,128)S(1)} %get-tuple-element.60.own), channel_id=1, source_target_pairs={{1,2},{3,4},{5,6},{7,8},{9,10},{11,12},{13,14},{2,1},{4,3},{6,5},{... | collective-permute-start | bytes 1179656 | tf_op jit(solution)/shard_map/ppermute | solution.py:66
  103.9 5.4 %collective-permute-start.27 = (f32[192,512]{1,0:T(8,128)S(1)}, f32[192,512]{1,0:T(8,128)S(1)}, u32[]{:S(2)}, u32[]{:S(2)}) collective-permute-start(f32[192,512]{1,0:T(8,128)S(1)} %get-tuple-element.60.own), channel_id=1, source_target_pairs={{0,1},{2,3},{4,5},{6,7},{8,9},{10,11},{12,13},{14,15},{1,0},{3,2},... | collective-permute-start | bytes 1179656 | tf_op jit(solution)/shard_map/ppermute | solution.py:66
  104.0 0.7 collective-permute-start.23
  104.9 16.4 %collective-permute-start.24 = (f32[64,512]{1,0:T(8,128)S(1)}, f32[64,512]{1,0:T(8,128)S(1)}, u32[]{:S(2)}, u32[]{:S(2)}) collective-permute-start(f32[64,512]{1,0:T(8,128)S(1)} %shard_map.60.own), channel_id=1, source_target_pairs={{1,2},{3,4},{5,6},{7,8},{9,10},{11,12},{13,14},{2,1},{4,3},{6,5},{... | collective-permute-start | bytes 393224 | tf_op jit(solution)/shard_map/ppermute | solution.py:66
  107.3 14.0 %collective-permute-start.25 = (f32[64,512]{1,0:T(8,128)S(1)}, f32[64,512]{1,0:T(8,128)S(1)}, u32[]{:S(2)}, u32[]{:S(2)}) collective-permute-start(f32[64,512]{1,0:T(8,128)S(1)} %shard_map.60.own), channel_id=1, source_target_pairs={{0,1},{2,3},{4,5},{6,7},{8,9},{10,11},{12,13},{14,15},{1,0},{3,2},... | collective-permute-start | bytes 393224 | tf_op jit(solution)/shard_map/ppermute | solution.py:66
  110.6 14.0 %collective-permute-start.28 = (f32[64,512]{1,0:T(8,128)S(1)}, f32[64,512]{1,0:T(8,128)S(1)}, u32[]{:S(2)}, u32[]{:S(2)}) collective-permute-start(f32[64,512]{1,0:T(8,128)S(1)} %get-tuple-element.62.last), channel_id=1, source_target_pairs={{0,16},{32,48},{64,80},{96,112},{128,144},{160,176},{192,208},{224... | collective-permute-start | bytes 393224 | tf_op jit(solution)/shard_map/ppermute | solution.py:66
  122.2 3.8 %collective-permute-start.29 = (f32[64,512]{1,0:T(8,128)S(1)}, f32[64,512]{1,0:T(8,128)S(1)}, u32[]{:S(2)}, u32[]{:S(2)}) collective-permute-start(f32[64,512]{1,0:T(8,128)S(1)} %shard_map.61.first), channel_id=1, source_target_pairs={{16,32},{48,64},{80,96},{112,128},{144,160},{176,192},{208,224},{3... | collective-permute-start | bytes 393224 | tf_op jit(solution)/shard_map/ppermute | solution.py:66

commit v5 on v4

--- a/solution.py
+++ b/solution.py
@@ -56,6 +56,10 @@
     return both[:rows] + (both[rows:] + dot(left[:rows], right_low))
 
 
+def even(axis):
+    return lax.axis_index(axis) % 2 == 0
+
+
 def iota(shape, dim):
     return lax.broadcasted_iota(jnp.int32, shape, dim)
 
@@ -66,13 +70,13 @@
     return lax.ppermute(value, axis, pairs + [(j, i) for i, j in pairs])
 
 
-def cells(where, at):
-    start = jnp.where(where[0] == 1, at, GROUPS - 1 - at) * HALF
+def cells(at):
+    start = jnp.where(even("gx"), at, GROUPS - 1 - at) * HALF
     return pl.ds(pl.multiple_of(start, HALF), HALF)
 
 
-def tables_kernel(where, x_table, first_table, last_table, y_high, y_low, across_high, across_low):
-    sign = jnp.where(where[0] == 1, 1, -1)
+def tables_kernel(x_table, first_table, last_table, y_high, y_low, across_high, across_low):
+    sign = jnp.where(even("gx"), 1, -1)
     whole = x_table.shape[1]
     rows = first_table.shape[1]
     row, col = iota((whole, whole), 0), iota((whole, whole), 1)
@@ -112,39 +116,39 @@
     )
 
 
-def order_kernel(where, rho_prev, potential, rho_ordered, potential_ordered):
+def order_kernel(rho_prev, potential, rho_ordered, potential_ordered):
     depth, _, length = rho_prev.shape
     rows = depth * HALF
     for source, ref in ((rho_prev, rho_ordered), (potential, potential_ordered)):
         for at in range(GROUPS):
-            ref[at * rows : (at + 1) * rows] = source[:, cells(where, at), :].reshape(rows, length)
-
-
-def first_kernel(sizes, which, where, rho_prev, out):
-    depth, _, length = rho_prev.shape
+            ref[at * rows : (at + 1) * rows] = source[:, cells(at), :].reshape(rows, length)
+
+
+def first_kernel(sizes, which, rho_prev, out):
+    depth, width, length = rho_prev.shape
     whole_x, whole_z = sizes
-    mass_z = inside_mass(where[3] + iota((depth, LANES), 0), whole_z)
+    mass_z = inside_mass(lax.axis_index("gz") * depth + iota((depth, LANES), 0), whole_z)
     mass_y = inside_mass(iota((1, length), 1), length)
     for place, at in enumerate(which):
-        span = cells(where, at)
-        mass_x = inside_mass(where[2] + span.start + iota((HALF, LANES), 0), whole_x)
+        span = cells(at)
+        mass_x = inside_mass(lax.axis_index("gx") * width + span.start + iota((HALF, LANES), 0), whole_x)
         for z in range(depth):
             mass = (mass_x[:, :1] * mass_z[z : z + 1, :1]) * mass_y
             start = (place * depth + z) * HALF
             out[start : start + HALF] = rho_prev[z, span, :] / mass
 
 
-def zy(depth, where, own, far, near, y_tables, lined):
-    even = where[1]
+def zy(depth, own, far, near, y_tables, lined):
     length = own.shape[1]
     rows = depth * HALF
+    near_after = even("gz")
     for start in range(0, own.shape[0], rows):
         span = slice(start, start + rows)
         for at in range(0, length, LANES):
             lanes = slice(at, at + LANES)
             far_part, near_part = far[span, lanes], near[span, lanes]
-            before = jnp.where(even == 1, far_part, near_part)
-            after = jnp.where(even == 1, near_part, far_part)
+            before = jnp.where(near_after, far_part, near_part)
+            after = jnp.where(near_after, near_part, far_part)
             line = [part[z * HALF : (z + 1) * HALF] for part in (before, own[span, lanes], after) for z in range(depth)]
             for z in range(depth):
                 here = z + depth
@@ -156,14 +160,14 @@
     return along_y(lined[...], *y_tables)
 
 
-def zy_one_kernel(depth, where, own, far, near, *rest):
+def zy_one_kernel(depth, own, far, near, *rest):
     *y_tables, out, lined = rest
-    out[...] = zy(depth, where, own, far, near, y_tables, lined)
-
-
-def zy_two_kernel(depth, where, own, far, near, *rest):
+    out[...] = zy(depth, own, far, near, y_tables, lined)
+
+
+def zy_two_kernel(depth, own, far, near, *rest):
     *y_tables, out, last, lined = rest
-    value = zy(depth, where, own, far, near, y_tables, lined)
+    value = zy(depth, own, far, near, y_tables, lined)
     rows = last.shape[0]
     out[...], last[...] = value[:-rows], value[-rows:]
 
@@ -230,7 +234,7 @@
         sums[:, LANES:] += lane_sums(result)
 
 
-def scale_kernel(where, first, rest, sums, out, ratio):
+def scale_kernel(first, rest, sums, out, ratio):
     totals = jnp.sum(sums[...], axis=0, keepdims=True)
     mass_prev, mass_new = jnp.sum(totals[:, :LANES]), jnp.sum(totals[:, LANES:])
     ones = jnp.ones((1, LANES), jnp.float32)
@@ -241,17 +245,15 @@
     rows = first.shape[0]
     parts = [first] + [rest.at[at * rows : (at + 1) * rows] for at in range(GROUPS - 1)]
     for at in range(GROUPS):
-        value = jnp.where(where[0] == 1, parts[at][...], parts[GROUPS - 1 - at][...])
+        value = jnp.where(even("gx"), parts[at][...], parts[GROUPS - 1 - at][...])
         out[:, at * HALF : (at + 1) * HALF, :] = (value * factor).reshape(depth, HALF, length)
 
 
-def call(kernel, inputs, shapes, scratch=(), scalars=1, dtype=jnp.float32):
-    specs = [pl.BlockSpec(memory_space=pltpu.SMEM)] * scalars
-    specs += [pl.BlockSpec(memory_space=pltpu.VMEM)] * (len(inputs) - scalars)
+def call(kernel, inputs, shapes, scratch=(), dtype=jnp.float32):
     return pl.pallas_call(
         kernel,
         out_shape=[jax.ShapeDtypeStruct(shape, dtype) for shape in shapes],
-        in_specs=specs,
+        in_specs=[pl.BlockSpec(memory_space=pltpu.VMEM)] * len(inputs),
         out_specs=[pl.BlockSpec(memory_space=pltpu.VMEM)] * len(shapes),
         scratch_shapes=scratch,
         compiler_params=pltpu.CompilerParams(vmem_limit_bytes=20 << 20),
@@ -260,20 +262,18 @@
 
 def step(rho_prev, potential):
     depth, width, length = rho_prev.shape
-    at_x, at_z = lax.axis_index("gx"), lax.axis_index("gz")
     size_x, size_z = lax.axis_size("gx"), lax.axis_size("gz")
-    where = jnp.stack([1 - at_x % 2, 1 - at_z % 2, at_x * width, at_z * depth]).astype(jnp.int32)
     rows = depth * HALF
     one, two, three, whole = ((count * rows, length) for count in (1, 2, 3, 4))
     halves = [pltpu.VMEM(whole, jnp.bfloat16)] * 2
 
     start = functools.partial(first_kernel, (width * size_x, depth * size_z))
-    (first,) = call(functools.partial(start, (0, GROUPS - 1)), (where, rho_prev), [two])
-    (rest,) = call(functools.partial(start, range(1, GROUPS - 1)), (where, rho_prev), [two])
+    (first,) = call(functools.partial(start, (0, GROUPS - 1)), (rho_prev,), [two])
+    (rest,) = call(functools.partial(start, range(1, GROUPS - 1)), (rho_prev,), [two])
     y_shapes = [(length // 2, length // 2)] * 4
     table_shapes = [(8 * rows, 4 * rows), (2 * rows, rows), (2 * rows, rows), *y_shapes]
-    x_table, first_table, last_table, *y_table = call(tables_kernel, (where,), table_shapes, dtype=jnp.bfloat16)
-    rho_ordered, potential_ordered = call(order_kernel, (where, rho_prev, potential), [whole, whole])
+    x_table, first_table, last_table, *y_table = call(tables_kernel, (), table_shapes, dtype=jnp.bfloat16)
+    rho_ordered, potential_ordered = call(order_kernel, (rho_prev, potential), [whole, whole])
 
     def heat_step(turn, kind, first, rest, whole, scaling):
         started, last = scaling is not None, kind == "last"
@@ -282,10 +282,10 @@
         far_rest = swap(rest, "gz", 1)
         near_rest = swap(rest, "gz", 0)
         kernel, shapes = (zy_one_kernel, [one]) if turn else (zy_two_kernel, [one, one])
-        inputs = (where, first, far, near, *y_table)
+        inputs = (first, far, near, *y_table)
         send1, *last_group = call(functools.partial(kernel, depth), inputs, shapes, [pltpu.VMEM(first.shape, jnp.float32)])
         kernel, shapes = (zy_two_kernel, [two, one]) if turn else (zy_one_kernel, [two])
-        inputs = (where, rest, far_rest, near_rest, *y_table)
+        inputs = (rest, far_rest, near_rest, *y_table)
         inner, *more = call(functools.partial(kernel, depth), inputs, shapes, [pltpu.VMEM(rest.shape, jnp.float32)])
         (send0,) = last_group or more
         recv0 = swap(send0, "gx", 0)
@@ -297,14 +297,12 @@
             (send1, inner, send0, recv0, x_table, last_table, whole, *more),
             [three, one] + total,
             halves,
-            0,
         )
         more = ((scaling[0],) if started else ()) + tuple(sums)
         new_first, *sums = call(
             functools.partial(first_group_kernel, kind, started),
             (part, recv1, first_table, whole, *more),
             [one] + total,
-            scalars=0,
         )
         return new_first, new_rest, *sums
 
@@ -319,7 +317,7 @@
     everyone = size_x * size_z
     sums = jnp.broadcast_to(sums[None], (everyone, 1, 2 * LANES))
     sums = lax.all_to_all(sums, ("gx", "gz"), 0, 0, tiled=True).reshape(everyone, 2 * LANES)
-    rho_next, ratio = call(scale_kernel, (where, first, rest, sums), [(depth, width, length), (1, LANES)])
+    rho_next, ratio = call(scale_kernel, (first, rest, sums), [(depth, width, length), (1, LANES)])
     return rho_next, ratio[0, :1]
 
 

time: 177 us -> 172 us (0.972)
  Pallas kernels: 21.5 us -> 13.4 us
  waiting for transfers between devices: 14.9 us -> 18.4 us
    pallas_call x25, Pallas kernels: 21.5 us -> 13.4 us  [call(): pl.pallas_call(kernel, out_shape=[jax.ShapeDtypeStruct(shape, dtype) for...]
    ppermute x30, waiting for transfers between devices: 14.9 us -> 18.4 us  [swap(): return lax.ppermute(value, axis, pairs + [(j, i) for i, j in pairs])]
  transfers between devices with their start and end apart: 30 -> 30, of which waited for: 9 -> 9; matrix products, arithmetic and copies ran while one was open for 0% -> 0% of each run, Pallas kernels for 9% -> 5%
where the time goes in v5:
time: 172 us; the launch traced here: 171 us
  starting transfers between devices  90.1 us (52%)
  blocking collectives  47 us (27%)
  waiting for transfers between devices  18.4 us (11%)
  Pallas kernels  13.4 us (8%)
    ppermute x30, starting transfers between devices, swap(): return lax.ppermute(value, axis, pairs + [(j, i) for i, j in pairs])  90.1 us
    all_to_all x1, blocking collectives, step(): lax.all_to_all(sums, ('gx', 'gz'), 0, 0, tiled=True)  47 us
    ppermute x30, waiting for transfers between devices, swap(): return lax.ppermute(value, axis, pairs + [(j, i) for i, j in pairs])  18.4 us
    pallas_call x25, Pallas kernels, call(): pl.pallas_call(kernel, out_shape=[jax.ShapeDtypeStruct(shape, dtype) for...  13.4 us
  transfers between devices with their start and end apart: 30, of which 9 were waited for; matrix products, arithmetic and copies ran while one was open for 0% of the time, Pallas kernels for 5%

profile of v5, /device:TPU:1, one launch (start us, length us, event | category | flops | bytes accessed | tf_op | source)
XLA Modules:
  0.0 171.2 jit_solution(16216097013093893921)
XLA Ops:
  0.6 1.0 copy-done
  1.8 4.5 %collective-permute-start = (f32[128,512]{1,0:T(8,128)S(1)}, f32[128,512]{1,0:T(8,128)S(1)}, u32[]{:S(2)}, u32[]{:S(2)}) collective-permute-start(f32[128,512]{1,0:T(8,128)S(1)} %shard_map.41.own), channel_id=1, source_target_pairs={{1,2},{3,4},{5,6},{7,8},{9,10},{11,12},{13,14},{2,1},{4,3},{6,5},{... | collective-permute-start | bytes 786440 | tf_op jit(solution)/shard_map/ppermute | solution.py:70
  6.5 3.5 %collective-permute-start.2 = (f32[128,512]{1,0:T(8,128)S(1)}, f32[128,512]{1,0:T(8,128)S(1)}, u32[]{:S(2)}, u32[]{:S(2)}) collective-permute-start(f32[128,512]{1,0:T(8,128)S(1)} %shard_map.44.own), channel_id=1, source_target_pairs={{1,2},{3,4},{5,6},{7,8},{9,10},{11,12},{13,14},{2,1},{4,3},{6,5},{... | collective-permute-start | bytes 786440 | tf_op jit(solution)/shard_map/ppermute | solution.py:70
  10.1 0.4 shard_map.42
  10.5 0.5 shard_map.43
  11.1 1.4 collective-permute-start.4
  12.5 1.6 collective-permute-done.2.far
  14.2 0.5 shard_map.45.inner
  14.7 1.0 collective-permute-done.4.recv0
  15.7 1.3 shard_map.47
  17.0 4.4 %collective-permute-start.8 = (f32[192,512]{1,0:T(8,128)S(1)}, f32[192,512]{1,0:T(8,128)S(1)}, u32[]{:S(2)}, u32[]{:S(2)}) collective-permute-start(f32[192,512]{1,0:T(8,128)S(1)} %get-tuple-element.47.own.rest_0_), channel_id=1, source_target_pairs={{1,2},{3,4},{5,6},{7,8},{9,10},{11,12},{13,14},{2,1},{4,3},{6,5},{... | collective-permute-start | bytes 1179656 | tf_op jit(solution)/shard_map/ppermute | solution.py:70
  21.5 0.7 collective-permute-start.5
  22.2 0.5 shard_map.48.own.rest_0_
  22.7 3.5 %collective-permute-start.6 = (f32[64,512]{1,0:T(8,128)S(1)}, f32[64,512]{1,0:T(8,128)S(1)}, u32[]{:S(2)}, u32[]{:S(2)}) collective-permute-start(f32[64,512]{1,0:T(8,128)S(1)} %shard_map.48.own.rest_0_), channel_id=1, source_target_pairs={{1,2},{3,4},{5,6},{7,8},{9,10},{11,12},{13,14},{2,1},{4,3},{6,5},{... | collective-permute-start | bytes 393224 | tf_op jit(solution)/shard_map/ppermute | solution.py:70
  26.3 0.5 collective-permute-done.8.far
  26.8 0.7 shard_map.50
  27.5 7.5 %collective-permute-start.10 = (f32[64,512]{1,0:T(8,128)S(1)}, f32[64,512]{1,0:T(8,128)S(1)}, u32[]{:S(2)}, u32[]{:S(2)}) collective-permute-start(f32[64,512]{1,0:T(8,128)S(1)} %get-tuple-element.49.last), channel_id=1, source_target_pairs={{0,16},{32,48},{64,80},{96,112},{128,144},{160,176},{192,208},{224... | collective-permute-start | bytes 393224 | tf_op jit(solution)/shard_map/ppermute | solution.py:70
  35.4 3.1 %collective-permute-done.10.recv0 = f32[64,512]{1,0:T(8,128)S(1)} collective-permute-done((f32[64,512]{1,0:T(8,128)S(1)}, f32[64,512]{1,0:T(8,128)S(1)}, u32[]{:S(2)}, u32[]{:S(2)}) %collective-permute-start.10) | collective-permute-done | bytes 131104 | tf_op jit(solution)/shard_map/ppermute | solution.py:70
  38.4 0.4 shard_map.51
  38.9 4.7 %collective-permute-start.14 = (f32[192,512]{1,0:T(8,128)S(1)}, f32[192,512]{1,0:T(8,128)S(1)}, u32[]{:S(2)}, u32[]{:S(2)}) collective-permute-start(f32[192,512]{1,0:T(8,128)S(1)} %get-tuple-element.52.own), channel_id=1, source_target_pairs={{1,2},{3,4},{5,6},{7,8},{9,10},{11,12},{13,14},{2,1},{4,3},{6,5},{... | collective-permute-start | bytes 1179656 | tf_op jit(solution)/shard_map/ppermute | solution.py:70
  43.7 0.7 collective-permute-start.11
  44.6 4.4 %collective-permute-start.12 = (f32[64,512]{1,0:T(8,128)S(1)}, f32[64,512]{1,0:T(8,128)S(1)}, u32[]{:S(2)}, u32[]{:S(2)}) collective-permute-start(f32[64,512]{1,0:T(8,128)S(1)} %shard_map.52.own), channel_id=1, source_target_pairs={{1,2},{3,4},{5,6},{7,8},{9,10},{11,12},{13,14},{2,1},{4,3},{6,5},{... | collective-permute-start | bytes 393224 | tf_op jit(solution)/shard_map/ppermute | solution.py:70
  49.2 0.7 shard_map.54
  49.9 11.6 %collective-permute-start.16 = (f32[64,512]{1,0:T(8,128)S(1)}, f32[64,512]{1,0:T(8,128)S(1)}, u32[]{:S(2)}, u32[]{:S(2)}) collective-permute-start(f32[64,512]{1,0:T(8,128)S(1)} %get-tuple-element.54.last), channel_id=1, source_target_pairs={{0,16},{32,48},{64,80},{96,112},{128,144},{160,176},{192,208},{224... | collective-permute-start | bytes 393224 | tf_op jit(solution)/shard_map/ppermute | solution.py:70
  61.5 0.3 shard_map.53.first
  61.8 3.1 %collective-permute-done.16.recv0 = f32[64,512]{1,0:T(8,128)S(1)} collective-permute-done((f32[64,512]{1,0:T(8,128)S(1)}, f32[64,512]{1,0:T(8,128)S(1)}, u32[]{:S(2)}, u32[]{:S(2)}) %collective-permute-start.16) | collective-permute-done | bytes 131104 | tf_op jit(solution)/shard_map/ppermute | solution.py:70
  64.9 1.2 shard_map.55
  66.1 7.1 %collective-permute-start.20 = (f32[192,512]{1,0:T(8,128)S(1)}, f32[192,512]{1,0:T(8,128)S(1)}, u32[]{:S(2)}, u32[]{:S(2)}) collective-permute-start(f32[192,512]{1,0:T(8,128)S(1)} %get-tuple-element.56.own.rest_0_), channel_id=1, source_target_pairs={{1,2},{3,4},{5,6},{7,8},{9,10},{11,12},{13,14},{2,1},{4,3},{6,5},{... | collective-permute-start | bytes 1179656 | tf_op jit(solution)/shard_map/ppermute | solution.py:70
  73.3 0.7 collective-permute-start.17
  74.0 0.5 shard_map.56.own.rest_0_
  74.5 2.4 %collective-permute-start.18 = (f32[64,512]{1,0:T(8,128)S(1)}, f32[64,512]{1,0:T(8,128)S(1)}, u32[]{:S(2)}, u32[]{:S(2)}) collective-permute-start(f32[64,512]{1,0:T(8,128)S(1)} %shard_map.56.own.rest_0_), channel_id=1, source_target_pairs={{1,2},{3,4},{5,6},{7,8},{9,10},{11,12},{13,14},{2,1},{4,3},{6,5},{... | collective-permute-start | bytes 393224 | tf_op jit(solution)/shard_map/ppermute | solution.py:70
  77.0 1.7 collective-permute-done.20.far
  78.7 0.7 shard_map.58
  79.4 10.9 %collective-permute-start.22 = (f32[64,512]{1,0:T(8,128)S(1)}, f32[64,512]{1,0:T(8,128)S(1)}, u32[]{:S(2)}, u32[]{:S(2)}) collective-permute-start(f32[64,512]{1,0:T(8,128)S(1)} %get-tuple-element.58.last), channel_id=1, source_target_pairs={{0,16},{32,48},{64,80},{96,112},{128,144},{160,176},{192,208},{224... | collective-permute-start | bytes 393224 | tf_op jit(solution)/shard_map/ppermute | solution.py:70
  90.6 3.1 %collective-permute-done.22.recv0 = f32[64,512]{1,0:T(8,128)S(1)} collective-permute-done((f32[64,512]{1,0:T(8,128)S(1)}, f32[64,512]{1,0:T(8,128)S(1)}, u32[]{:S(2)}, u32[]{:S(2)}) %collective-permute-start.22) | collective-permute-done | bytes 131104 | tf_op jit(solution)/shard_map/ppermute | solution.py:70
  93.6 0.4 shard_map.59
  94.1 7.0 %collective-permute-start.26 = (f32[192,512]{1,0:T(8,128)S(1)}, f32[192,512]{1,0:T(8,128)S(1)}, u32[]{:S(2)}, u32[]{:S(2)}) collective-permute-start(f32[192,512]{1,0:T(8,128)S(1)} %get-tuple-element.60.own), channel_id=1, source_target_pairs={{1,2},{3,4},{5,6},{7,8},{9,10},{11,12},{13,14},{2,1},{4,3},{6,5},{... | collective-permute-start | bytes 1179656 | tf_op jit(solution)/shard_map/ppermute | solution.py:70
  101.2 0.7 collective-permute-start.23
  102.1 2.4 %collective-permute-start.24 = (f32[64,512]{1,0:T(8,128)S(1)}, f32[64,512]{1,0:T(8,128)S(1)}, u32[]{:S(2)}, u32[]{:S(2)}) collective-permute-start(f32[64,512]{1,0:T(8,128)S(1)} %shard_map.60.own), channel_id=1, source_target_pairs={{1,2},{3,4},{5,6},{7,8},{9,10},{11,12},{13,14},{2,1},{4,3},{6,5},{... | collective-permute-start | bytes 393224 | tf_op jit(solution)/shard_map/ppermute | solution.py:70
  104.6 2.0 %collective-permute-done.26.far = f32[192,512]{1,0:T(8,128)S(1)} collective-permute-done((f32[192,512]{1,0:T(8,128)S(1)}, f32[192,512]{1,0:T(8,128)S(1)}, u32[]{:S(2)}, u32[]{:S(2)}) %collective-permute-start.26) | collective-permute-done | bytes 393248 | tf_op jit(solution)/shard_map/ppermute | solution.py:70
  106.5 0.7 shard_map.62
  107.2 10.6 %collective-permute-start.28 = (f32[64,512]{1,0:T(8,128)S(1)}, f32[64,512]{1,0:T(8,128)S(1)}, u32[]{:S(2)}, u32[]{:S(2)}) collective-permute-start(f32[64,512]{1,0:T(8,128)S(1)} %get-tuple-element.62.last), channel_id=1, source_target_pairs={{0,16},{32,48},{64,80},{96,112},{128,144},{160,176},{192,208},{224... | collective-permute-start | bytes 393224 | tf_op jit(solution)/shard_map/ppermute | solution.py:70
  118.2 0.7 collective-permute-start.29
  118.9 2.4 %collective-permute-done.28.recv0 = f32[64,512]{1,0:T(8,128)S(1)} collective-permute-done((f32[64,512]{1,0:T(8,128)S(1)}, f32[64,512]{1,0:T(8,128)S(1)}, u32[]{:S(2)}, u32[]{:S(2)}) %collective-permute-start.28) | collective-permute-done | bytes 131104 | tf_op jit(solution)/shard_map/ppermute | solution.py:70
  121.3 1.2 shard_map.63
  122.5 0.5 shard_map.64
  123.2 47.0 %all_to_all.5 = f32[256,1,256]{2,1,0:T(1,128)S(1)} all-to-all(f32[256,1,256]{2,1,0:T(1,128)S(1)} %broadcast_in_dim.9), channel_id=1, replica_groups=mesh['gx'=16,'gz'=16] {'gx','gz'}, dimensions={0} | all-to-all | bytes 524288 | tf_op jit(solution)/shard_map/all_to_all | solution.py:319
  170.2 1.0 shard_map.65
  (46 shorter events, 2.8 us)
Async XLA Ops:
  0.6 1.0 copy-start
  1.8 8.7 %collective-permute-start = (f32[128,512]{1,0:T(8,128)S(1)}, f32[128,512]{1,0:T(8,128)S(1)}, u32[]{:S(2)}, u32[]{:S(2)}) collective-permute-start(f32[128,512]{1,0:T(8,128)S(1)} %shard_map.41.own), channel_id=1, source_target_pairs={{1,2},{3,4},{5,6},{7,8},{9,10},{11,12},{13,14},{2,1},{4,3},{6,5},{... | collective-permute-start | bytes 786440 | tf_op jit(solution)/shard_map/ppermute | solution.py:70
  6.3 4.2 %collective-permute-start.1 = (f32[128,512]{1,0:T(8,128)S(1)}, f32[128,512]{1,0:T(8,128)S(1)}, u32[]{:S(2)}, u32[]{:S(2)}) collective-permute-start(f32[128,512]{1,0:T(8,128)S(1)} %shard_map.41.own), channel_id=1, source_target_pairs={{0,1},{2,3},{4,5},{6,7},{8,9},{10,11},{12,13},{14,15},{1,0},{3,2},... | collective-permute-start | bytes 786440 | tf_op jit(solution)/shard_map/ppermute | solution.py:70
  6.5 7.7 %collective-permute-start.2 = (f32[128,512]{1,0:T(8,128)S(1)}, f32[128,512]{1,0:T(8,128)S(1)}, u32[]{:S(2)}, u32[]{:S(2)}) collective-permute-start(f32[128,512]{1,0:T(8,128)S(1)} %shard_map.44.own), channel_id=1, source_target_pairs={{1,2},{3,4},{5,6},{7,8},{9,10},{11,12},{13,14},{2,1},{4,3},{6,5},{... | collective-permute-start | bytes 786440 | tf_op jit(solution)/shard_map/ppermute | solution.py:70
  10.0 4.2 %collective-permute-start.3 = (f32[128,512]{1,0:T(8,128)S(1)}, f32[128,512]{1,0:T(8,128)S(1)}, u32[]{:S(2)}, u32[]{:S(2)}) collective-permute-start(f32[128,512]{1,0:T(8,128)S(1)} %shard_map.44.own), channel_id=1, source_target_pairs={{0,1},{2,3},{4,5},{6,7},{8,9},{10,11},{12,13},{14,15},{1,0},{3,2},... | collective-permute-start | bytes 786440 | tf_op jit(solution)/shard_map/ppermute | solution.py:70
  10.5 1.9 %copy-start.1 = (f32[8,32,512]{2,1,0:T(8,128)S(1)}, f32[8,32,512]{2,1,0:T(8,128)}, u32[]{:S(2)}) copy-start(f32[8,32,512]{2,1,0:T(8,128)} %rho_prev.5) | copy-start | bytes 1572868
  10.5 1.9 %copy-start.2 = (f32[8,32,512]{2,1,0:T(8,128)S(1)}, f32[8,32,512]{2,1,0:T(8,128)}, u32[]{:S(2)}) copy-start(f32[8,32,512]{2,1,0:T(8,128)} %potential.1) | copy-start | bytes 1572868
  11.1 4.7 %collective-permute-start.4 = (f32[64,512]{1,0:T(8,128)S(1)}, f32[64,512]{1,0:T(8,128)S(1)}, u32[]{:S(2)}, u32[]{:S(2)}) collective-permute-start(f32[64,512]{1,0:T(8,128)S(1)} %get-tuple-element.41.last), channel_id=1, source_target_pairs={{0,16},{32,48},{64,80},{96,112},{128,144},{160,176},{192,208},{224... | collective-permute-start | bytes 393224 | tf_op jit(solution)/shard_map/ppermute | solution.py:70
  17.0 9.8 %collective-permute-start.8 = (f32[192,512]{1,0:T(8,128)S(1)}, f32[192,512]{1,0:T(8,128)S(1)}, u32[]{:S(2)}, u32[]{:S(2)}) collective-permute-start(f32[192,512]{1,0:T(8,128)S(1)} %get-tuple-element.47.own.rest_0_), channel_id=1, source_target_pairs={{1,2},{3,4},{5,6},{7,8},{9,10},{11,12},{13,14},{2,1},{4,3},{6,5},{... | collective-permute-start | bytes 1179656 | tf_op jit(solution)/shard_map/ppermute | solution.py:70
  21.4 5.4 %collective-permute-start.9 = (f32[192,512]{1,0:T(8,128)S(1)}, f32[192,512]{1,0:T(8,128)S(1)}, u32[]{:S(2)}, u32[]{:S(2)}) collective-permute-start(f32[192,512]{1,0:T(8,128)S(1)} %get-tuple-element.47.own.rest_0_), channel_id=1, source_target_pairs={{0,1},{2,3},{4,5},{6,7},{8,9},{10,11},{12,13},{14,15},{1,0},{3,2},... | collective-permute-start | bytes 1179656 | tf_op jit(solution)/shard_map/ppermute | solution.py:70
  21.5 0.7 collective-permute-start.5
  22.7 12.4 %collective-permute-start.6 = (f32[64,512]{1,0:T(8,128)S(1)}, f32[64,512]{1,0:T(8,128)S(1)}, u32[]{:S(2)}, u32[]{:S(2)}) collective-permute-start(f32[64,512]{1,0:T(8,128)S(1)} %shard_map.48.own.rest_0_), channel_id=1, source_target_pairs={{1,2},{3,4},{5,6},{7,8},{9,10},{11,12},{13,14},{2,1},{4,3},{6,5},{... | collective-permute-start | bytes 393224 | tf_op jit(solution)/shard_map/ppermute | solution.py:70
  26.2 8.9 %collective-permute-start.7 = (f32[64,512]{1,0:T(8,128)S(1)}, f32[64,512]{1,0:T(8,128)S(1)}, u32[]{:S(2)}, u32[]{:S(2)}) collective-permute-start(f32[64,512]{1,0:T(8,128)S(1)} %shard_map.48.own.rest_0_), channel_id=1, source_target_pairs={{0,1},{2,3},{4,5},{6,7},{8,9},{10,11},{12,13},{14,15},{1,0},{3,2},... | collective-permute-start | bytes 393224 | tf_op jit(solution)/shard_map/ppermute | solution.py:70
  27.5 10.9 %collective-permute-start.10 = (f32[64,512]{1,0:T(8,128)S(1)}, f32[64,512]{1,0:T(8,128)S(1)}, u32[]{:S(2)}, u32[]{:S(2)}) collective-permute-start(f32[64,512]{1,0:T(8,128)S(1)} %get-tuple-element.49.last), channel_id=1, source_target_pairs={{0,16},{32,48},{64,80},{96,112},{128,144},{160,176},{192,208},{224... | collective-permute-start | bytes 393224 | tf_op jit(solution)/shard_map/ppermute | solution.py:70
  38.9 10.3 %collective-permute-start.14 = (f32[192,512]{1,0:T(8,128)S(1)}, f32[192,512]{1,0:T(8,128)S(1)}, u32[]{:S(2)}, u32[]{:S(2)}) collective-permute-start(f32[192,512]{1,0:T(8,128)S(1)} %get-tuple-element.52.own), channel_id=1, source_target_pairs={{1,2},{3,4},{5,6},{7,8},{9,10},{11,12},{13,14},{2,1},{4,3},{6,5},{... | collective-permute-start | bytes 1179656 | tf_op jit(solution)/shard_map/ppermute | solution.py:70
  43.6 5.5 %collective-permute-start.15 = (f32[192,512]{1,0:T(8,128)S(1)}, f32[192,512]{1,0:T(8,128)S(1)}, u32[]{:S(2)}, u32[]{:S(2)}) collective-permute-start(f32[192,512]{1,0:T(8,128)S(1)} %get-tuple-element.52.own), channel_id=1, source_target_pairs={{0,1},{2,3},{4,5},{6,7},{8,9},{10,11},{12,13},{14,15},{1,0},{3,2},... | collective-permute-start | bytes 1179656 | tf_op jit(solution)/shard_map/ppermute | solution.py:70
  43.7 0.7 collective-permute-start.11
  44.6 16.8 %collective-permute-start.12 = (f32[64,512]{1,0:T(8,128)S(1)}, f32[64,512]{1,0:T(8,128)S(1)}, u32[]{:S(2)}, u32[]{:S(2)}) collective-permute-start(f32[64,512]{1,0:T(8,128)S(1)} %shard_map.52.own), channel_id=1, source_target_pairs={{1,2},{3,4},{5,6},{7,8},{9,10},{11,12},{13,14},{2,1},{4,3},{6,5},{... | collective-permute-start | bytes 393224 | tf_op jit(solution)/shard_map/ppermute | solution.py:70
  49.0 12.4 %collective-permute-start.13 = (f32[64,512]{1,0:T(8,128)S(1)}, f32[64,512]{1,0:T(8,128)S(1)}, u32[]{:S(2)}, u32[]{:S(2)}) collective-permute-start(f32[64,512]{1,0:T(8,128)S(1)} %shard_map.52.own), channel_id=1, source_target_pairs={{0,1},{2,3},{4,5},{6,7},{8,9},{10,11},{12,13},{14,15},{1,0},{3,2},... | collective-permute-start | bytes 393224 | tf_op jit(solution)/shard_map/ppermute | solution.py:70
  49.9 15.0 %collective-permute-start.16 = (f32[64,512]{1,0:T(8,128)S(1)}, f32[64,512]{1,0:T(8,128)S(1)}, u32[]{:S(2)}, u32[]{:S(2)}) collective-permute-start(f32[64,512]{1,0:T(8,128)S(1)} %get-tuple-element.54.last), channel_id=1, source_target_pairs={{0,16},{32,48},{64,80},{96,112},{128,144},{160,176},{192,208},{224... | collective-permute-start | bytes 393224 | tf_op jit(solution)/shard_map/ppermute | solution.py:70
  66.1 12.5 %collective-permute-start.20 = (f32[192,512]{1,0:T(8,128)S(1)}, f32[192,512]{1,0:T(8,128)S(1)}, u32[]{:S(2)}, u32[]{:S(2)}) collective-permute-start(f32[192,512]{1,0:T(8,128)S(1)} %get-tuple-element.56.own.rest_0_), channel_id=1, source_target_pairs={{1,2},{3,4},{5,6},{7,8},{9,10},{11,12},{13,14},{2,1},{4,3},{6,5},{... | collective-permute-start | bytes 1179656 | tf_op jit(solution)/shard_map/ppermute | solution.py:70
  73.2 5.4 %collective-permute-start.21 = (f32[192,512]{1,0:T(8,128)S(1)}, f32[192,512]{1,0:T(8,128)S(1)}, u32[]{:S(2)}, u32[]{:S(2)}) collective-permute-start(f32[192,512]{1,0:T(8,128)S(1)} %get-tuple-element.56.own.rest_0_), channel_id=1, source_target_pairs={{0,1},{2,3},{4,5},{6,7},{8,9},{10,11},{12,13},{14,15},{1,0},{3,2},... | collective-permute-start | bytes 1179656 | tf_op jit(solution)/shard_map/ppermute | solution.py:70
  73.3 0.7 collective-permute-start.17
  74.5 15.7 %collective-permute-start.18 = (f32[64,512]{1,0:T(8,128)S(1)}, f32[64,512]{1,0:T(8,128)S(1)}, u32[]{:S(2)}, u32[]{:S(2)}) collective-permute-start(f32[64,512]{1,0:T(8,128)S(1)} %shard_map.56.own.rest_0_), channel_id=1, source_target_pairs={{1,2},{3,4},{5,6},{7,8},{9,10},{11,12},{13,14},{2,1},{4,3},{6,5},{... | collective-permute-start | bytes 393224 | tf_op jit(solution)/shard_map/ppermute | solution.py:70
  76.9 13.4 %collective-permute-start.19 = (f32[64,512]{1,0:T(8,128)S(1)}, f32[64,512]{1,0:T(8,128)S(1)}, u32[]{:S(2)}, u32[]{:S(2)}) collective-permute-start(f32[64,512]{1,0:T(8,128)S(1)} %shard_map.56.own.rest_0_), channel_id=1, source_target_pairs={{0,1},{2,3},{4,5},{6,7},{8,9},{10,11},{12,13},{14,15},{1,0},{3,2},... | collective-permute-start | bytes 393224 | tf_op jit(solution)/shard_map/ppermute | solution.py:70
  79.4 14.3 %collective-permute-start.22 = (f32[64,512]{1,0:T(8,128)S(1)}, f32[64,512]{1,0:T(8,128)S(1)}, u32[]{:S(2)}, u32[]{:S(2)}) collective-permute-start(f32[64,512]{1,0:T(8,128)S(1)} %get-tuple-element.58.last), channel_id=1, source_target_pairs={{0,16},{32,48},{64,80},{96,112},{128,144},{160,176},{192,208},{224... | collective-permute-start | bytes 393224 | tf_op jit(solution)/shard_map/ppermute | solution.py:70
  94.1 12.4 %collective-permute-start.26 = (f32[192,512]{1,0:T(8,128)S(1)}, f32[192,512]{1,0:T(8,128)S(1)}, u32[]{:S(2)}, u32[]{:S(2)}) collective-permute-start(f32[192,512]{1,0:T(8,128)S(1)} %get-tuple-element.60.own), channel_id=1, source_target_pairs={{1,2},{3,4},{5,6},{7,8},{9,10},{11,12},{13,14},{2,1},{4,3},{6,5},{... | collective-permute-start | bytes 1179656 | tf_op jit(solution)/shard_map/ppermute | solution.py:70
  101.1 5.4 %collective-permute-start.27 = (f32[192,512]{1,0:T(8,128)S(1)}, f32[192,512]{1,0:T(8,128)S(1)}, u32[]{:S(2)}, u32[]{:S(2)}) collective-permute-start(f32[192,512]{1,0:T(8,128)S(1)} %get-tuple-element.60.own), channel_id=1, source_target_pairs={{0,1},{2,3},{4,5},{6,7},{8,9},{10,11},{12,13},{14,15},{1,0},{3,2},... | collective-permute-start | bytes 1179656 | tf_op jit(solution)/shard_map/ppermute | solution.py:70
  101.2 0.7 collective-permute-start.23
  102.1 15.8 %collective-permute-start.24 = (f32[64,512]{1,0:T(8,128)S(1)}, f32[64,512]{1,0:T(8,128)S(1)}, u32[]{:S(2)}, u32[]{:S(2)}) collective-permute-start(f32[64,512]{1,0:T(8,128)S(1)} %shard_map.60.own), channel_id=1, source_target_pairs={{1,2},{3,4},{5,6},{7,8},{9,10},{11,12},{13,14},{2,1},{4,3},{6,5},{... | collective-permute-start | bytes 393224 | tf_op jit(solution)/shard_map/ppermute | solution.py:70
  104.5 13.4 %collective-permute-start.25 = (f32[64,512]{1,0:T(8,128)S(1)}, f32[64,512]{1,0:T(8,128)S(1)}, u32[]{:S(2)}, u32[]{:S(2)}) collective-permute-start(f32[64,512]{1,0:T(8,128)S(1)} %shard_map.60.own), channel_id=1, source_target_pairs={{0,1},{2,3},{4,5},{6,7},{8,9},{10,11},{12,13},{14,15},{1,0},{3,2},... | collective-permute-start | bytes 393224 | tf_op jit(solution)/shard_map/ppermute | solution.py:70
  107.2 14.0 %collective-permute-start.28 = (f32[64,512]{1,0:T(8,128)S(1)}, f32[64,512]{1,0:T(8,128)S(1)}, u32[]{:S(2)}, u32[]{:S(2)}) collective-permute-start(f32[64,512]{1,0:T(8,128)S(1)} %get-tuple-element.62.last), channel_id=1, source_target_pairs={{0,16},{32,48},{64,80},{96,112},{128,144},{160,176},{192,208},{224... | collective-permute-start | bytes 393224 | tf_op jit(solution)/shard_map/ppermute | solution.py:70
  118.2 4.3 %collective-permute-start.29 = (f32[64,512]{1,0:T(8,128)S(1)}, f32[64,512]{1,0:T(8,128)S(1)}, u32[]{:S(2)}, u32[]{:S(2)}) collective-permute-start(f32[64,512]{1,0:T(8,128)S(1)} %shard_map.61.first), channel_id=1, source_target_pairs={{16,32},{48,64},{80,96},{112,128},{144,160},{176,192},{208,224},{3... | collective-permute-start | bytes 393224 | tf_op jit(solution)/shard_map/ppermute | solution.py:70

commit v6 on v5

--- a/solution.py
+++ b/solution.py
@@ -68,6 +68,12 @@
     size = lax.axis_size(axis)
     pairs = [(i, i + 1) for i in range(first, size - 1, 2)]
     return lax.ppermute(value, axis, pairs + [(j, i) for i, j in pairs])
+
+
+def gather_pairs(value, axis):
+    size = lax.axis_size(axis)
+    pairs = [[i, (i + 1) % size] for i in range(1, size, 2)]
+    return lax.all_gather(value, axis, axis_index_groups=pairs, tiled=True)
 
 
 def cells(at):
@@ -142,11 +148,17 @@
     length = own.shape[1]
     rows = depth * HALF
     near_after = even("gz")
+    paired = far.shape[0] > own.shape[0]
+    at_z = lax.axis_index("gz")
+    inside = (at_z > 0) & (at_z < lax.axis_size("gz") - 1)
     for start in range(0, own.shape[0], rows):
         span = slice(start, start + rows)
         for at in range(0, length, LANES):
             lanes = slice(at, at + LANES)
             far_part, near_part = far[span, lanes], near[span, lanes]
+            if paired:
+                other = far[start + own.shape[0] : start + own.shape[0] + rows, lanes]
+                far_part = jnp.where(inside, jnp.where(near_after, far_part, other), 0.0)
             before = jnp.where(near_after, far_part, near_part)
             after = jnp.where(near_after, near_part, far_part)
             line = [part[z * HALF : (z + 1) * HALF] for part in (before, own[span, lanes], after) for z in range(depth)]
@@ -277,8 +289,8 @@
 
     def heat_step(turn, kind, first, rest, whole, scaling):
         started, last = scaling is not None, kind == "last"
-        far = swap(first, "gz", 1)
         near = swap(first, "gz", 0)
+        far = gather_pairs(first, "gz") if last else swap(first, "gz", 1)
         far_rest = swap(rest, "gz", 1)
         near_rest = swap(rest, "gz", 0)
         kernel, shapes = (zy_one_kernel, [one]) if turn else (zy_two_kernel, [one, one])

time: 172 us -> 172 us (level)
  blocking collectives: 47 us -> 50.8 us
  waiting for transfers between devices: 18.4 us -> 15.4 us
    all_gather x0 -> x1, blocking collectives: none -> 5.58 us  [gather_pairs(): return lax.all_gather(value, axis, axis_index_groups=pairs, tiled=True)]
    ppermute x30 -> x29, waiting for transfers between devices: 18.4 us -> 15.4 us  [swap(): return lax.ppermute(value, axis, pairs + [(j, i) for i, j in pairs])]
    all_to_all x1, blocking collectives: 47 us -> 45.2 us  [step(): lax.all_to_all(sums, ('gx', 'gz'), 0, 0, tiled=True)]
    ppermute x30 -> x29, starting transfers between devices: 90.1 us -> 89.9 us  [swap(): return lax.ppermute(value, axis, pairs + [(j, i) for i, j in pairs])]
  transfers between devices with their start and end apart: 30 -> 29, of which waited for: 9 -> 8; matrix products, arithmetic and copies ran while one was open for 0% -> 0% of each run, Pallas kernels for 5% -> 5%
where the time goes in v6:
time: 172 us
  starting transfers between devices  89.9 us (52%)
  blocking collectives  50.8 us (30%)
  waiting for transfers between devices  15.4 us (9%)
  Pallas kernels  13.4 us (8%)
    ppermute x29, starting transfers between devices, swap(): return lax.ppermute(value, axis, pairs + [(j, i) for i, j in pairs])  89.9 us
    all_to_all x1, blocking collectives, step(): lax.all_to_all(sums, ('gx', 'gz'), 0, 0, tiled=True)  45.2 us
    ppermute x29, waiting for transfers between devices, swap(): return lax.ppermute(value, axis, pairs + [(j, i) for i, j in pairs])  15.4 us
    pallas_call x25, Pallas kernels, call(): pl.pallas_call(kernel, out_shape=[jax.ShapeDtypeStruct(shape, dtype) for...  13.4 us
    all_gather x1, blocking collectives, gather_pairs(): return lax.all_gather(value, axis, axis_index_groups=pairs, tiled=True)  5.58 us
  transfers between devices with their start and end apart: 29, of which 8 were waited for; matrix products, arithmetic and copies ran while one was open for 0% of the time, Pallas kernels for 5%

profile of v6, /device:TPU:1, one launch (start us, length us, event | category | flops | bytes accessed | tf_op | source)
XLA Modules:
  0.0 171.8 jit_solution(15987868314707808399)
XLA Ops:
  0.6 1.0 copy-done
  1.8 4.5 %collective-permute-start = (f32[128,512]{1,0:T(8,128)S(1)}, f32[128,512]{1,0:T(8,128)S(1)}, u32[]{:S(2)}, u32[]{:S(2)}) collective-permute-start(f32[128,512]{1,0:T(8,128)S(1)} %shard_map.41.own), channel_id=1, source_target_pairs={{1,2},{3,4},{5,6},{7,8},{9,10},{11,12},{13,14},{2,1},{4,3},{6,5},{... | collective-permute-start | bytes 786440 | tf_op jit(solution)/shard_map/ppermute | solution.py:70
  6.5 3.5 %collective-permute-start.2 = (f32[128,512]{1,0:T(8,128)S(1)}, f32[128,512]{1,0:T(8,128)S(1)}, u32[]{:S(2)}, u32[]{:S(2)}) collective-permute-start(f32[128,512]{1,0:T(8,128)S(1)} %shard_map.44.own), channel_id=1, source_target_pairs={{1,2},{3,4},{5,6},{7,8},{9,10},{11,12},{13,14},{2,1},{4,3},{6,5},{... | collective-permute-start | bytes 786440 | tf_op jit(solution)/shard_map/ppermute | solution.py:70
  10.1 0.4 shard_map.42
  10.5 0.5 shard_map.43
  11.1 1.4 collective-permute-start.4
  12.5 1.6 collective-permute-done.2.far
  14.2 0.5 shard_map.45.inner
  14.7 1.0 collective-permute-done.4.recv0
  15.7 1.3 shard_map.47
  17.0 4.4 %collective-permute-start.8 = (f32[192,512]{1,0:T(8,128)S(1)}, f32[192,512]{1,0:T(8,128)S(1)}, u32[]{:S(2)}, u32[]{:S(2)}) collective-permute-start(f32[192,512]{1,0:T(8,128)S(1)} %get-tuple-element.47.own.rest_0_), channel_id=1, source_target_pairs={{1,2},{3,4},{5,6},{7,8},{9,10},{11,12},{13,14},{2,1},{4,3},{6,5},{... | collective-permute-start | bytes 1179656 | tf_op jit(solution)/shard_map/ppermute | solution.py:70
  21.5 0.7 collective-permute-start.5
  22.2 0.5 shard_map.48.own.rest_0_
  22.7 3.5 %collective-permute-start.6 = (f32[64,512]{1,0:T(8,128)S(1)}, f32[64,512]{1,0:T(8,128)S(1)}, u32[]{:S(2)}, u32[]{:S(2)}) collective-permute-start(f32[64,512]{1,0:T(8,128)S(1)} %shard_map.48.own.rest_0_), channel_id=1, source_target_pairs={{1,2},{3,4},{5,6},{7,8},{9,10},{11,12},{13,14},{2,1},{4,3},{6,5},{... | collective-permute-start | bytes 393224 | tf_op jit(solution)/shard_map/ppermute | solution.py:70
  26.3 0.5 collective-permute-done.8.far
  26.8 0.7 shard_map.50
  27.5 7.5 %collective-permute-start.10 = (f32[64,512]{1,0:T(8,128)S(1)}, f32[64,512]{1,0:T(8,128)S(1)}, u32[]{:S(2)}, u32[]{:S(2)}) collective-permute-start(f32[64,512]{1,0:T(8,128)S(1)} %get-tuple-element.49.last), channel_id=1, source_target_pairs={{0,16},{32,48},{64,80},{96,112},{128,144},{160,176},{192,208},{224... | collective-permute-start | bytes 393224 | tf_op jit(solution)/shard_map/ppermute | solution.py:70
  35.4 3.1 %collective-permute-done.10.recv0 = f32[64,512]{1,0:T(8,128)S(1)} collective-permute-done((f32[64,512]{1,0:T(8,128)S(1)}, f32[64,512]{1,0:T(8,128)S(1)}, u32[]{:S(2)}, u32[]{:S(2)}) %collective-permute-start.10) | collective-permute-done | bytes 131104 | tf_op jit(solution)/shard_map/ppermute | solution.py:70
  38.4 0.4 shard_map.51
  38.9 4.7 %collective-permute-start.14 = (f32[192,512]{1,0:T(8,128)S(1)}, f32[192,512]{1,0:T(8,128)S(1)}, u32[]{:S(2)}, u32[]{:S(2)}) collective-permute-start(f32[192,512]{1,0:T(8,128)S(1)} %get-tuple-element.52.own), channel_id=1, source_target_pairs={{1,2},{3,4},{5,6},{7,8},{9,10},{11,12},{13,14},{2,1},{4,3},{6,5},{... | collective-permute-start | bytes 1179656 | tf_op jit(solution)/shard_map/ppermute | solution.py:70
  43.7 0.7 collective-permute-start.11
  44.6 4.4 %collective-permute-start.12 = (f32[64,512]{1,0:T(8,128)S(1)}, f32[64,512]{1,0:T(8,128)S(1)}, u32[]{:S(2)}, u32[]{:S(2)}) collective-permute-start(f32[64,512]{1,0:T(8,128)S(1)} %shard_map.52.own), channel_id=1, source_target_pairs={{1,2},{3,4},{5,6},{7,8},{9,10},{11,12},{13,14},{2,1},{4,3},{6,5},{... | collective-permute-start | bytes 393224 | tf_op jit(solution)/shard_map/ppermute | solution.py:70
  49.2 0.7 shard_map.54
  49.9 11.6 %collective-permute-start.16 = (f32[64,512]{1,0:T(8,128)S(1)}, f32[64,512]{1,0:T(8,128)S(1)}, u32[]{:S(2)}, u32[]{:S(2)}) collective-permute-start(f32[64,512]{1,0:T(8,128)S(1)} %get-tuple-element.54.last), channel_id=1, source_target_pairs={{0,16},{32,48},{64,80},{96,112},{128,144},{160,176},{192,208},{224... | collective-permute-start | bytes 393224 | tf_op jit(solution)/shard_map/ppermute | solution.py:70
  61.8 3.1 %collective-permute-done.16.recv0 = f32[64,512]{1,0:T(8,128)S(1)} collective-permute-done((f32[64,512]{1,0:T(8,128)S(1)}, f32[64,512]{1,0:T(8,128)S(1)}, u32[]{:S(2)}, u32[]{:S(2)}) %collective-permute-start.16) | collective-permute-done | bytes 131104 | tf_op jit(solution)/shard_map/ppermute | solution.py:70
  64.9 1.2 shard_map.55
  66.1 7.1 %collective-permute-start.20 = (f32[192,512]{1,0:T(8,128)S(1)}, f32[192,512]{1,0:T(8,128)S(1)}, u32[]{:S(2)}, u32[]{:S(2)}) collective-permute-start(f32[192,512]{1,0:T(8,128)S(1)} %get-tuple-element.56.own.rest_0_), channel_id=1, source_target_pairs={{1,2},{3,4},{5,6},{7,8},{9,10},{11,12},{13,14},{2,1},{4,3},{6,5},{... | collective-permute-start | bytes 1179656 | tf_op jit(solution)/shard_map/ppermute | solution.py:70
  73.3 0.7 collective-permute-start.17
  74.0 0.5 shard_map.56.own.rest_0_
  74.5 2.4 %collective-permute-start.18 = (f32[64,512]{1,0:T(8,128)S(1)}, f32[64,512]{1,0:T(8,128)S(1)}, u32[]{:S(2)}, u32[]{:S(2)}) collective-permute-start(f32[64,512]{1,0:T(8,128)S(1)} %shard_map.56.own.rest_0_), channel_id=1, source_target_pairs={{1,2},{3,4},{5,6},{7,8},{9,10},{11,12},{13,14},{2,1},{4,3},{6,5},{... | collective-permute-start | bytes 393224 | tf_op jit(solution)/shard_map/ppermute | solution.py:70
  77.0 1.6 collective-permute-done.20.far
  78.7 0.7 shard_map.58
  79.4 10.9 %collective-permute-start.22 = (f32[64,512]{1,0:T(8,128)S(1)}, f32[64,512]{1,0:T(8,128)S(1)}, u32[]{:S(2)}, u32[]{:S(2)}) collective-permute-start(f32[64,512]{1,0:T(8,128)S(1)} %get-tuple-element.58.last), channel_id=1, source_target_pairs={{0,16},{32,48},{64,80},{96,112},{128,144},{160,176},{192,208},{224... | collective-permute-start | bytes 393224 | tf_op jit(solution)/shard_map/ppermute | solution.py:70
  90.6 3.1 %collective-permute-done.22.recv0 = f32[64,512]{1,0:T(8,128)S(1)} collective-permute-done((f32[64,512]{1,0:T(8,128)S(1)}, f32[64,512]{1,0:T(8,128)S(1)}, u32[]{:S(2)}, u32[]{:S(2)}) %collective-permute-start.22) | collective-permute-done | bytes 131104 | tf_op jit(solution)/shard_map/ppermute | solution.py:70
  93.6 0.4 shard_map.59
  94.1 7.0 %collective-permute-start.25 = (f32[192,512]{1,0:T(8,128)S(1)}, f32[192,512]{1,0:T(8,128)S(1)}, u32[]{:S(2)}, u32[]{:S(2)}) collective-permute-start(f32[192,512]{1,0:T(8,128)S(1)} %get-tuple-element.60.own), channel_id=1, source_target_pairs={{1,2},{3,4},{5,6},{7,8},{9,10},{11,12},{13,14},{2,1},{4,3},{6,5},{... | collective-permute-start | bytes 1179656 | tf_op jit(solution)/shard_map/ppermute | solution.py:70
  101.2 0.7 collective-permute-start.23
  102.1 0.6 collective-permute-start.24
  102.6 5.6 %all_gather.3.far = f32[128,512]{1,0:T(8,128)S(1)} all-gather(f32[64,512]{1,0:T(8,128)S(1)} %shard_map.60.own), channel_id=1, replica_groups={{1,2},{3,4},{5,6},{7,8},{9,10},{11,12},{13,14},{15,0},{17,18},{19,20},{..., dimensions={0}, use_global_device_ids=true | all-gather | bytes 393216 | tf_op jit(solution)/shard_map/all_gather | solution.py:76
  108.2 0.7 shard_map.62
  108.9 12.4 %collective-permute-start.27 = (f32[64,512]{1,0:T(8,128)S(1)}, f32[64,512]{1,0:T(8,128)S(1)}, u32[]{:S(2)}, u32[]{:S(2)}) collective-permute-start(f32[64,512]{1,0:T(8,128)S(1)} %get-tuple-element.62.last), channel_id=1, source_target_pairs={{0,16},{32,48},{64,80},{96,112},{128,144},{160,176},{192,208},{224... | collective-permute-start | bytes 393224 | tf_op jit(solution)/shard_map/ppermute | solution.py:70
  121.3 0.3 shard_map.61.first
  121.6 0.7 collective-permute-start.28
  122.3 1.3 collective-permute-done.27.recv0
  123.7 1.2 shard_map.63
  124.9 0.5 shard_map.64
  125.6 45.2 %all_to_all.5 = f32[256,1,256]{2,1,0:T(1,128)S(1)} all-to-all(f32[256,1,256]{2,1,0:T(1,128)S(1)} %broadcast_in_dim.9), channel_id=1, replica_groups=mesh['gx'=16,'gz'=16] {'gx','gz'}, dimensions={0} | all-to-all | bytes 524288 | tf_op jit(solution)/shard_map/all_to_all | solution.py:331
  170.8 1.0 shard_map.65
  (45 shorter events, 2.7 us)
Async XLA Ops:
  0.6 1.0 copy-start
  1.8 8.7 %collective-permute-start = (f32[128,512]{1,0:T(8,128)S(1)}, f32[128,512]{1,0:T(8,128)S(1)}, u32[]{:S(2)}, u32[]{:S(2)}) collective-permute-start(f32[128,512]{1,0:T(8,128)S(1)} %shard_map.41.own), channel_id=1, source_target_pairs={{1,2},{3,4},{5,6},{7,8},{9,10},{11,12},{13,14},{2,1},{4,3},{6,5},{... | collective-permute-start | bytes 786440 | tf_op jit(solution)/shard_map/ppermute | solution.py:70
  6.3 4.2 %collective-permute-start.1 = (f32[128,512]{1,0:T(8,128)S(1)}, f32[128,512]{1,0:T(8,128)S(1)}, u32[]{:S(2)}, u32[]{:S(2)}) collective-permute-start(f32[128,512]{1,0:T(8,128)S(1)} %shard_map.41.own), channel_id=1, source_target_pairs={{0,1},{2,3},{4,5},{6,7},{8,9},{10,11},{12,13},{14,15},{1,0},{3,2},... | collective-permute-start | bytes 786440 | tf_op jit(solution)/shard_map/ppermute | solution.py:70
  6.5 7.7 %collective-permute-start.2 = (f32[128,512]{1,0:T(8,128)S(1)}, f32[128,512]{1,0:T(8,128)S(1)}, u32[]{:S(2)}, u32[]{:S(2)}) collective-permute-start(f32[128,512]{1,0:T(8,128)S(1)} %shard_map.44.own), channel_id=1, source_target_pairs={{1,2},{3,4},{5,6},{7,8},{9,10},{11,12},{13,14},{2,1},{4,3},{6,5},{... | collective-permute-start | bytes 786440 | tf_op jit(solution)/shard_map/ppermute | solution.py:70
  10.0 4.2 %collective-permute-start.3 = (f32[128,512]{1,0:T(8,128)S(1)}, f32[128,512]{1,0:T(8,128)S(1)}, u32[]{:S(2)}, u32[]{:S(2)}) collective-permute-start(f32[128,512]{1,0:T(8,128)S(1)} %shard_map.44.own), channel_id=1, source_target_pairs={{0,1},{2,3},{4,5},{6,7},{8,9},{10,11},{12,13},{14,15},{1,0},{3,2},... | collective-permute-start | bytes 786440 | tf_op jit(solution)/shard_map/ppermute | solution.py:70
  10.5 1.9 %copy-start.1 = (f32[8,32,512]{2,1,0:T(8,128)S(1)}, f32[8,32,512]{2,1,0:T(8,128)}, u32[]{:S(2)}) copy-start(f32[8,32,512]{2,1,0:T(8,128)} %rho_prev.5) | copy-start | bytes 1572868
  10.5 1.9 %copy-start.2 = (f32[8,32,512]{2,1,0:T(8,128)S(1)}, f32[8,32,512]{2,1,0:T(8,128)}, u32[]{:S(2)}) copy-start(f32[8,32,512]{2,1,0:T(8,128)} %potential.1) | copy-start | bytes 1572868
  11.1 4.7 %collective-permute-start.4 = (f32[64,512]{1,0:T(8,128)S(1)}, f32[64,512]{1,0:T(8,128)S(1)}, u32[]{:S(2)}, u32[]{:S(2)}) collective-permute-start(f32[64,512]{1,0:T(8,128)S(1)} %get-tuple-element.41.last), channel_id=1, source_target_pairs={{0,16},{32,48},{64,80},{96,112},{128,144},{160,176},{192,208},{224... | collective-permute-start | bytes 393224 | tf_op jit(solution)/shard_map/ppermute | solution.py:70
  17.0 9.8 %collective-permute-start.8 = (f32[192,512]{1,0:T(8,128)S(1)}, f32[192,512]{1,0:T(8,128)S(1)}, u32[]{:S(2)}, u32[]{:S(2)}) collective-permute-start(f32[192,512]{1,0:T(8,128)S(1)} %get-tuple-element.47.own.rest_0_), channel_id=1, source_target_pairs={{1,2},{3,4},{5,6},{7,8},{9,10},{11,12},{13,14},{2,1},{4,3},{6,5},{... | collective-permute-start | bytes 1179656 | tf_op jit(solution)/shard_map/ppermute | solution.py:70
  21.4 5.4 %collective-permute-start.9 = (f32[192,512]{1,0:T(8,128)S(1)}, f32[192,512]{1,0:T(8,128)S(1)}, u32[]{:S(2)}, u32[]{:S(2)}) collective-permute-start(f32[192,512]{1,0:T(8,128)S(1)} %get-tuple-element.47.own.rest_0_), channel_id=1, source_target_pairs={{0,1},{2,3},{4,5},{6,7},{8,9},{10,11},{12,13},{14,15},{1,0},{3,2},... | collective-permute-start | bytes 1179656 | tf_op jit(solution)/shard_map/ppermute | solution.py:70
  21.5 0.7 collective-permute-start.5
  22.7 12.4 %collective-permute-start.6 = (f32[64,512]{1,0:T(8,128)S(1)}, f32[64,512]{1,0:T(8,128)S(1)}, u32[]{:S(2)}, u32[]{:S(2)}) collective-permute-start(f32[64,512]{1,0:T(8,128)S(1)} %shard_map.48.own.rest_0_), channel_id=1, source_target_pairs={{1,2},{3,4},{5,6},{7,8},{9,10},{11,12},{13,14},{2,1},{4,3},{6,5},{... | collective-permute-start | bytes 393224 | tf_op jit(solution)/shard_map/ppermute | solution.py:70
  26.2 8.9 %collective-permute-start.7 = (f32[64,512]{1,0:T(8,128)S(1)}, f32[64,512]{1,0:T(8,128)S(1)}, u32[]{:S(2)}, u32[]{:S(2)}) collective-permute-start(f32[64,512]{1,0:T(8,128)S(1)} %shard_map.48.own.rest_0_), channel_id=1, source_target_pairs={{0,1},{2,3},{4,5},{6,7},{8,9},{10,11},{12,13},{14,15},{1,0},{3,2},... | collective-permute-start | bytes 393224 | tf_op jit(solution)/shard_map/ppermute | solution.py:70
  27.5 10.9 %collective-permute-start.10 = (f32[64,512]{1,0:T(8,128)S(1)}, f32[64,512]{1,0:T(8,128)S(1)}, u32[]{:S(2)}, u32[]{:S(2)}) collective-permute-start(f32[64,512]{1,0:T(8,128)S(1)} %get-tuple-element.49.last), channel_id=1, source_target_pairs={{0,16},{32,48},{64,80},{96,112},{128,144},{160,176},{192,208},{224... | collective-permute-start | bytes 393224 | tf_op jit(solution)/shard_map/ppermute | solution.py:70
  38.9 10.3 %collective-permute-start.14 = (f32[192,512]{1,0:T(8,128)S(1)}, f32[192,512]{1,0:T(8,128)S(1)}, u32[]{:S(2)}, u32[]{:S(2)}) collective-permute-start(f32[192,512]{1,0:T(8,128)S(1)} %get-tuple-element.52.own), channel_id=1, source_target_pairs={{1,2},{3,4},{5,6},{7,8},{9,10},{11,12},{13,14},{2,1},{4,3},{6,5},{... | collective-permute-start | bytes 1179656 | tf_op jit(solution)/shard_map/ppermute | solution.py:70
  43.6 5.5 %collective-permute-start.15 = (f32[192,512]{1,0:T(8,128)S(1)}, f32[192,512]{1,0:T(8,128)S(1)}, u32[]{:S(2)}, u32[]{:S(2)}) collective-permute-start(f32[192,512]{1,0:T(8,128)S(1)} %get-tuple-element.52.own), channel_id=1, source_target_pairs={{0,1},{2,3},{4,5},{6,7},{8,9},{10,11},{12,13},{14,15},{1,0},{3,2},... | collective-permute-start | bytes 1179656 | tf_op jit(solution)/shard_map/ppermute | solution.py:70
  43.7 0.7 collective-permute-start.11
  44.6 16.8 %collective-permute-start.12 = (f32[64,512]{1,0:T(8,128)S(1)}, f32[64,512]{1,0:T(8,128)S(1)}, u32[]{:S(2)}, u32[]{:S(2)}) collective-permute-start(f32[64,512]{1,0:T(8,128)S(1)} %shard_map.52.own), channel_id=1, source_target_pairs={{1,2},{3,4},{5,6},{7,8},{9,10},{11,12},{13,14},{2,1},{4,3},{6,5},{... | collective-permute-start | bytes 393224 | tf_op jit(solution)/shard_map/ppermute | solution.py:70
  49.0 12.4 %collective-permute-start.13 = (f32[64,512]{1,0:T(8,128)S(1)}, f32[64,512]{1,0:T(8,128)S(1)}, u32[]{:S(2)}, u32[]{:S(2)}) collective-permute-start(f32[64,512]{1,0:T(8,128)S(1)} %shard_map.52.own), channel_id=1, source_target_pairs={{0,1},{2,3},{4,5},{6,7},{8,9},{10,11},{12,13},{14,15},{1,0},{3,2},... | collective-permute-start | bytes 393224 | tf_op jit(solution)/shard_map/ppermute | solution.py:70
  49.9 15.0 %collective-permute-start.16 = (f32[64,512]{1,0:T(8,128)S(1)}, f32[64,512]{1,0:T(8,128)S(1)}, u32[]{:S(2)}, u32[]{:S(2)}) collective-permute-start(f32[64,512]{1,0:T(8,128)S(1)} %get-tuple-element.54.last), channel_id=1, source_target_pairs={{0,16},{32,48},{64,80},{96,112},{128,144},{160,176},{192,208},{224... | collective-permute-start | bytes 393224 | tf_op jit(solution)/shard_map/ppermute | solution.py:70
  66.1 12.5 %collective-permute-start.20 = (f32[192,512]{1,0:T(8,128)S(1)}, f32[192,512]{1,0:T(8,128)S(1)}, u32[]{:S(2)}, u32[]{:S(2)}) collective-permute-start(f32[192,512]{1,0:T(8,128)S(1)} %get-tuple-element.56.own.rest_0_), channel_id=1, source_target_pairs={{1,2},{3,4},{5,6},{7,8},{9,10},{11,12},{13,14},{2,1},{4,3},{6,5},{... | collective-permute-start | bytes 1179656 | tf_op jit(solution)/shard_map/ppermute | solution.py:70
  73.2 5.4 %collective-permute-start.21 = (f32[192,512]{1,0:T(8,128)S(1)}, f32[192,512]{1,0:T(8,128)S(1)}, u32[]{:S(2)}, u32[]{:S(2)}) collective-permute-start(f32[192,512]{1,0:T(8,128)S(1)} %get-tuple-element.56.own.rest_0_), channel_id=1, source_target_pairs={{0,1},{2,3},{4,5},{6,7},{8,9},{10,11},{12,13},{14,15},{1,0},{3,2},... | collective-permute-start | bytes 1179656 | tf_op jit(solution)/shard_map/ppermute | solution.py:70
  73.3 0.7 collective-permute-start.17
  74.5 15.7 %collective-permute-start.18 = (f32[64,512]{1,0:T(8,128)S(1)}, f32[64,512]{1,0:T(8,128)S(1)}, u32[]{:S(2)}, u32[]{:S(2)}) collective-permute-start(f32[64,512]{1,0:T(8,128)S(1)} %shard_map.56.own.rest_0_), channel_id=1, source_target_pairs={{1,2},{3,4},{5,6},{7,8},{9,10},{11,12},{13,14},{2,1},{4,3},{6,5},{... | collective-permute-start | bytes 393224 | tf_op jit(solution)/shard_map/ppermute | solution.py:70
  76.9 13.3 %collective-permute-start.19 = (f32[64,512]{1,0:T(8,128)S(1)}, f32[64,512]{1,0:T(8,128)S(1)}, u32[]{:S(2)}, u32[]{:S(2)}) collective-permute-start(f32[64,512]{1,0:T(8,128)S(1)} %shard_map.56.own.rest_0_), channel_id=1, source_target_pairs={{0,1},{2,3},{4,5},{6,7},{8,9},{10,11},{12,13},{14,15},{1,0},{3,2},... | collective-permute-start | bytes 393224 | tf_op jit(solution)/shard_map/ppermute | solution.py:70
  79.4 14.3 %collective-permute-start.22 = (f32[64,512]{1,0:T(8,128)S(1)}, f32[64,512]{1,0:T(8,128)S(1)}, u32[]{:S(2)}, u32[]{:S(2)}) collective-permute-start(f32[64,512]{1,0:T(8,128)S(1)} %get-tuple-element.58.last), channel_id=1, source_target_pairs={{0,16},{32,48},{64,80},{96,112},{128,144},{160,176},{192,208},{224... | collective-permute-start | bytes 393224 | tf_op jit(solution)/shard_map/ppermute | solution.py:70
  94.1 14.1 %collective-permute-start.25 = (f32[192,512]{1,0:T(8,128)S(1)}, f32[192,512]{1,0:T(8,128)S(1)}, u32[]{:S(2)}, u32[]{:S(2)}) collective-permute-start(f32[192,512]{1,0:T(8,128)S(1)} %get-tuple-element.60.own), channel_id=1, source_target_pairs={{1,2},{3,4},{5,6},{7,8},{9,10},{11,12},{13,14},{2,1},{4,3},{6,5},{... | collective-permute-start | bytes 1179656 | tf_op jit(solution)/shard_map/ppermute | solution.py:70
  101.1 7.2 %collective-permute-start.26 = (f32[192,512]{1,0:T(8,128)S(1)}, f32[192,512]{1,0:T(8,128)S(1)}, u32[]{:S(2)}, u32[]{:S(2)}) collective-permute-start(f32[192,512]{1,0:T(8,128)S(1)} %get-tuple-element.60.own), channel_id=1, source_target_pairs={{0,1},{2,3},{4,5},{6,7},{8,9},{10,11},{12,13},{14,15},{1,0},{3,2},... | collective-permute-start | bytes 1179656 | tf_op jit(solution)/shard_map/ppermute | solution.py:70
  101.2 0.7 collective-permute-start.23
  102.1 19.2 %collective-permute-start.24 = (f32[64,512]{1,0:T(8,128)S(1)}, f32[64,512]{1,0:T(8,128)S(1)}, u32[]{:S(2)}, u32[]{:S(2)}) collective-permute-start(f32[64,512]{1,0:T(8,128)S(1)} %shard_map.60.own), channel_id=1, source_target_pairs={{0,1},{2,3},{4,5},{6,7},{8,9},{10,11},{12,13},{14,15},{1,0},{3,2},... | collective-permute-start | bytes 393224 | tf_op jit(solution)/shard_map/ppermute | solution.py:70
  108.9 14.7 %collective-permute-start.27 = (f32[64,512]{1,0:T(8,128)S(1)}, f32[64,512]{1,0:T(8,128)S(1)}, u32[]{:S(2)}, u32[]{:S(2)}) collective-permute-start(f32[64,512]{1,0:T(8,128)S(1)} %get-tuple-element.62.last), channel_id=1, source_target_pairs={{0,16},{32,48},{64,80},{96,112},{128,144},{160,176},{192,208},{224... | collective-permute-start | bytes 393224 | tf_op jit(solution)/shard_map/ppermute | solution.py:70
  121.6 3.2 %collective-permute-start.28 = (f32[64,512]{1,0:T(8,128)S(1)}, f32[64,512]{1,0:T(8,128)S(1)}, u32[]{:S(2)}, u32[]{:S(2)}) collective-permute-start(f32[64,512]{1,0:T(8,128)S(1)} %shard_map.61.first), channel_id=1, source_target_pairs={{16,32},{48,64},{80,96},{112,128},{144,160},{176,192},{208,224},{3... | collective-permute-start | bytes 393224 | tf_op jit(solution)/shard_map/ppermute | solution.py:70

commit v7 on v5

--- a/solution.py
+++ b/solution.py
@@ -190,7 +190,8 @@
 
 def lane_sums(value):
     rows = jnp.sum(value, axis=0, keepdims=True)
-    return sum(rows[:, i : i + LANES] for i in range(0, rows.shape[1], LANES))
+    lanes = sum(rows[:, i : i + LANES] for i in range(0, rows.shape[1], LANES))
+    return lanes[:, : LANES // 2] + lanes[:, LANES // 2 :]
 
 
 def rest_kernel(kind, started, first, inner, last, recv0, x_table, last_table, whole, *rest):
@@ -214,8 +215,7 @@
     result = finish(kind, value, slice(rows, 4 * rows), whole, scaling)
     out[...] = result
     if kind == "last":
-        sums[:, :LANES] = lane_sums(rho_prev[...])
-        sums[:, LANES:] = lane_sums(result)
+        sums[...] = jnp.concatenate([lane_sums(rho_prev[...]), lane_sums(result)], axis=1)
 
 
 def first_group_kernel(kind, started, part, recv1, first_table, whole, *rest):
@@ -230,13 +230,13 @@
     result = finish(kind, value, slice(0, value.shape[0]), whole, scaling)
     out[...] = result
     if kind == "last":
-        sums[...] = sums_rest[...]
-        sums[:, LANES:] += lane_sums(result)
+        new = lane_sums(result)
+        sums[...] = sums_rest[...] + jnp.concatenate([jnp.zeros_like(new), new], axis=1)
 
 
 def scale_kernel(first, rest, sums, out, ratio):
     totals = jnp.sum(sums[...], axis=0, keepdims=True)
-    mass_prev, mass_new = jnp.sum(totals[:, :LANES]), jnp.sum(totals[:, LANES:])
+    mass_prev, mass_new = jnp.sum(totals[:, : LANES // 2]), jnp.sum(totals[:, LANES // 2 :])
     ones = jnp.ones((1, LANES), jnp.float32)
     prev, new = mass_prev * ones, mass_new * ones
     ratio[...] = new / prev
@@ -291,7 +291,7 @@
         recv0 = swap(send0, "gx", 0)
         recv1 = swap(send1, "gx", 1)
         more = ((scaling[1],) if started else ()) + ((rho_ordered,) if last else ())
-        total = [(1, 2 * LANES)] if last else []
+        total = [(1, LANES)] if last else []
         new_rest, part, *sums = call(
             functools.partial(rest_kernel, kind, started),
             (send1, inner, send0, recv0, x_table, last_table, whole, *more),
@@ -315,8 +315,8 @@
         else:
             first, rest, sums = heat_step(2 * sweep, "last", first, rest, potential_ordered, scaling)
     everyone = size_x * size_z
-    sums = jnp.broadcast_to(sums[None], (everyone, 1, 2 * LANES))
-    sums = lax.all_to_all(sums, ("gx", "gz"), 0, 0, tiled=True).reshape(everyone, 2 * LANES)
+    sums = jnp.broadcast_to(sums, (everyone, LANES))
+    sums = lax.all_to_all(sums, ("gx", "gz"), 0, 0, tiled=True)
     rho_next, ratio = call(scale_kernel, (first, rest, sums), [(depth, width, length), (1, LANES)])
     return rho_next, ratio[0, :1]
 

time: 172 us -> 169 us (0.983)
  blocking collectives: 47 us -> 44.3 us
    all_to_all x1, blocking collectives: 47 us -> 44.3 us  [step(): sums = lax.all_to_all(sums, ('gx', 'gz'), 0, 0, tiled=True)]
where the time goes in v7:
time: 169 us
  starting transfers between devices  90.1 us (53%)
  blocking collectives  44.3 us (26%)
  waiting for transfers between devices  18.4 us (11%)
  Pallas kernels  13.7 us (8%)
    ppermute x30, starting transfers between devices, swap(): return lax.ppermute(value, axis, pairs + [(j, i) for i, j in pairs])  90.1 us
    all_to_all x1, blocking collectives, step(): sums = lax.all_to_all(sums, ('gx', 'gz'), 0, 0, tiled=True)  44.3 us
    ppermute x30, waiting for transfers between devices, swap(): return lax.ppermute(value, axis, pairs + [(j, i) for i, j in pairs])  18.4 us
    pallas_call x25, Pallas kernels, call(): pl.pallas_call(kernel, out_shape=[jax.ShapeDtypeStruct(shape, dtype) for...  13.7 us
  transfers between devices with their start and end apart: 30, of which 9 were waited for; matrix products, arithmetic and copies ran while one was open for 0% of the time, Pallas kernels for 5%

profile of v7, /device:TPU:1, one launch (start us, length us, event | category | flops | bytes accessed | tf_op | source)
XLA Modules:
  0.0 168.7 jit_solution(9638194988051725832)
XLA Ops:
  0.6 1.0 copy-done
  1.8 4.5 %collective-permute-start = (f32[128,512]{1,0:T(8,128)S(1)}, f32[128,512]{1,0:T(8,128)S(1)}, u32[]{:S(2)}, u32[]{:S(2)}) collective-permute-start(f32[128,512]{1,0:T(8,128)S(1)} %shard_map.41.own), channel_id=1, source_target_pairs={{1,2},{3,4},{5,6},{7,8},{9,10},{11,12},{13,14},{2,1},{4,3},{6,5},{... | collective-permute-start | bytes 786440 | tf_op jit(solution)/shard_map/ppermute | solution.py:70
  6.5 3.5 %collective-permute-start.2 = (f32[128,512]{1,0:T(8,128)S(1)}, f32[128,512]{1,0:T(8,128)S(1)}, u32[]{:S(2)}, u32[]{:S(2)}) collective-permute-start(f32[128,512]{1,0:T(8,128)S(1)} %shard_map.44.own), channel_id=1, source_target_pairs={{1,2},{3,4},{5,6},{7,8},{9,10},{11,12},{13,14},{2,1},{4,3},{6,5},{... | collective-permute-start | bytes 786440 | tf_op jit(solution)/shard_map/ppermute | solution.py:70
  10.1 0.4 shard_map.42
  10.5 0.5 shard_map.43
  11.1 1.4 collective-permute-start.4
  12.5 1.6 collective-permute-done.2.far
  14.2 0.5 shard_map.45.inner
  14.7 1.0 collective-permute-done.4.recv0
  15.7 1.3 shard_map.47
  17.0 4.4 %collective-permute-start.8 = (f32[192,512]{1,0:T(8,128)S(1)}, f32[192,512]{1,0:T(8,128)S(1)}, u32[]{:S(2)}, u32[]{:S(2)}) collective-permute-start(f32[192,512]{1,0:T(8,128)S(1)} %get-tuple-element.47.own.rest_0_), channel_id=1, source_target_pairs={{1,2},{3,4},{5,6},{7,8},{9,10},{11,12},{13,14},{2,1},{4,3},{6,5},{... | collective-permute-start | bytes 1179656 | tf_op jit(solution)/shard_map/ppermute | solution.py:70
  21.5 0.7 collective-permute-start.5
  22.2 0.5 shard_map.48.own.rest_0_
  22.7 3.5 %collective-permute-start.6 = (f32[64,512]{1,0:T(8,128)S(1)}, f32[64,512]{1,0:T(8,128)S(1)}, u32[]{:S(2)}, u32[]{:S(2)}) collective-permute-start(f32[64,512]{1,0:T(8,128)S(1)} %shard_map.48.own.rest_0_), channel_id=1, source_target_pairs={{1,2},{3,4},{5,6},{7,8},{9,10},{11,12},{13,14},{2,1},{4,3},{6,5},{... | collective-permute-start | bytes 393224 | tf_op jit(solution)/shard_map/ppermute | solution.py:70
  26.3 0.5 collective-permute-done.8.far
  26.8 0.7 shard_map.50
  27.5 7.5 %collective-permute-start.10 = (f32[64,512]{1,0:T(8,128)S(1)}, f32[64,512]{1,0:T(8,128)S(1)}, u32[]{:S(2)}, u32[]{:S(2)}) collective-permute-start(f32[64,512]{1,0:T(8,128)S(1)} %get-tuple-element.49.last), channel_id=1, source_target_pairs={{0,16},{32,48},{64,80},{96,112},{128,144},{160,176},{192,208},{224... | collective-permute-start | bytes 393224 | tf_op jit(solution)/shard_map/ppermute | solution.py:70
  35.4 3.1 %collective-permute-done.10.recv0 = f32[64,512]{1,0:T(8,128)S(1)} collective-permute-done((f32[64,512]{1,0:T(8,128)S(1)}, f32[64,512]{1,0:T(8,128)S(1)}, u32[]{:S(2)}, u32[]{:S(2)}) %collective-permute-start.10) | collective-permute-done | bytes 131104 | tf_op jit(solution)/shard_map/ppermute | solution.py:70
  38.4 0.4 shard_map.51
  38.9 4.7 %collective-permute-start.14 = (f32[192,512]{1,0:T(8,128)S(1)}, f32[192,512]{1,0:T(8,128)S(1)}, u32[]{:S(2)}, u32[]{:S(2)}) collective-permute-start(f32[192,512]{1,0:T(8,128)S(1)} %get-tuple-element.52.own), channel_id=1, source_target_pairs={{1,2},{3,4},{5,6},{7,8},{9,10},{11,12},{13,14},{2,1},{4,3},{6,5},{... | collective-permute-start | bytes 1179656 | tf_op jit(solution)/shard_map/ppermute | solution.py:70
  43.7 0.7 collective-permute-start.11
  44.6 4.4 %collective-permute-start.12 = (f32[64,512]{1,0:T(8,128)S(1)}, f32[64,512]{1,0:T(8,128)S(1)}, u32[]{:S(2)}, u32[]{:S(2)}) collective-permute-start(f32[64,512]{1,0:T(8,128)S(1)} %shard_map.52.own), channel_id=1, source_target_pairs={{1,2},{3,4},{5,6},{7,8},{9,10},{11,12},{13,14},{2,1},{4,3},{6,5},{... | collective-permute-start | bytes 393224 | tf_op jit(solution)/shard_map/ppermute | solution.py:70
  49.2 0.7 shard_map.54
  49.9 11.6 %collective-permute-start.16 = (f32[64,512]{1,0:T(8,128)S(1)}, f32[64,512]{1,0:T(8,128)S(1)}, u32[]{:S(2)}, u32[]{:S(2)}) collective-permute-start(f32[64,512]{1,0:T(8,128)S(1)} %get-tuple-element.54.last), channel_id=1, source_target_pairs={{0,16},{32,48},{64,80},{96,112},{128,144},{160,176},{192,208},{224... | collective-permute-start | bytes 393224 | tf_op jit(solution)/shard_map/ppermute | solution.py:70
  61.5 0.3 shard_map.53.first
  61.8 3.1 %collective-permute-done.16.recv0 = f32[64,512]{1,0:T(8,128)S(1)} collective-permute-done((f32[64,512]{1,0:T(8,128)S(1)}, f32[64,512]{1,0:T(8,128)S(1)}, u32[]{:S(2)}, u32[]{:S(2)}) %collective-permute-start.16) | collective-permute-done | bytes 131104 | tf_op jit(solution)/shard_map/ppermute | solution.py:70
  64.9 1.2 shard_map.55
  66.1 7.1 %collective-permute-start.20 = (f32[192,512]{1,0:T(8,128)S(1)}, f32[192,512]{1,0:T(8,128)S(1)}, u32[]{:S(2)}, u32[]{:S(2)}) collective-permute-start(f32[192,512]{1,0:T(8,128)S(1)} %get-tuple-element.56.own.rest_0_), channel_id=1, source_target_pairs={{1,2},{3,4},{5,6},{7,8},{9,10},{11,12},{13,14},{2,1},{4,3},{6,5},{... | collective-permute-start | bytes 1179656 | tf_op jit(solution)/shard_map/ppermute | solution.py:70
  73.3 0.7 collective-permute-start.17
  74.0 0.5 shard_map.56.own.rest_0_
  74.5 2.4 %collective-permute-start.18 = (f32[64,512]{1,0:T(8,128)S(1)}, f32[64,512]{1,0:T(8,128)S(1)}, u32[]{:S(2)}, u32[]{:S(2)}) collective-permute-start(f32[64,512]{1,0:T(8,128)S(1)} %shard_map.56.own.rest_0_), channel_id=1, source_target_pairs={{1,2},{3,4},{5,6},{7,8},{9,10},{11,12},{13,14},{2,1},{4,3},{6,5},{... | collective-permute-start | bytes 393224 | tf_op jit(solution)/shard_map/ppermute | solution.py:70
  77.0 1.7 collective-permute-done.20.far
  78.7 0.7 shard_map.58
  79.4 10.9 %collective-permute-start.22 = (f32[64,512]{1,0:T(8,128)S(1)}, f32[64,512]{1,0:T(8,128)S(1)}, u32[]{:S(2)}, u32[]{:S(2)}) collective-permute-start(f32[64,512]{1,0:T(8,128)S(1)} %get-tuple-element.58.last), channel_id=1, source_target_pairs={{0,16},{32,48},{64,80},{96,112},{128,144},{160,176},{192,208},{224... | collective-permute-start | bytes 393224 | tf_op jit(solution)/shard_map/ppermute | solution.py:70
  90.6 3.1 %collective-permute-done.22.recv0 = f32[64,512]{1,0:T(8,128)S(1)} collective-permute-done((f32[64,512]{1,0:T(8,128)S(1)}, f32[64,512]{1,0:T(8,128)S(1)}, u32[]{:S(2)}, u32[]{:S(2)}) %collective-permute-start.22) | collective-permute-done | bytes 131104 | tf_op jit(solution)/shard_map/ppermute | solution.py:70
  93.6 0.4 shard_map.59
  94.1 7.0 %collective-permute-start.26 = (f32[192,512]{1,0:T(8,128)S(1)}, f32[192,512]{1,0:T(8,128)S(1)}, u32[]{:S(2)}, u32[]{:S(2)}) collective-permute-start(f32[192,512]{1,0:T(8,128)S(1)} %get-tuple-element.60.own), channel_id=1, source_target_pairs={{1,2},{3,4},{5,6},{7,8},{9,10},{11,12},{13,14},{2,1},{4,3},{6,5},{... | collective-permute-start | bytes 1179656 | tf_op jit(solution)/shard_map/ppermute | solution.py:70
  101.2 0.7 collective-permute-start.23
  102.1 2.4 %collective-permute-start.24 = (f32[64,512]{1,0:T(8,128)S(1)}, f32[64,512]{1,0:T(8,128)S(1)}, u32[]{:S(2)}, u32[]{:S(2)}) collective-permute-start(f32[64,512]{1,0:T(8,128)S(1)} %shard_map.60.own), channel_id=1, source_target_pairs={{1,2},{3,4},{5,6},{7,8},{9,10},{11,12},{13,14},{2,1},{4,3},{6,5},{... | collective-permute-start | bytes 393224 | tf_op jit(solution)/shard_map/ppermute | solution.py:70
  104.6 2.0 %collective-permute-done.26.far = f32[192,512]{1,0:T(8,128)S(1)} collective-permute-done((f32[192,512]{1,0:T(8,128)S(1)}, f32[192,512]{1,0:T(8,128)S(1)}, u32[]{:S(2)}, u32[]{:S(2)}) %collective-permute-start.26) | collective-permute-done | bytes 393248 | tf_op jit(solution)/shard_map/ppermute | solution.py:70
  106.5 0.7 shard_map.62
  107.2 10.6 %collective-permute-start.28 = (f32[64,512]{1,0:T(8,128)S(1)}, f32[64,512]{1,0:T(8,128)S(1)}, u32[]{:S(2)}, u32[]{:S(2)}) collective-permute-start(f32[64,512]{1,0:T(8,128)S(1)} %get-tuple-element.62.last), channel_id=1, source_target_pairs={{0,16},{32,48},{64,80},{96,112},{128,144},{160,176},{192,208},{224... | collective-permute-start | bytes 393224 | tf_op jit(solution)/shard_map/ppermute | solution.py:70
  118.2 0.7 collective-permute-start.29
  118.9 2.4 %collective-permute-done.28.recv0 = f32[64,512]{1,0:T(8,128)S(1)} collective-permute-done((f32[64,512]{1,0:T(8,128)S(1)}, f32[64,512]{1,0:T(8,128)S(1)}, u32[]{:S(2)}, u32[]{:S(2)}) %collective-permute-start.28) | collective-permute-done | bytes 131104 | tf_op jit(solution)/shard_map/ppermute | solution.py:70
  121.3 1.3 shard_map.63
  122.6 0.6 shard_map.64
  123.3 44.3 %all_to_all.8 = f32[256,1,128]{2,1,0:T(1,128)S(1)} all-to-all(f32[256,1,128]{2,1,0:T(1,128)S(1)} %broadcast_in_dim.2), channel_id=1, replica_groups=mesh['gx'=16,'gz'=16] {'gx','gz'}, dimensions={0} | all-to-all | bytes 262144 | tf_op jit(solution)/shard_map/all_to_all | solution.py:319
  167.6 1.1 shard_map.65
  (45 shorter events, 2.7 us)
Async XLA Ops:
  0.6 1.0 copy-start
  1.8 8.7 %collective-permute-start = (f32[128,512]{1,0:T(8,128)S(1)}, f32[128,512]{1,0:T(8,128)S(1)}, u32[]{:S(2)}, u32[]{:S(2)}) collective-permute-start(f32[128,512]{1,0:T(8,128)S(1)} %shard_map.41.own), channel_id=1, source_target_pairs={{1,2},{3,4},{5,6},{7,8},{9,10},{11,12},{13,14},{2,1},{4,3},{6,5},{... | collective-permute-start | bytes 786440 | tf_op jit(solution)/shard_map/ppermute | solution.py:70
  6.3 4.2 %collective-permute-start.1 = (f32[128,512]{1,0:T(8,128)S(1)}, f32[128,512]{1,0:T(8,128)S(1)}, u32[]{:S(2)}, u32[]{:S(2)}) collective-permute-start(f32[128,512]{1,0:T(8,128)S(1)} %shard_map.41.own), channel_id=1, source_target_pairs={{0,1},{2,3},{4,5},{6,7},{8,9},{10,11},{12,13},{14,15},{1,0},{3,2},... | collective-permute-start | bytes 786440 | tf_op jit(solution)/shard_map/ppermute | solution.py:70
  6.5 7.7 %collective-permute-start.2 = (f32[128,512]{1,0:T(8,128)S(1)}, f32[128,512]{1,0:T(8,128)S(1)}, u32[]{:S(2)}, u32[]{:S(2)}) collective-permute-start(f32[128,512]{1,0:T(8,128)S(1)} %shard_map.44.own), channel_id=1, source_target_pairs={{1,2},{3,4},{5,6},{7,8},{9,10},{11,12},{13,14},{2,1},{4,3},{6,5},{... | collective-permute-start | bytes 786440 | tf_op jit(solution)/shard_map/ppermute | solution.py:70
  10.0 4.2 %collective-permute-start.3 = (f32[128,512]{1,0:T(8,128)S(1)}, f32[128,512]{1,0:T(8,128)S(1)}, u32[]{:S(2)}, u32[]{:S(2)}) collective-permute-start(f32[128,512]{1,0:T(8,128)S(1)} %shard_map.44.own), channel_id=1, source_target_pairs={{0,1},{2,3},{4,5},{6,7},{8,9},{10,11},{12,13},{14,15},{1,0},{3,2},... | collective-permute-start | bytes 786440 | tf_op jit(solution)/shard_map/ppermute | solution.py:70
  10.5 1.9 %copy-start.1 = (f32[8,32,512]{2,1,0:T(8,128)S(1)}, f32[8,32,512]{2,1,0:T(8,128)}, u32[]{:S(2)}) copy-start(f32[8,32,512]{2,1,0:T(8,128)} %rho_prev.5) | copy-start | bytes 1572868
  10.5 1.9 %copy-start.2 = (f32[8,32,512]{2,1,0:T(8,128)S(1)}, f32[8,32,512]{2,1,0:T(8,128)}, u32[]{:S(2)}) copy-start(f32[8,32,512]{2,1,0:T(8,128)} %potential.1) | copy-start | bytes 1572868
  11.1 4.7 %collective-permute-start.4 = (f32[64,512]{1,0:T(8,128)S(1)}, f32[64,512]{1,0:T(8,128)S(1)}, u32[]{:S(2)}, u32[]{:S(2)}) collective-permute-start(f32[64,512]{1,0:T(8,128)S(1)} %get-tuple-element.41.last), channel_id=1, source_target_pairs={{0,16},{32,48},{64,80},{96,112},{128,144},{160,176},{192,208},{224... | collective-permute-start | bytes 393224 | tf_op jit(solution)/shard_map/ppermute | solution.py:70
  17.0 9.8 %collective-permute-start.8 = (f32[192,512]{1,0:T(8,128)S(1)}, f32[192,512]{1,0:T(8,128)S(1)}, u32[]{:S(2)}, u32[]{:S(2)}) collective-permute-start(f32[192,512]{1,0:T(8,128)S(1)} %get-tuple-element.47.own.rest_0_), channel_id=1, source_target_pairs={{1,2},{3,4},{5,6},{7,8},{9,10},{11,12},{13,14},{2,1},{4,3},{6,5},{... | collective-permute-start | bytes 1179656 | tf_op jit(solution)/shard_map/ppermute | solution.py:70
  21.4 5.4 %collective-permute-start.9 = (f32[192,512]{1,0:T(8,128)S(1)}, f32[192,512]{1,0:T(8,128)S(1)}, u32[]{:S(2)}, u32[]{:S(2)}) collective-permute-start(f32[192,512]{1,0:T(8,128)S(1)} %get-tuple-element.47.own.rest_0_), channel_id=1, source_target_pairs={{0,1},{2,3},{4,5},{6,7},{8,9},{10,11},{12,13},{14,15},{1,0},{3,2},... | collective-permute-start | bytes 1179656 | tf_op jit(solution)/shard_map/ppermute | solution.py:70
  21.5 0.7 collective-permute-start.5
  22.7 12.4 %collective-permute-start.6 = (f32[64,512]{1,0:T(8,128)S(1)}, f32[64,512]{1,0:T(8,128)S(1)}, u32[]{:S(2)}, u32[]{:S(2)}) collective-permute-start(f32[64,512]{1,0:T(8,128)S(1)} %shard_map.48.own.rest_0_), channel_id=1, source_target_pairs={{1,2},{3,4},{5,6},{7,8},{9,10},{11,12},{13,14},{2,1},{4,3},{6,5},{... | collective-permute-start | bytes 393224 | tf_op jit(solution)/shard_map/ppermute | solution.py:70
  26.2 8.9 %collective-permute-start.7 = (f32[64,512]{1,0:T(8,128)S(1)}, f32[64,512]{1,0:T(8,128)S(1)}, u32[]{:S(2)}, u32[]{:S(2)}) collective-permute-start(f32[64,512]{1,0:T(8,128)S(1)} %shard_map.48.own.rest_0_), channel_id=1, source_target_pairs={{0,1},{2,3},{4,5},{6,7},{8,9},{10,11},{12,13},{14,15},{1,0},{3,2},... | collective-permute-start | bytes 393224 | tf_op jit(solution)/shard_map/ppermute | solution.py:70
  27.5 10.9 %collective-permute-start.10 = (f32[64,512]{1,0:T(8,128)S(1)}, f32[64,512]{1,0:T(8,128)S(1)}, u32[]{:S(2)}, u32[]{:S(2)}) collective-permute-start(f32[64,512]{1,0:T(8,128)S(1)} %get-tuple-element.49.last), channel_id=1, source_target_pairs={{0,16},{32,48},{64,80},{96,112},{128,144},{160,176},{192,208},{224... | collective-permute-start | bytes 393224 | tf_op jit(solution)/shard_map/ppermute | solution.py:70
  38.9 10.3 %collective-permute-start.14 = (f32[192,512]{1,0:T(8,128)S(1)}, f32[192,512]{1,0:T(8,128)S(1)}, u32[]{:S(2)}, u32[]{:S(2)}) collective-permute-start(f32[192,512]{1,0:T(8,128)S(1)} %get-tuple-element.52.own), channel_id=1, source_target_pairs={{1,2},{3,4},{5,6},{7,8},{9,10},{11,12},{13,14},{2,1},{4,3},{6,5},{... | collective-permute-start | bytes 1179656 | tf_op jit(solution)/shard_map/ppermute | solution.py:70
  43.6 5.5 %collective-permute-start.15 = (f32[192,512]{1,0:T(8,128)S(1)}, f32[192,512]{1,0:T(8,128)S(1)}, u32[]{:S(2)}, u32[]{:S(2)}) collective-permute-start(f32[192,512]{1,0:T(8,128)S(1)} %get-tuple-element.52.own), channel_id=1, source_target_pairs={{0,1},{2,3},{4,5},{6,7},{8,9},{10,11},{12,13},{14,15},{1,0},{3,2},... | collective-permute-start | bytes 1179656 | tf_op jit(solution)/shard_map/ppermute | solution.py:70
  43.7 0.7 collective-permute-start.11
  44.6 16.8 %collective-permute-start.12 = (f32[64,512]{1,0:T(8,128)S(1)}, f32[64,512]{1,0:T(8,128)S(1)}, u32[]{:S(2)}, u32[]{:S(2)}) collective-permute-start(f32[64,512]{1,0:T(8,128)S(1)} %shard_map.52.own), channel_id=1, source_target_pairs={{1,2},{3,4},{5,6},{7,8},{9,10},{11,12},{13,14},{2,1},{4,3},{6,5},{... | collective-permute-start | bytes 393224 | tf_op jit(solution)/shard_map/ppermute | solution.py:70
  49.0 12.4 %collective-permute-start.13 = (f32[64,512]{1,0:T(8,128)S(1)}, f32[64,512]{1,0:T(8,128)S(1)}, u32[]{:S(2)}, u32[]{:S(2)}) collective-permute-start(f32[64,512]{1,0:T(8,128)S(1)} %shard_map.52.own), channel_id=1, source_target_pairs={{0,1},{2,3},{4,5},{6,7},{8,9},{10,11},{12,13},{14,15},{1,0},{3,2},... | collective-permute-start | bytes 393224 | tf_op jit(solution)/shard_map/ppermute | solution.py:70
  49.9 15.0 %collective-permute-start.16 = (f32[64,512]{1,0:T(8,128)S(1)}, f32[64,512]{1,0:T(8,128)S(1)}, u32[]{:S(2)}, u32[]{:S(2)}) collective-permute-start(f32[64,512]{1,0:T(8,128)S(1)} %get-tuple-element.54.last), channel_id=1, source_target_pairs={{0,16},{32,48},{64,80},{96,112},{128,144},{160,176},{192,208},{224... | collective-permute-start | bytes 393224 | tf_op jit(solution)/shard_map/ppermute | solution.py:70
  66.1 12.5 %collective-permute-start.20 = (f32[192,512]{1,0:T(8,128)S(1)}, f32[192,512]{1,0:T(8,128)S(1)}, u32[]{:S(2)}, u32[]{:S(2)}) collective-permute-start(f32[192,512]{1,0:T(8,128)S(1)} %get-tuple-element.56.own.rest_0_), channel_id=1, source_target_pairs={{1,2},{3,4},{5,6},{7,8},{9,10},{11,12},{13,14},{2,1},{4,3},{6,5},{... | collective-permute-start | bytes 1179656 | tf_op jit(solution)/shard_map/ppermute | solution.py:70
  73.2 5.4 %collective-permute-start.21 = (f32[192,512]{1,0:T(8,128)S(1)}, f32[192,512]{1,0:T(8,128)S(1)}, u32[]{:S(2)}, u32[]{:S(2)}) collective-permute-start(f32[192,512]{1,0:T(8,128)S(1)} %get-tuple-element.56.own.rest_0_), channel_id=1, source_target_pairs={{0,1},{2,3},{4,5},{6,7},{8,9},{10,11},{12,13},{14,15},{1,0},{3,2},... | collective-permute-start | bytes 1179656 | tf_op jit(solution)/shard_map/ppermute | solution.py:70
  73.3 0.7 collective-permute-start.17
  74.5 15.7 %collective-permute-start.18 = (f32[64,512]{1,0:T(8,128)S(1)}, f32[64,512]{1,0:T(8,128)S(1)}, u32[]{:S(2)}, u32[]{:S(2)}) collective-permute-start(f32[64,512]{1,0:T(8,128)S(1)} %shard_map.56.own.rest_0_), channel_id=1, source_target_pairs={{1,2},{3,4},{5,6},{7,8},{9,10},{11,12},{13,14},{2,1},{4,3},{6,5},{... | collective-permute-start | bytes 393224 | tf_op jit(solution)/shard_map/ppermute | solution.py:70
  76.9 13.4 %collective-permute-start.19 = (f32[64,512]{1,0:T(8,128)S(1)}, f32[64,512]{1,0:T(8,128)S(1)}, u32[]{:S(2)}, u32[]{:S(2)}) collective-permute-start(f32[64,512]{1,0:T(8,128)S(1)} %shard_map.56.own.rest_0_), channel_id=1, source_target_pairs={{0,1},{2,3},{4,5},{6,7},{8,9},{10,11},{12,13},{14,15},{1,0},{3,2},... | collective-permute-start | bytes 393224 | tf_op jit(solution)/shard_map/ppermute | solution.py:70
  79.4 14.3 %collective-permute-start.22 = (f32[64,512]{1,0:T(8,128)S(1)}, f32[64,512]{1,0:T(8,128)S(1)}, u32[]{:S(2)}, u32[]{:S(2)}) collective-permute-start(f32[64,512]{1,0:T(8,128)S(1)} %get-tuple-element.58.last), channel_id=1, source_target_pairs={{0,16},{32,48},{64,80},{96,112},{128,144},{160,176},{192,208},{224... | collective-permute-start | bytes 393224 | tf_op jit(solution)/shard_map/ppermute | solution.py:70
  94.1 12.4 %collective-permute-start.26 = (f32[192,512]{1,0:T(8,128)S(1)}, f32[192,512]{1,0:T(8,128)S(1)}, u32[]{:S(2)}, u32[]{:S(2)}) collective-permute-start(f32[192,512]{1,0:T(8,128)S(1)} %get-tuple-element.60.own), channel_id=1, source_target_pairs={{1,2},{3,4},{5,6},{7,8},{9,10},{11,12},{13,14},{2,1},{4,3},{6,5},{... | collective-permute-start | bytes 1179656 | tf_op jit(solution)/shard_map/ppermute | solution.py:70
  101.1 5.4 %collective-permute-start.27 = (f32[192,512]{1,0:T(8,128)S(1)}, f32[192,512]{1,0:T(8,128)S(1)}, u32[]{:S(2)}, u32[]{:S(2)}) collective-permute-start(f32[192,512]{1,0:T(8,128)S(1)} %get-tuple-element.60.own), channel_id=1, source_target_pairs={{0,1},{2,3},{4,5},{6,7},{8,9},{10,11},{12,13},{14,15},{1,0},{3,2},... | collective-permute-start | bytes 1179656 | tf_op jit(solution)/shard_map/ppermute | solution.py:70
  101.2 0.7 collective-permute-start.23
  102.1 15.8 %collective-permute-start.24 = (f32[64,512]{1,0:T(8,128)S(1)}, f32[64,512]{1,0:T(8,128)S(1)}, u32[]{:S(2)}, u32[]{:S(2)}) collective-permute-start(f32[64,512]{1,0:T(8,128)S(1)} %shard_map.60.own), channel_id=1, source_target_pairs={{1,2},{3,4},{5,6},{7,8},{9,10},{11,12},{13,14},{2,1},{4,3},{6,5},{... | collective-permute-start | bytes 393224 | tf_op jit(solution)/shard_map/ppermute | solution.py:70
  104.5 13.4 %collective-permute-start.25 = (f32[64,512]{1,0:T(8,128)S(1)}, f32[64,512]{1,0:T(8,128)S(1)}, u32[]{:S(2)}, u32[]{:S(2)}) collective-permute-start(f32[64,512]{1,0:T(8,128)S(1)} %shard_map.60.own), channel_id=1, source_target_pairs={{0,1},{2,3},{4,5},{6,7},{8,9},{10,11},{12,13},{14,15},{1,0},{3,2},... | collective-permute-start | bytes 393224 | tf_op jit(solution)/shard_map/ppermute | solution.py:70
  107.2 14.0 %collective-permute-start.28 = (f32[64,512]{1,0:T(8,128)S(1)}, f32[64,512]{1,0:T(8,128)S(1)}, u32[]{:S(2)}, u32[]{:S(2)}) collective-permute-start(f32[64,512]{1,0:T(8,128)S(1)} %get-tuple-element.62.last), channel_id=1, source_target_pairs={{0,16},{32,48},{64,80},{96,112},{128,144},{160,176},{192,208},{224... | collective-permute-start | bytes 393224 | tf_op jit(solution)/shard_map/ppermute | solution.py:70
  118.2 4.4 %collective-permute-start.29 = (f32[64,512]{1,0:T(8,128)S(1)}, f32[64,512]{1,0:T(8,128)S(1)}, u32[]{:S(2)}, u32[]{:S(2)}) collective-permute-start(f32[64,512]{1,0:T(8,128)S(1)} %shard_map.61.first), channel_id=1, source_target_pairs={{16,32},{48,64},{80,96},{112,128},{144,160},{176,192},{208,224},{3... | collective-permute-start | bytes 393224 | tf_op jit(solution)/shard_map/ppermute | solution.py:70
